TPU v7x, 512 devices: a whole 4x4x16 slice. The times are simulated.
512 devices in a mesh: req: 64 (over z, x), tp: 8 (over y, core).
Axes of the slice: x: 4, y: 4, z: 16, core: 2. Of those that a mesh axis runs over, the one named last changes fastest.
Arguments:
- tokens: bfloat16 [32768, 1024], P('req', 'tp'), may hold values from -24 to 24
- qkv_weight: bfloat16 [1024, 3, 1024], P(None, None, 'tp'), may hold values from -0.1875 to 0.1875
- out_weight: bfloat16 [1024, 1024], P('tp'), may hold values from -0.1875 to 0.1875
- attn_gain: float32 [1024], replicated, may hold values from 0.1 to 1.9
- attn_shift: float32 [1024], replicated, may hold values from -3 to 3
- up_weight: bfloat16 [1024, 4096], P(None, 'tp'), may hold values from -0.1875 to 0.1875
- down_weight: bfloat16 [4096, 1024], P('tp'), may hold values from -0.09375 to 0.09375
- mlp_gain: float32 [1024], replicated, may hold values from 0.1 to 1.9
- mlp_shift: float32 [1024], replicated, may hold values from -3 to 3
- prefix_cache: bfloat16 [128, 256, 2, 1024], P('req', None, None, 'tp'), may hold values from -6 to 6
- earlier_cache: bfloat16 [2048, 16, 2, 1024], P('req', None, None, 'tp'), may hold values from -6 to 6
- suffix_len: int32 [4096], P('req'), may hold values from 1 to 15, as said below
- prefix_id: int32 [4096], P('req'), may hold values from 0 to 127, as said below
- earlier_slot: int32 [4096], P('req'), may hold values from -1 to 2047, as said below
Outputs:
- encoded: bfloat16 [32768, 1024], P('req', 'tp')
Inputs may be any that keep to these rules, and one draw needn't show every extreme that they name: `suffix_len`: requests 2g and 2g+1 of a device together fill its tokens g * 16 to (g + 1) * 16 - 1. `prefix_id`: both requests of a pair read prefix caches held by the same index of req, and the 32 pairs of a device read caches held by 32 different indices. `earlier_slot`: exactly one request of each pair continues an earlier cache, every row of earlier_cache is continued by exactly one request, and the 32 pairs of a device continue caches held by 32 different indices of req.
All inputs are finite; a program needn't handle non-finite values.
Results may differ from a plain program's by a relative error of at most 0.0049.
The roundings to bfloat16 on the way count: a program that leaves them out, or rounds other values in their place, can miss the bound.
Values may be sent and summed in bfloat16 or wider, within the bound.
No kernel may reach another device: no remote copies, remote signals or barrier semaphores. Data moves between devices by JAX's collectives and lax.ppermute only.
A program may use at most 64 MiB of HBM per device.

v0:
```python
import jax
import jax.numpy as jnp
from jax import lax
from jax.sharding import PartitionSpec as P

HD = 64


scale_qk = 0.125
neg_fill = -1e30
epsilon = 1e-05


def partial_attend(scores, allowed):
    masked = jnp.where(allowed, scores, neg_fill)
    row_max = jnp.max(masked, axis=-1, keepdims=True)
    weights = jnp.exp(masked - row_max)
    return (row_max[..., 0], jnp.sum(weights, axis=-1), weights.astype(jnp.bfloat16))


def attend_blocks(queries, blocks, allowed):
    block_count, capacity, head_count, head_width = queries.shape
    key_rows = blocks[:, :, 0].reshape(block_count, -1, head_count, head_width)
    value_rows = blocks[:, :, 1].reshape(block_count, -1, head_count, head_width)
    scores = (
        jnp.einsum("nqhd,nkhd->nqhk", queries, key_rows, preferred_element_type=jnp.float32)
        * scale_qk
    )
    row_max, totals, weights = partial_attend(scores, allowed[:, :, None, None])
    result = jnp.einsum("nqhk,nkhd->nqhd", weights, value_rows, preferred_element_type=jnp.float32)
    return (result, row_max, totals)


def place(route_map, payload):
    return jnp.einsum(
        "og,g...->o...", route_map, payload, preferred_element_type=jnp.float32
    ).astype(jnp.bfloat16)


def collect(route_map, payload):
    return jnp.einsum("og,o...->g...", route_map, payload, precision=lax.Precision.HIGHEST)


def owner_prefix(incoming_q, incoming_pick, prefix_cache):
    block_count, capacity, local_width = incoming_q.shape
    head_count = local_width // HD
    stored, span = (prefix_cache.shape[0], prefix_cache.shape[1])
    queries = incoming_q.reshape(block_count, capacity, head_count, HD)
    key_rows = prefix_cache[:, :, 0].reshape(stored, span, head_count, HD)
    value_rows = prefix_cache[:, :, 1].reshape(stored, span, head_count, HD)
    scores = (
        jnp.einsum("nqhd,pkhd->nqhpk", queries, key_rows, preferred_element_type=jnp.float32)
        * scale_qk
    )
    allowed = jnp.broadcast_to((incoming_pick > 0)[:, :, None, :, None], scores.shape)
    flat_shape = (block_count, capacity, head_count, stored * span)
    row_max, totals, weights = partial_attend(
        scores.reshape(flat_shape), allowed.reshape(flat_shape)
    )
    weights = weights.reshape(block_count, capacity, head_count, stored, span)
    result = jnp.einsum("nqhpk,pkhd->nqhd", weights, value_rows, preferred_element_type=jnp.float32)
    return (result.reshape(block_count, capacity, local_width), row_max, totals)


def owner_earlier(incoming_q, incoming_sel, earlier_cache):
    block_count, capacity, local_width = incoming_q.shape
    head_count = local_width // HD
    block_sel = jnp.max(incoming_sel, axis=1)
    blocks = jnp.einsum(
        "nj,jetc->netc", block_sel, earlier_cache, preferred_element_type=jnp.float32
    ).astype(jnp.bfloat16)
    row_on = jnp.max(incoming_sel, axis=2) > 0
    result, row_max, totals = attend_blocks(
        incoming_q.reshape(block_count, capacity, head_count, HD), blocks, row_on
    )
    return (result.reshape(block_count, capacity, local_width), row_max, totals)


def norm_rows(hidden, scale_vec, shift_vec):
    row_mean = jnp.mean(hidden, axis=-1, keepdims=True)
    centred = hidden - row_mean
    row_var = jnp.mean(centred * centred, axis=-1, keepdims=True)
    return centred * lax.rsqrt(row_var + epsilon) * scale_vec + shift_vec


def local(
    tokens,
    qkv_weight,
    out_weight,
    attn_gain,
    attn_shift,
    up_weight,
    down_weight,
    mlp_gain,
    mlp_shift,
    prefix_cache,
    earlier_cache,
    suffix_len,
    prefix_id,
    earlier_slot,
):
    devices = lax.axis_size("req")
    gathered = lax.all_gather(tokens, "tp", axis=1, tiled=True)
    tok_rows, model_width = gathered.shape
    local_width = qkv_weight.shape[2]
    head_count = local_width // HD
    group_count = suffix_len.shape[0] // 2
    capacity = tok_rows // group_count
    stored = prefix_cache.shape[0]
    slot_count = earlier_cache.shape[0]
    qkv_rows = jnp.dot(
        gathered,
        qkv_weight.reshape(model_width, 3 * local_width),
        preferred_element_type=jnp.float32,
    ).astype(jnp.bfloat16)
    qkv_rows = qkv_rows.reshape(group_count, capacity, 3, local_width)
    queries = qkv_rows[:, :, 0]
    query_heads = queries.reshape(group_count, capacity, head_count, HD)
    key_heads = qkv_rows[:, :, 1].reshape(group_count, capacity, head_count, HD)
    value_heads = qkv_rows[:, :, 2].reshape(group_count, capacity, head_count, HD)
    length_pairs = suffix_len.reshape(group_count, 2)
    in_first = jnp.arange(capacity)[None, :] < length_pairs[:, :1]
    causal = (jnp.arange(capacity)[:, None] >= jnp.arange(capacity)[None, :])[None, :, None, :]
    same_req = (in_first[:, :, None] == in_first[:, None, :])[:, :, None, :] & causal
    scores = (
        jnp.einsum("gqhd,gkhd->gqhk", query_heads, key_heads, preferred_element_type=jnp.float32)
        * scale_qk
    )
    own_max, own_total, own_weights = partial_attend(scores, same_req)
    own_out = jnp.einsum(
        "gqhk,gkhd->gqhd", own_weights, value_heads, preferred_element_type=jnp.float32
    )
    prefix_pairs = prefix_id.reshape(group_count, 2)
    owner_pre = prefix_pairs[:, 0] // stored
    route_pre = (jnp.arange(devices)[:, None] == owner_pre[None, :]).astype(jnp.bfloat16)
    local_pick = jnp.where(in_first, prefix_pairs[:, :1], prefix_pairs[:, 1:]) % stored
    pick_hot = (local_pick[:, :, None] == jnp.arange(stored)).astype(jnp.bfloat16)
    send_query = place(route_pre, queries)
    send_pick = place(route_pre, pick_hot)
    slot_pairs = earlier_slot.reshape(group_count, 2)
    slot_group = jnp.maximum(slot_pairs[:, 0], slot_pairs[:, 1])
    owner_erl = slot_group // slot_count
    route_erl = (jnp.arange(devices)[:, None] == owner_erl[None, :]).astype(jnp.bfloat16)
    carry_on = jnp.where(in_first, slot_pairs[:, :1] >= 0, slot_pairs[:, 1:] >= 0)
    slot_hot = (slot_group % slot_count)[:, None] == jnp.arange(slot_count)
    erl_sel = place(route_erl, (carry_on[:, :, None] & slot_hot[:, None, :]).astype(jnp.bfloat16))
    send_erl = place(route_erl, queries)
    got_query, got_pick, got_erl, got_sel = (
        lax.all_to_all(send_query, "req", split_axis=0, concat_axis=0, tiled=True),
        lax.all_to_all(send_pick, "req", split_axis=0, concat_axis=0, tiled=True),
        lax.all_to_all(send_erl, "req", split_axis=0, concat_axis=0, tiled=True),
        lax.all_to_all(erl_sel, "req", split_axis=0, concat_axis=0, tiled=True),
    )
    pre_res = owner_prefix(got_query, got_pick, prefix_cache)
    erl_res = owner_earlier(got_erl, got_sel, earlier_cache)
    returned = (
        lax.all_to_all(pre_res[0], "req", split_axis=0, concat_axis=0, tiled=True),
        lax.all_to_all(pre_res[1], "req", split_axis=0, concat_axis=0, tiled=True),
        lax.all_to_all(pre_res[2], "req", split_axis=0, concat_axis=0, tiled=True),
        lax.all_to_all(erl_res[0], "req", split_axis=0, concat_axis=0, tiled=True),
        lax.all_to_all(erl_res[1], "req", split_axis=0, concat_axis=0, tiled=True),
        lax.all_to_all(erl_res[2], "req", split_axis=0, concat_axis=0, tiled=True),
    )
    pre_back = returned[:3]
    route_erl32 = route_erl.astype(jnp.float32)
    erl_out = collect(route_erl32, returned[3]).reshape(group_count, capacity, head_count, HD)
    erl_max = collect(route_erl32, returned[4])
    erl_total = collect(route_erl32, returned[5])
    route_pre32 = route_pre.astype(jnp.float32)
    pre_out = collect(route_pre32, pre_back[0]).reshape(group_count, capacity, head_count, HD)
    pre_max = collect(route_pre32, pre_back[1])
    pre_total = collect(route_pre32, pre_back[2])
    on_rows = carry_on[:, :, None]
    erl_max = jnp.where(on_rows, erl_max, neg_fill)
    erl_total = jnp.where(on_rows, erl_total, 0.0)
    erl_out = jnp.where(on_rows[..., None], erl_out, 0.0)
    merged_max = jnp.maximum(jnp.maximum(own_max, pre_max), erl_max)
    own_scale = jnp.exp(own_max - merged_max)
    pre_scale = jnp.exp(pre_max - merged_max)
    erl_scale = jnp.exp(erl_max - merged_max)
    merged_total = own_total * own_scale + pre_total * pre_scale + erl_total * erl_scale
    mixed = (
        own_out * own_scale[..., None]
        + pre_out * pre_scale[..., None]
        + erl_out * erl_scale[..., None]
    ) / merged_total[..., None]
    attended = mixed.reshape(tok_rows, local_width).astype(jnp.bfloat16)
    projected_part = jnp.dot(attended, out_weight, preferred_element_type=jnp.float32)
    share_width = tokens.shape[1]
    col_start = lax.axis_index("tp") * share_width
    projected = lax.psum(projected_part, "tp")
    normed = norm_rows(gathered.astype(jnp.float32) + projected, attn_gain, attn_shift).astype(
        jnp.bfloat16
    )
    inner = jax.nn.gelu(
        jnp.dot(normed, up_weight, preferred_element_type=jnp.float32), approximate=False
    ).astype(jnp.bfloat16)
    lowered = lax.psum(jnp.dot(inner, down_weight, preferred_element_type=jnp.float32), "tp")
    encoded = norm_rows(normed.astype(jnp.float32) + lowered, mlp_gain, mlp_shift).astype(
        jnp.bfloat16
    )
    return lax.dynamic_slice_in_dim(encoded, col_start, share_width, 1)


def solution(mesh):
    placed = (
        P("req", "tp"),
        P(None, None, "tp"),
        P("tp", None),
        P(),
        P(),
        P(None, "tp"),
        P("tp", None),
        P(),
        P(),
        P("req", None, None, "tp"),
        P("req", None, None, "tp"),
        P("req"),
        P("req"),
        P("req"),
    )
    return jax.shard_map(
        local, mesh=mesh, in_specs=placed, out_specs=P("req", "tp"), check_vma=False
    )
```

profile of v0, /device:TPU:1, one launch (start us, length us, event | category | flops | bytes accessed | tf_op | source)
XLA Modules:
  0.0 460.2 jit_solution(18138188225698854665)
XLA Ops:
  6.5 0.7 all-gather.2.cloned.1.call-update
  7.3 0.7 reshape.379
  8.0 0.8 reshape.380
  9.4 0.7 copy.173
  10.1 19.1 %all-to-all-start = ((bf16[64,16,2]{1,2,0:T(2,128)(2,1)}), bf16[64,16,2]{1,2,0:T(2,128)(2,1)S(1)}, u32[]{:S(2)}, u32[]{:S(2)}) async-start(bf16[64,16,2]{1,2,0:T(2,128)(2,1)} %copy.173), calls=%async_computation | async-start | bytes 65536 | tf_op jit(solution)/shard_map/all_to_all | solution.py:150
  29.2 0.8 reshape.382
  31.1 0.8 reshape.409
  32.2 14.0 %all-gather.2.cloned.1.call-done = bf16[512,1024]{1,0:T(8,128)(2,1)} async-done(((bf16[512,128]{1,0:T(8,128)(2,1)}), bf16[512,1024]{1,0:T(8,128)(2,1)}) %all-gather.2.cloned.1.call-update) | async-done | bytes 1048592 | tf_op jit(solution)/shard_map/all_gather | solution.py:103
  46.3 2.0 convolution_convert_fusion.1
  48.4 15.4 %all-to-all-start.3 = ((bf16[64,2,256]{2,1,0:T(2,128)(2,1)}), bf16[64,2,256]{2,1,0:T(2,128)(2,1)S(1)}, u32[]{:S(2)}, u32[]{:S(2)}) async-start(bf16[64,2,256]{2,1,0:T(2,128)(2,1)} %reshape.409), calls=%async_computation.3 | async-start | bytes 131072 | tf_op jit(solution)/shard_map/all_to_all | solution.py:152
  63.8 1.6 slice_reduce_fusion.1
  65.8 0.9 copy.188
  66.7 11.1 %all-to-all-done.3 = bf16[64,2,256]{2,1,0:T(2,128)(2,1)S(1)} async-done(((bf16[64,2,256]{2,1,0:T(2,128)(2,1)}), bf16[64,2,256]{2,1,0:T(2,128)(2,1)S(1)}, u32[]{:S(2)}, u32[]{:S(2)}) %all-to-all-start.3) | async-done | bytes 65568 | tf_op jit(solution)/shard_map/all_to_all | solution.py:152
  77.8 4.7 %all-to-all-start.4 = ((bf16[64,16,128]{2,1,0:T(8,128)(2,1)}), bf16[64,16,128]{2,1,0:T(8,128)(2,1)S(1)}, u32[]{:S(2)}, u32[]{:S(2)}) async-start(bf16[64,16,128]{2,1,0:T(8,128)(2,1)} %copy.188), calls=%async_computation.4 | async-start | bytes 524288 | tf_op jit(solution)/shard_map/all_to_all | solution.py:151
  82.5 0.4 fusion.164
  83.6 0.9 copy.174
  84.5 16.1 %all-to-all-done.4 = bf16[64,16,128]{2,1,0:T(8,128)(2,1)S(1)} async-done(((bf16[64,16,128]{2,1,0:T(8,128)(2,1)}), bf16[64,16,128]{2,1,0:T(8,128)(2,1)S(1)}, u32[]{:S(2)}, u32[]{:S(2)}) %all-to-all-start.4) | async-done | bytes 262176 | tf_op jit(solution)/shard_map/all_to_all | solution.py:151
  100.6 8.4 %all-to-all-start.1 = ((bf16[64,16,128]{2,1,0:T(8,128)(2,1)}), bf16[64,16,128]{2,1,0:T(8,128)(2,1)S(1)}, u32[]{:S(2)}, u32[]{:S(2)}) async-start(bf16[64,16,128]{2,1,0:T(8,128)(2,1)} %copy.174), calls=%async_computation.1 | async-start | bytes 524288 | tf_op jit(solution)/shard_map/all_to_all | solution.py:149
  109.8 1.1 reshape_squeeze.25
  110.9 1.0 reshape.383
  111.9 2.4 fusion.165
  114.3 13.1 %all-to-all-done.1 = bf16[64,16,128]{2,1,0:T(8,128)(2,1)S(1)} async-done(((bf16[64,16,128]{2,1,0:T(8,128)(2,1)}), bf16[64,16,128]{2,1,0:T(8,128)(2,1)S(1)}, u32[]{:S(2)}, u32[]{:S(2)}) %all-to-all-start.1) | async-done | bytes 262176 | tf_op jit(solution)/shard_map/all_to_all | solution.py:149
  127.4 8.4 %all-to-all-start.5 = ((f32[64,16,2]{1,2,0:T(2,128)}), f32[64,16,2]{1,2,0:T(2,128)S(1)}, u32[]{:S(2)}, u32[]{:S(2)}) async-start(f32[64,16,2]{1,2,0:T(2,128)} %get-tuple-element.27), calls=%async_computation.5 | async-start | bytes 131072 | tf_op jit(solution)/shard_map/all_to_all | solution.py:161
  135.8 1.1 reshape.381
  136.9 3.6 bitcast_reduce_fusion
  140.5 1.8 fusion.33
  142.3 7.3 %all-to-all-done.5 = f32[64,16,2]{1,2,0:T(2,128)S(1)} async-done(((f32[64,16,2]{1,2,0:T(2,128)}), f32[64,16,2]{1,2,0:T(2,128)S(1)}, u32[]{:S(2)}, u32[]{:S(2)}) %all-to-all-start.5) | async-done | bytes 8224 | tf_op jit(solution)/shard_map/all_to_all | solution.py:161
  149.6 7.1 %all-to-all-start.9 = ((f32[64,16,2]{1,2,0:T(2,128)}), f32[64,16,2]{1,2,0:T(2,128)S(1)}, u32[]{:S(2)}, u32[]{:S(2)}) async-start(f32[64,16,2]{1,2,0:T(2,128)} %fusion.33), calls=%async_computation.9 | async-start | bytes 131072 | tf_op jit(solution)/shard_map/all_to_all | solution.py:162
  156.7 5.3 %fusion.1 = f32[64,16,2]{1,0,2:T(8,128)S(1)} fusion(f32[2,64,16,2,256]{4,2,3,1,0:T(8,128)} %get-tuple-element.30, f32[64,16,2]{1,0,2:T(8,128)S(1)} %get-tuple-element.29, pred[64,16,2]{1,2,0:T(4,128)(4,1)S(1)} %broadcast_compare_fusion), kind=kLoop, calls=%fused_computation.4 | loop fusion | flops 4192256 | bytes 4212736 | tf_op jit(solution)/shard_map/reduce_sum | solution.py:18
  162.0 0.7 copy.209
  162.7 8.0 %all-to-all-done.9 = f32[64,16,2]{1,2,0:T(2,128)S(1)} async-done(((f32[64,16,2]{1,2,0:T(2,128)}), f32[64,16,2]{1,2,0:T(2,128)S(1)}, u32[]{:S(2)}, u32[]{:S(2)}) %all-to-all-start.9) | async-done | bytes 8224 | tf_op jit(solution)/shard_map/all_to_all | solution.py:162
  170.7 6.8 %all-to-all-start.8 = ((f32[64,16,2]{1,2,0:T(2,128)}), f32[64,16,2]{1,2,0:T(2,128)}, u32[]{:S(2)}, u32[]{:S(2)}) async-start(f32[64,16,2]{1,2,0:T(2,128)} %copy.209), calls=%async_computation.8 | async-start | bytes 131072 | tf_op jit(solution)/shard_map/all_to_all | solution.py:159
  177.8 1.5 copy.178
  179.3 12.1 %all-to-all-done.8 = f32[64,16,2]{1,2,0:T(2,128)} async-done(((f32[64,16,2]{1,2,0:T(2,128)}), f32[64,16,2]{1,2,0:T(2,128)}, u32[]{:S(2)}, u32[]{:S(2)}) %all-to-all-start.8) | async-done | bytes 8224 | tf_op jit(solution)/shard_map/all_to_all | solution.py:159
  191.4 4.6 all-to-all-start.2
  195.9 1.4 convolution_bitcast_fusion
  197.3 0.5 copy.203
  197.8 1.4 reshape.386
  199.3 10.7 %all-to-all-done.2 = f32[64,16,2]{1,2,0:T(2,128)S(1)} async-done(((f32[64,16,2]{1,2,0:T(2,128)}), f32[64,16,2]{1,2,0:T(2,128)S(1)}, u32[]{:S(2)}, u32[]{:S(2)}) %all-to-all-start.2) | async-done | bytes 8224 | tf_op jit(solution)/shard_map/all_to_all | solution.py:158
  209.9 4.6 %all-to-all-start.7 = ((f32[64,16,128]{2,1,0:T(8,128)}), f32[64,16,128]{2,1,0:T(8,128)S(1)}, u32[]{:S(2)}, u32[]{:S(2)}) async-start(f32[64,16,128]{2,1,0:T(8,128)} %reshape.386), calls=%async_computation.7 | async-start | bytes 1048576 | tf_op jit(solution)/shard_map/all_to_all | solution.py:160
  214.7 2.9 fusion.8
  217.7 0.8 copy.196
  218.5 1.4 reshape.384
  219.9 22.4 %all-to-all-done.7 = f32[64,16,128]{2,1,0:T(8,128)S(1)} async-done(((f32[64,16,128]{2,1,0:T(8,128)}), f32[64,16,128]{2,1,0:T(8,128)S(1)}, u32[]{:S(2)}, u32[]{:S(2)}) %all-to-all-start.7) | async-done | bytes 524320 | tf_op jit(solution)/shard_map/all_to_all | solution.py:160
  242.3 9.0 %all-to-all-start.6 = ((f32[64,16,128]{2,1,0:T(8,128)}), f32[64,16,128]{2,1,0:T(8,128)S(1)}, u32[]{:S(2)}, u32[]{:S(2)}) async-start(f32[64,16,128]{2,1,0:T(8,128)} %reshape.384), calls=%async_computation.6 | async-start | bytes 1048576 | tf_op jit(solution)/shard_map/all_to_all | solution.py:157
  251.9 0.8 reshape_squeeze.21
  252.9 0.4 fusion.166
  254.4 1.1 fusion.22
  255.8 0.5 fusion.42
  256.6 22.9 %all-to-all-done.6 = f32[64,16,128]{2,1,0:T(8,128)S(1)} async-done(((f32[64,16,128]{2,1,0:T(8,128)}), f32[64,16,128]{2,1,0:T(8,128)S(1)}, u32[]{:S(2)}, u32[]{:S(2)}) %all-to-all-start.6) | async-done | bytes 524320 | tf_op jit(solution)/shard_map/all_to_all | solution.py:157
  279.5 0.5 fusion.45
  280.3 1.9 fusion.19
  282.6 1.7 fusion.169
  284.4 75.6 %all-reduce.3.cloned.1.call-done = f32[512,1024]{1,0:T(8,128)} async-done(((f32[512,1024]{1,0:T(8,128)}), f32[512,1024]{1,0:T(8,128)}) %all-reduce.3.cloned.1.call-update) | async-done | bytes 2097168 | tf_op jit(solution)/shard_map/psum | solution.py:191
  360.0 2.0 fusion.35
  362.3 0.5 multiply_reduce_fusion.1
  362.8 0.5 add_convert_fusion
  363.3 5.9 %fusion.36 = f32[512,1024]{1,0:T(8,128)} fusion(bf16[512,1024]{1,0:T(8,128)(2,1)S(1)} %copy-done, bf16[512,1024]{1,0:T(8,128)(2,1)S(1)} %add_convert_fusion, bf16[1024,512]{1,0:T(8,128)(2,1)} %param.19), kind=kOutput, calls=%fused_computation.63 | convolution fusion | flops 1090781184 | bytes 5242880 | tf_op jit(solution)/shard_map/dot_general | solution.py:198
  369.3 0.8 dynamic-slice
  370.0 0.8 dynamic-slice.1
  370.8 79.4 %all-reduce.5.cloned.1.call-done = f32[512,1024]{1,0:T(8,128)} async-done(((f32[512,1024]{1,0:T(8,128)}), f32[512,1024]{1,0:T(8,128)}) %all-reduce.5.cloned.1.call-update) | async-done | bytes 2097168 | tf_op jit(solution)/shard_map/psum | solution.py:198
  450.2 2.0 fusion.7
  452.4 0.5 multiply_reduce_fusion
  452.9 0.8 fusion.85
  (105 shorter events, 8.0 us)
Async XLA Ops:
  6.5 356.8 %copy-start = (bf16[512,1024]{1,0:T(8,128)(2,1)S(1)}, bf16[512,1024]{1,0:T(8,128)(2,1)}, u32[]{:S(2)}) copy-start(bf16[512,1024]{1,0:T(8,128)(2,1)} %param.20) | copy-start | bytes 3145732
  6.5 25.4 %copy-start.5 = (bf16[1024,3,128]{2,0,1:T(8,128)(2,1)S(1)}, bf16[1024,3,128]{2,0,1:T(8,128)(2,1)}, u32[]{:S(2)}) copy-start(bf16[1024,3,128]{2,0,1:T(8,128)(2,1)} %param.15) | copy-start | bytes 2359300
  6.5 39.7 %all-gather.2.cloned.1.call-start = ((), (), s32[]{:S(2)}) async-start(), calls=%async_computation.10 | async-start | bytes 1179648 | tf_op jit(solution)/shard_map/all_gather | solution.py:103
  9.2 74.1 %copy-start.18 = (s32[32]{0:T(128)}, s32[32]{0:T(128)S(1)}, u32[]{:S(2)}) copy-start(s32[32]{0:T(128)S(1)} %and_select_fusion.1) | copy-start | bytes 388
  10.1 38.3 %all-to-all-start = ((bf16[64,16,2]{1,2,0:T(2,128)(2,1)}), bf16[64,16,2]{1,2,0:T(2,128)(2,1)S(1)}, u32[]{:S(2)}, u32[]{:S(2)}) async-start(bf16[64,16,2]{1,2,0:T(2,128)(2,1)} %copy.173), calls=%async_computation | async-start | bytes 65536 | tf_op jit(solution)/shard_map/all_to_all | solution.py:150
  48.2 34.2 %copy-start.4 = (bf16[2,256,2,128]{3,2,1,0:T(2,128)(2,1)S(1)}, bf16[2,256,2,128]{3,2,1,0:T(2,128)(2,1)}, u32[]{:S(2)}) copy-start(bf16[2,256,2,128]{3,2,1,0:T(2,128)(2,1)} %param.23) | copy-start | bytes 786436
  48.4 29.4 %all-to-all-start.3 = ((bf16[64,2,256]{2,1,0:T(2,128)(2,1)}), bf16[64,2,256]{2,1,0:T(2,128)(2,1)S(1)}, u32[]{:S(2)}, u32[]{:S(2)}) async-start(bf16[64,2,256]{2,1,0:T(2,128)(2,1)} %reshape.409), calls=%async_computation.3 | async-start | bytes 131072 | tf_op jit(solution)/shard_map/all_to_all | solution.py:152
  66.7 42.8 %copy-start.8 = (bf16[32,16,2,128]{3,2,1,0:T(2,128)(2,1)S(1)}, bf16[32,16,2,128]{3,2,1,0:T(2,128)(2,1)}, u32[]{:S(2)}) copy-start(bf16[32,16,2,128]{3,2,1,0:T(2,128)(2,1)} %param.24) | copy-start | bytes 786436
  77.8 22.8 %all-to-all-start.4 = ((bf16[64,16,128]{2,1,0:T(8,128)(2,1)}), bf16[64,16,128]{2,1,0:T(8,128)(2,1)S(1)}, u32[]{:S(2)}, u32[]{:S(2)}) async-start(bf16[64,16,128]{2,1,0:T(8,128)(2,1)} %copy.188), calls=%async_computation.4 | async-start | bytes 524288 | tf_op jit(solution)/shard_map/all_to_all | solution.py:151
  83.0 73.7 %copy-start.16 = (pred[64,16,2]{1,2,0:T(4,128)(4,1)}, pred[64,16,2]{1,2,0:T(4,128)(4,1)S(1)}, u32[]{:S(2)}) copy-start(pred[64,16,2]{1,2,0:T(4,128)(4,1)S(1)} %broadcast_compare_fusion) | copy-start | bytes 6148
  100.6 26.8 %all-to-all-start.1 = ((bf16[64,16,128]{2,1,0:T(8,128)(2,1)}), bf16[64,16,128]{2,1,0:T(8,128)(2,1)S(1)}, u32[]{:S(2)}, u32[]{:S(2)}) async-start(bf16[64,16,128]{2,1,0:T(8,128)(2,1)} %copy.174), calls=%async_computation.1 | async-start | bytes 524288 | tf_op jit(solution)/shard_map/all_to_all | solution.py:149
  127.4 22.2 %all-to-all-start.5 = ((f32[64,16,2]{1,2,0:T(2,128)}), f32[64,16,2]{1,2,0:T(2,128)S(1)}, u32[]{:S(2)}, u32[]{:S(2)}) async-start(f32[64,16,2]{1,2,0:T(2,128)} %get-tuple-element.27), calls=%async_computation.5 | async-start | bytes 131072 | tf_op jit(solution)/shard_map/all_to_all | solution.py:161
  140.5 21.5 %copy-start.6 = (f32[64,16,2]{1,0,2:T(8,128)}, f32[64,16,2]{1,0,2:T(8,128)S(1)}, u32[]{:S(2)}) copy-start(f32[64,16,2]{1,0,2:T(8,128)S(1)} %get-tuple-element.29) | copy-start | bytes 24580
  149.6 12.4 %copy-start.10 = (f32[64,16,2]{1,2,0:T(2,128)}, f32[64,16,2]{1,2,0:T(2,128)S(1)}, u32[]{:S(2)}) copy-start(f32[64,16,2]{1,2,0:T(2,128)S(1)} %all-to-all-done.5) | copy-start | bytes 24580
  149.6 21.1 %all-to-all-start.9 = ((f32[64,16,2]{1,2,0:T(2,128)}), f32[64,16,2]{1,2,0:T(2,128)S(1)}, u32[]{:S(2)}, u32[]{:S(2)}) async-start(f32[64,16,2]{1,2,0:T(2,128)} %fusion.33), calls=%async_computation.9 | async-start | bytes 131072 | tf_op jit(solution)/shard_map/all_to_all | solution.py:162
  170.7 6.8 %copy-start.12 = (f32[64,16,2]{1,2,0:T(2,128)}, f32[64,16,2]{1,2,0:T(2,128)S(1)}, u32[]{:S(2)}) copy-start(f32[64,16,2]{1,2,0:T(2,128)S(1)} %all-to-all-done.9) | copy-start | bytes 24580
  170.7 20.7 %all-to-all-start.8 = ((f32[64,16,2]{1,2,0:T(2,128)}), f32[64,16,2]{1,2,0:T(2,128)}, u32[]{:S(2)}, u32[]{:S(2)}) async-start(f32[64,16,2]{1,2,0:T(2,128)} %copy.209), calls=%async_computation.8 | async-start | bytes 131072 | tf_op jit(solution)/shard_map/all_to_all | solution.py:159
  191.4 18.5 %all-to-all-start.2 = ((f32[64,16,2]{1,2,0:T(2,128)}), f32[64,16,2]{1,2,0:T(2,128)S(1)}, u32[]{:S(2)}, u32[]{:S(2)}) async-start(f32[64,16,2]{1,2,0:T(2,128)} %copy.178), calls=%async_computation.2 | async-start | bytes 131072 | tf_op jit(solution)/shard_map/all_to_all | solution.py:158
  197.3 17.4 %copy-start.7 = (f32[64,16,2]{1,0,2:T(8,128)S(1)}, f32[64,16,2]{1,0,2:T(8,128)}, u32[]{:S(2)}) copy-start(f32[64,16,2]{1,0,2:T(8,128)} %copy-done.6) | copy-start | bytes 24580
  197.3 17.4 %copy-start.17 = (pred[64,16,2]{1,2,0:T(4,128)(4,1)S(1)}, pred[64,16,2]{1,2,0:T(4,128)(4,1)}, u32[]{:S(2)}) copy-start(pred[64,16,2]{1,2,0:T(4,128)(4,1)} %copy-done.16) | copy-start | bytes 6148
  209.9 4.8 %copy-start.14 = (f32[64,16,2]{1,2,0:T(2,128)}, f32[64,16,2]{1,2,0:T(2,128)S(1)}, u32[]{:S(2)}) copy-start(f32[64,16,2]{1,2,0:T(2,128)S(1)} %all-to-all-done.2) | copy-start | bytes 24580
  209.9 32.4 %all-to-all-start.7 = ((f32[64,16,128]{2,1,0:T(8,128)}), f32[64,16,128]{2,1,0:T(8,128)S(1)}, u32[]{:S(2)}, u32[]{:S(2)}) async-start(f32[64,16,128]{2,1,0:T(8,128)} %reshape.386), calls=%async_computation.7 | async-start | bytes 1048576 | tf_op jit(solution)/shard_map/all_to_all | solution.py:160
  219.9 33.7 %copy-start.15 = (f32[64,16,2]{1,2,0:T(2,128)S(1)}, f32[64,16,2]{1,2,0:T(2,128)}, u32[]{:S(2)}) copy-start(f32[64,16,2]{1,2,0:T(2,128)} %copy-done.14) | copy-start | bytes 24580
  219.9 33.7 %copy-start.19 = (s32[32]{0:T(128)S(1)}, s32[32]{0:T(128)}, u32[]{:S(2)}) copy-start(s32[32]{0:T(128)} %copy-done.18) | copy-start | bytes 388
  219.9 34.0 %copy-start.11 = (f32[64,16,2]{1,2,0:T(2,128)S(1)}, f32[64,16,2]{1,2,0:T(2,128)}, u32[]{:S(2)}) copy-start(f32[64,16,2]{1,2,0:T(2,128)} %copy-done.10) | copy-start | bytes 24580
  242.3 37.2 %all-to-all-start.6 = ((f32[64,16,128]{2,1,0:T(8,128)}), f32[64,16,128]{2,1,0:T(8,128)S(1)}, u32[]{:S(2)}, u32[]{:S(2)}) async-start(f32[64,16,128]{2,1,0:T(8,128)} %reshape.384), calls=%async_computation.6 | async-start | bytes 1048576 | tf_op jit(solution)/shard_map/all_to_all | solution.py:157
  251.3 4.1 copy-start.13
  251.3 108.7 %all-reduce.3.cloned.1.call-start = ((), (), s32[]{:S(2)}) async-start(), calls=%async_computation.11 | async-start | bytes 4194304 | tf_op jit(solution)/shard_map/psum | solution.py:191
  252.9 26.6 %copy-start.20 = (s32[32]{0:T(128)S(1)}, s32[32]{0:T(128)}, u32[]{:S(2)}) copy-start(s32[32]{0:T(128)} %copy-done.18) | copy-start | bytes 388
  280.3 2.3 copy-start.9
  282.6 77.4 %copy-start.2 = (bf16[512,1024]{1,0:T(8,128)(2,1)S(1)}, bf16[512,1024]{1,0:T(8,128)(2,1)}, u32[]{:S(2)}) copy-start(bf16[512,1024]{1,0:T(8,128)(2,1)} %all-gather.2.cloned.1.call-done) | copy-start | bytes 3145732
  284.4 165.8 %all-reduce.5.cloned.1.call-start = ((), (), s32[]{:S(2)}) async-start(), calls=%async_computation.12 | async-start | bytes 4194304 | tf_op jit(solution)/shard_map/psum | solution.py:198
  360.0 2.2 copy-start.1
  362.1 0.7 copy-start.21
  362.1 0.7 copy-start.22
  450.2 2.2 copy-start.3
Sparse Core Ops, SparseCore 0:
  9.5 36.7 all-gather.1
  284.5 75.4 all-reduce.2
  369.4 80.7 all-reduce.4
where the time goes:
time: 462 us; the launch traced here: 460 us
  waiting for transfers between devices  293 us (63%)
  starting transfers between devices  88.3 us (19%)
  matrix products  26.3 us (6%)
  local copies, waits for them, and re-layouts  23.7 us (5%)
  other arithmetic  14.7 us (3%)
  between operations  13.8 us (3%)
    psum x1, waiting for transfers between devices, local(): lax.psum(jnp.dot(inner, down_weight, preferred_element_type=jnp.float32),...  79.4 us
    psum x1, waiting for transfers between devices, local(): projected = lax.psum(projected_part, 'tp')  75.6 us
    all_to_all x1, waiting for transfers between devices, local(): lax.all_to_all(pre_res[0], 'req', split_axis=0, concat_axis=0, tiled=True)  22.9 us
    all_to_all x1, waiting for transfers between devices, local(): lax.all_to_all(erl_res[0], 'req', split_axis=0, concat_axis=0, tiled=True)  22.4 us
    all_to_all x1, starting transfers between devices, local(): lax.all_to_all(send_pick, 'req', split_axis=0, concat_axis=0, tiled=True)  19.1 us
    all_to_all x1, waiting for transfers between devices, local(): lax.all_to_all(send_erl, 'req', split_axis=0, concat_axis=0, tiled=True)  16.1 us
    all_to_all x1, starting transfers between devices, local(): lax.all_to_all(erl_sel, 'req', split_axis=0, concat_axis=0, tiled=True)  15.4 us
    all_gather x1, waiting for transfers between devices, local(): gathered = lax.all_gather(tokens, 'tp', axis=1, tiled=True)  14 us
  transfers between devices with their start and end apart: 13, of which 12 were waited for; matrix products, arithmetic and copies ran while one was open for 10% of the time, Pallas kernels for 0%

commit v1 on v0

v1 whole, which is shorter than its diff:
```python
import jax
import jax.numpy as jnp
from jax import lax
from jax.experimental import pallas as pl
from jax.experimental.pallas import tpu as pltpu
from jax.sharding import Mesh, PartitionSpec as P

HD = 64
REQ = ("z", "x")
TP = ("y", "c")
SCALE = 0.125
NEG = -1e30
EPS = 1e-05
bf16 = jnp.bfloat16
f32 = jnp.float32

VM = pl.BlockSpec(memory_space=pltpu.VMEM)
SM = pl.BlockSpec(memory_space=pltpu.SMEM)


def iota(shape, axis):
    return lax.broadcasted_iota(jnp.int32, shape, axis)


def head_mask(x, h):
    lane = iota(x.shape, len(x.shape) - 1)
    return jnp.where((lane >= HD) == (h == 1), x, jnp.zeros_like(x))


def dot_t(a, b):
    return lax.dot_general(a, b, (((1,), (1,)), ((), ())), preferred_element_type=f32)


def dot(a, b):
    return jnp.dot(a, b, preferred_element_type=f32)


def softmax_parts(scores, allowed):
    masked = scores if allowed is None else jnp.where(allowed, scores, NEG)
    top = jnp.max(masked, axis=-1, keepdims=True)
    weights = jnp.exp(masked - top)
    total = jnp.sum(weights, axis=-1, keepdims=True)
    return weights.astype(bf16), 1.0 / total, top + jnp.log(total)


def qkv_kernel(pairs, own_ref, far_ref, w_ref, info_ref, send_ref, qkv_ref):
    slots = send_ref.shape[0]
    row = iota((16, 128), 0)
    for b in range(slots // 8):
        rows = pl.ds(8 * b, 8)
        send_ref[rows, 0:16, :] = jnp.zeros((8, 16, 128), bf16)
        base = jnp.broadcast_to(info_ref[rows, :][:, None, :], (8, 16, 128))
        send_ref[rows, 16:32, :] = jnp.where(row[None] == 15, base, 0.0).astype(bf16)

    def block(b, carry):
        r0 = pl.multiple_of(b * 128, 128)
        rows = pl.ds(r0, 128)
        parts = [own_ref[i, rows, :] for i in range(4)] + [far_ref[i, rows, :] for i in range(4)]
        out = dot(jnp.concatenate(parts, axis=1), w_ref[...])
        qkv_ref[rows, :] = out.astype(bf16)
        q = out[:, :128].astype(bf16)
        for p in range(8):
            g = b * 8 + p
            qp = q[16 * p : 16 * p + 16]
            send_ref[pairs[0, g], 0:16, :] = qp
            qf = qp.astype(f32)
            moved = jnp.where(pairs[2, g] == 1, pltpu.roll(qf, 15, 0), qf)
            slot = pairs[1, g]
            held = send_ref[slot, 16:32, :].astype(f32)
            send_ref[slot, 16:32, :] = jnp.where(row == 15, held, moved).astype(bf16)
        return carry

    lax.fori_loop(0, 4, block, 0)


def own_kernel(qkv_ref, len_ref, out_ref, lse_ref):
    r = iota((128, 128), 0)
    c = iota((128, 128), 1)

    def block(b, carry):
        rows = pl.ds(pl.multiple_of(b * 128, 128), 128)
        q = qkv_ref[rows, 0:128]
        k = qkv_ref[rows, 128:256]
        v = qkv_ref[rows, 256:384]
        span = len_ref[rows, :]
        same = ((r // 16) == (c // 16)) & (c <= r) & (((r % 16) < span) == ((c % 16) < span))
        res = []
        for h in range(2):
            w, inv, lse = softmax_parts(dot_t(head_mask(q, h), k) * SCALE, same)
            res.append((dot(w, v) * inv, jnp.broadcast_to(lse, (128, 128))))
        out_ref[rows, :] = head_mask(res[0][0], 0) + head_mask(res[1][0], 1)
        lse_ref[rows, :] = head_mask(res[0][1], 0) + head_mask(res[1][1], 1)
        return carry

    lax.fori_loop(0, 4, block, 0)


def owner_kernel(got_ref, pk_ref, pv_ref, ek_ref, ev_ref, ret_ref):
    sub = iota((8, 16, 128), 1)
    lane = iota((8, 16, 128), 2)
    key_row = iota((128, 512), 1) // 16

    def block(b, carry):
        slots = pl.ds(b * 8, 8)
        q_pre = got_ref[slots, 0:16, :].reshape(128, 128)
        erl_in = got_ref[slots, 16:32, :]
        q_erl = erl_in.reshape(128, 128)
        info = jnp.broadcast_to(erl_in.astype(f32)[:, 15:16, :], (8, 16, 128))
        pick = jnp.sum(jnp.where(lane == sub, info, 0.0), axis=-1, keepdims=True)
        pick = pick.reshape(128, 1) > 0.5
        row_j = jnp.sum(jnp.where(lane == 16, info, 0.0), axis=-1, keepdims=True)
        row_j = row_j.reshape(128, 1).astype(jnp.int32) - 1
        mine = key_row == row_j
        pre, erl, stats = [], [], []
        for h in range(2):
            q = head_mask(q_pre, h)
            s = jnp.where(pick, dot_t(q, pk_ref[1]), dot_t(q, pk_ref[0])) * SCALE
            w, inv, lse = softmax_parts(s, None)
            none = jnp.zeros_like(w)
            o = dot(jnp.where(pick, none, w), pv_ref[0]) + dot(jnp.where(pick, w, none), pv_ref[1])
            pre.append(o * inv)
            stats.append(lse)
        for h in range(2):
            w, inv, lse = softmax_parts(dot_t(head_mask(q_erl, h), ek_ref[...]) * SCALE, mine)
            erl.append(dot(w, ev_ref[...]) * inv)
            stats.append(lse)
        ret_ref[slots, 0:16, :] = (
            (head_mask(pre[0], 0) + head_mask(pre[1], 1)).astype(bf16).reshape(8, 16, 128)
        )
        erl_out = (head_mask(erl[0], 0) + head_mask(erl[1], 1)).reshape(8, 16, 128)
        group = lane // 16
        spread = jnp.zeros((8, 16, 128), f32)
        for n in range(4):
            want = ((group // 4) * 2 + group % 2) == n
            spread = jnp.where(want, stats[n].reshape(8, 16, 1), spread)
        line = jnp.sum(jnp.where(lane % 16 == sub, spread, 0.0), axis=1, keepdims=True)
        high = line.astype(bf16).astype(f32)
        line = jnp.where((group[:, 0:1] // 2) % 2 == 1, line - high, high)
        ret_ref[slots, 16:32, :] = jnp.where(
            sub == 15, jnp.broadcast_to(line, (8, 16, 128)), erl_out
        ).astype(bf16)
        return carry

    lax.fori_loop(0, 8, block, 0)


def merge_kernel(
    pairs, ret_ref, own_ref, lse_ref, out_ref, pre_o, pre_s, erl_o, erl_s, erl_on
):
    row = iota((16, 128), 0)
    lane = iota((16, 128), 1)
    diag = (lane % 16) == row

    def block(b, carry):
        for p in range(8):
            g = b * 8 + p
            rows = pl.ds(pl.multiple_of(b * 128, 128) + 16 * p, 16)
            slot, slot_e, second, span = pairs[0, g], pairs[1, g], pairs[2, g], pairs[3, g]
            pre_o[rows, :] = ret_ref[slot, 0:16, :].astype(f32)
            line = jnp.broadcast_to(ret_ref[slot, 16:32, :].astype(f32)[15:16, :], (16, 128))
            pre_s[rows, :] = jnp.where(diag & (lane < 64), line, 0.0)
            part = ret_ref[slot_e, 16:32, :].astype(f32)
            line = jnp.broadcast_to(part[15:16, :], (16, 128))
            stat = jnp.where(diag & (lane >= 64), line, 0.0)
            late = second == 1
            erl_o[rows, :] = jnp.where(late, pltpu.roll(part, 1, 0), part)
            erl_s[rows, :] = jnp.where(late, pltpu.roll(stat, 1, 0), stat)
            erl_on[rows, :] = ((row < span) == jnp.logical_not(late)).astype(f32)
        rows = pl.ds(pl.multiple_of(b * 128, 128), 128)
        a = iota((128, 128), 0)
        c = iota((128, 128), 1)
        pick = (((a // 16) % 2) == (c // 64)).astype(bf16)
        l_pre = dot(pre_s[rows, :].astype(bf16), pick)
        l_erl = dot(erl_s[rows, :].astype(bf16), pick)
        on = erl_on[rows, :] > 0.5
        l_erl = jnp.where(on, l_erl, NEG)
        l_own = lse_ref[rows, :]
        top = jnp.maximum(jnp.maximum(l_own, l_pre), l_erl)
        w_own = jnp.exp(l_own - top)
        w_pre = jnp.exp(l_pre - top)
        w_erl = jnp.exp(l_erl - top)
        mixed = w_own * own_ref[rows, :] + w_pre * pre_o[rows, :]
        mixed = mixed + w_erl * jnp.where(on, erl_o[rows, :], 0.0)
        out_ref[rows, :] = (mixed / (w_own + w_pre + w_erl)).astype(bf16)
        return carry

    lax.fori_loop(0, 4, block, 0)


def norm_rows(hidden, gain, shift):
    mean = jnp.mean(hidden, axis=-1, keepdims=True)
    centred = hidden - mean
    var = jnp.mean(centred * centred, axis=-1, keepdims=True)
    return centred * lax.rsqrt(var + EPS) * gain + shift


def tail_kernel(
    att_ref, tok_ref, w_out, ag_ref, as_ref, mg_ref, ms_ref, up_ref, down_ref, out_ref, normed, acc
):
    t = pl.program_id(0)

    @pl.when(t == 0)
    def _():
        att = jnp.concatenate([att_ref[i] for i in range(8)], axis=1)
        proj = [
            dot(att, w_out[:, 128 * n : 128 * n + 128, :].reshape(1024, 512)) for n in range(2)
        ]
        hidden = tok_ref[...].astype(f32) + jnp.concatenate(proj, axis=1)
        normed[...] = norm_rows(hidden, ag_ref[...], as_ref[...]).astype(bf16)
        acc[...] = jnp.zeros_like(acc)

    h = dot(normed[...], up_ref[0])
    inner = (0.5 * h * (1.0 + lax.erf(h * 0.7071067811865476))).astype(bf16)
    for n in range(2):
        cols = pl.ds(512 * n, 512)
        acc[:, cols] += dot(inner, down_ref[0, 512 * n : 512 * n + 512, :])

    @pl.when(t == 7)
    def _():
        hidden = normed[...].astype(f32) + acc[...]
        done = norm_rows(hidden, mg_ref[...], ms_ref[...]).astype(bf16)
        for i in range(8):
            out_ref[i] = done[:, 128 * i : 128 * i + 128]


def swap_all(value, axis):
    return lax.all_to_all(value, axis, split_axis=0, concat_axis=0, tiled=True)


def cost(flops, size, trans=0):
    return pl.CostEstimate(flops=flops, bytes_accessed=size, transcendentals=trans)


def local(
    tokens,
    qkv_weight,
    out_weight,
    attn_gain,
    attn_shift,
    up_weight,
    down_weight,
    mlp_gain,
    mlp_shift,
    prefix_cache,
    earlier_cache,
    suffix_len,
    prefix_id,
    earlier_slot,
):
    n_req = lax.axis_size(REQ)
    core = lax.axis_index("c")
    rank = lax.axis_index(TP)

    own_half = swap_all(jnp.broadcast_to(tokens[None], (4, 512, 128)), "y")
    far_half = lax.ppermute(own_half, "c", [(0, 1), (1, 0)])

    shards = jnp.concatenate(
        [
            up_weight,
            down_weight[:, :512],
            down_weight[:, 512:],
            out_weight[:, :512],
            out_weight[:, 512:],
        ],
        axis=0,
    )
    shards = lax.all_gather(shards, TP, axis=0, tiled=False)

    lengths = suffix_len.reshape(32, 2)[:, 0]
    prefix = prefix_id.reshape(32, 2)
    slots = earlier_slot.reshape(32, 2)
    own_pre = prefix[:, 0] // 2
    slot = jnp.maximum(slots[:, 0], slots[:, 1])
    own_erl = slot // 32
    second = (slots[:, 1] >= 0).astype(jnp.int32)
    pairs = jnp.stack([own_pre, own_erl, second, lengths])
    idx = jnp.arange(16)
    picks = jnp.where(idx[None] < lengths[:, None], prefix[:, :1] % 2, prefix[:, 1:] % 2)
    owners = jnp.arange(n_req)[:, None]
    info_pre = jnp.sum(
        jnp.where((owners == own_pre[None])[:, :, None], picks[None], 0), axis=1
    )
    info_erl = jnp.sum(jnp.where(owners == own_erl[None], slot[None] % 32 + 1, 0), axis=1)
    info = jnp.concatenate(
        [info_pre, info_erl[:, None], jnp.zeros((n_req, 111), jnp.int32)], axis=1
    ).astype(f32)

    w_split = qkv_weight.reshape(4, 2, 128, 384)
    w_own = jnp.where(core == 0, w_split[:, 0], w_split[:, 1]).reshape(512, 384)
    w_far = jnp.where(core == 0, w_split[:, 1], w_split[:, 0]).reshape(512, 384)
    w_qkv = jnp.concatenate([w_own, w_far], axis=0)

    send, qkv = pl.pallas_call(
        qkv_kernel,
        in_specs=[SM, VM, VM, VM, VM],
        out_specs=[VM, VM],
        out_shape=[
            jax.ShapeDtypeStruct((n_req, 32, 128), bf16),
            jax.ShapeDtypeStruct((512, 384), bf16),
        ],
        cost_estimate=cost(2 * 512 * 1024 * 384, 3 << 20),
        name="qkv_place",
    )(pairs, own_half, far_half, w_qkv, info)

    got = swap_all(send, REQ)

    len_rows = jnp.broadcast_to(lengths[:, None, None], (32, 16, 1)).reshape(512, 1)
    own_out, own_lse = pl.pallas_call(
        own_kernel,
        in_specs=[VM, VM],
        out_specs=[VM, VM],
        out_shape=[jax.ShapeDtypeStruct((512, 128), f32)] * 2,
        cost_estimate=cost(2 * 512 * 128 * 128 * 4, 1 << 20, 2 * 512 * 128),
        name="own_attention",
    )(qkv, len_rows)

    ret = pl.pallas_call(
        owner_kernel,
        in_specs=[VM] * 5,
        out_specs=VM,
        out_shape=jax.ShapeDtypeStruct((n_req, 32, 128), bf16),
        cost_estimate=cost(2 * 1024 * 128 * 4096, 2 << 20, 2 * 1024 * 768),
        name="owner_attention",
    )(
        got,
        prefix_cache[:, :, 0],
        prefix_cache[:, :, 1],
        earlier_cache[:, :, 0].reshape(512, 128),
        earlier_cache[:, :, 1].reshape(512, 128),
    )

    back = swap_all(ret, REQ)

    attended = pl.pallas_call(
        merge_kernel,
        in_specs=[SM, VM, VM, VM],
        out_specs=VM,
        out_shape=jax.ShapeDtypeStruct((512, 128), bf16),
        scratch_shapes=[pltpu.VMEM((512, 128), f32)] * 5,
        cost_estimate=cost(2 * 512 * 128 * 256, 1 << 20, 3 * 512 * 128),
        name="merge",
    )(pairs, back, own_out, own_lse)

    att = swap_all(attended.reshape(8, 64, 128), TP)

    own_rows = lax.dynamic_slice_in_dim(own_half, rank * 64, 64, 1)
    far_rows = lax.dynamic_slice_in_dim(far_half, rank * 64, 64, 1)
    even = jnp.where(core == 0, own_rows, far_rows)
    odd = jnp.where(core == 0, far_rows, own_rows)
    tok_rows = jnp.stack([even, odd], axis=1).transpose(2, 0, 1, 3).reshape(64, 1024)

    whole = lambda *shape: pl.BlockSpec(shape, lambda t: (0,) * len(shape))
    encoded = pl.pallas_call(
        tail_kernel,
        grid=(8,),
        in_specs=[
            whole(8, 64, 128),
            whole(64, 1024),
            pl.BlockSpec((8, 256, 512), lambda t: (0, 8, 0)),
            whole(1, 1024),
            whole(1, 1024),
            whole(1, 1024),
            whole(1, 1024),
            pl.BlockSpec((1, 1024, 512), lambda t: (t, 0, 0)),
            pl.BlockSpec((1, 1024, 512), lambda t: (t, 1, 0)),
        ],
        out_specs=whole(8, 64, 128),
        out_shape=jax.ShapeDtypeStruct((8, 64, 128), bf16),
        scratch_shapes=[pltpu.VMEM((64, 1024), bf16), pltpu.VMEM((64, 1024), f32)],
        compiler_params=pltpu.CompilerParams(vmem_limit_bytes=32 << 20),
        cost_estimate=cost(2 * 64 * 9 * 1024 * 1024, 19 << 20, 64 * 4096),
        name="project_norm_ffn",
    )(
        att,
        tok_rows,
        shards,
        attn_gain.reshape(1, 1024),
        attn_shift.reshape(1, 1024),
        mlp_gain.reshape(1, 1024),
        mlp_shift.reshape(1, 1024),
        shards,
        shards,
    )
    return swap_all(encoded, TP).reshape(512, 128)


def solution(mesh):
    split = Mesh(mesh.devices.reshape(16, 4, 4, 2), ("z", "x", "y", "c"))
    placed = (
        P(REQ, TP),
        P(None, None, TP),
        P(TP, None),
        P(),
        P(),
        P(None, TP),
        P(TP, None),
        P(),
        P(),
        P(REQ, None, None, TP),
        P(REQ, None, None, TP),
        P(REQ),
        P(REQ),
        P(REQ),
    )
    return jax.shard_map(
        local, mesh=split, in_specs=placed, out_specs=P(REQ, TP), check_vma=False
    )
```

time: 462 us -> 180 us (0.39)
  waiting for transfers between devices: 293 us -> 59.5 us
  starting transfers between devices: 88.3 us -> 43.8 us
  Pallas kernels: 0 us -> 28.1 us
  matrix products: 26.3 us -> 0 us
  other arithmetic: 14.7 us -> 5.82 us
  blocking collectives: 0 us -> 8.52 us
    psum x2 -> x0, waiting for transfers between devices: 155 us -> none  [the longest x1 79.4 us: local(): lax.psum(jnp.dot(inner, down_weight, preferred_element_type=jnp.float32),...]
    all_to_all x10 -> x4, waiting for transfers between devices: 124 us -> 59.5 us  [swap_all(): return lax.all_to_all(value, axis, split_axis=0, concat_axis=0, tiled=True)]
    all_to_all x10 -> x4, starting transfers between devices: 88 us -> 35.5 us  [swap_all(): return lax.all_to_all(value, axis, split_axis=0, concat_axis=0, tiled=True)]
    pallas_call x0 -> x5, Pallas kernels: none -> 28.1 us  [the longest x1 11.6 us: local(): pl.pallas_call(owner_kernel, in_specs=[VM] * 5, out_specs=VM, out_shape=j...]
    dot_general x19 -> x0, matrix products: 26.1 us -> none  [the longest x1 5.9 us: local(): jnp.dot(inner, down_weight, preferred_element_type=jnp.float32)]
    all_gather x1, waiting for transfers between devices: 14 us -> 0.01 us  [local(): shards = lax.all_gather(shards, TP, axis=0, tiled=False)]
    reduce_sum x7 -> x2, other arithmetic: 12.3 us -> 0.23 us  [the longest x1 0.14 us: local(): jnp.sum(jnp.where((owners == own_pre[None])[:, :, None], picks[None], 0),...]
    unnamed x53 -> x46, local copies, waits for them, and re-layouts: 2.23 us -> 14.1 us
  transfers between devices with their start and end apart: 13 -> 6, of which waited for: 12 -> 4; matrix products, arithmetic and copies ran while one was open for 10% -> 7% of each run, Pallas kernels for 0% -> 13%
where the time goes in v1:
time: 180 us
  waiting for transfers between devices  59.5 us (33%)
  starting transfers between devices  43.8 us (24%)
  Pallas kernels  28.1 us (16%)
  local copies, waits for them, and re-layouts  20 us (11%)
  between operations  13.7 us (8%)
  blocking collectives  8.52 us (5%)
  other arithmetic  5.82 us (3%)
    all_to_all x4, waiting for transfers between devices, swap_all(): return lax.all_to_all(value, axis, split_axis=0, concat_axis=0, tiled=True)  59.5 us
    all_to_all x4, starting transfers between devices, swap_all(): return lax.all_to_all(value, axis, split_axis=0, concat_axis=0, tiled=True)  35.5 us
    unnamed x46, local copies, waits for them, and re-layouts  14.1 us
    pallas_call x1, Pallas kernels, local(): pl.pallas_call(owner_kernel, in_specs=[VM] * 5, out_specs=VM, out_shape=j...  11.6 us
    all_to_all x1, blocking collectives, swap_all(): return lax.all_to_all(value, axis, split_axis=0, concat_axis=0, tiled=True)  8.52 us
    ppermute x1, starting transfers between devices, local(): far_half = lax.ppermute(own_half, 'c', [(0, 1), (1, 0)])  8.35 us
    pallas_call x1, Pallas kernels, local(): pl.pallas_call(tail_kernel, grid=(8,), in_specs=[whole(8, 64, 128), whole...  5.64 us
    pallas_call x1, Pallas kernels, local(): pl.pallas_call(own_kernel, in_specs=[VM, VM], out_specs=[VM, VM], out_sha...  4.28 us
  transfers between devices with their start and end apart: 6, of which 4 were waited for; matrix products, arithmetic and copies ran while one was open for 7% of the time, Pallas kernels for 13%

profile of v1, /device:TPU:1, one launch (start us, length us, event | category | flops | bytes accessed | tf_op | source)
XLA Modules:
  0.0 179.5 jit_solution(16290331629249271692)
XLA Ops:
  6.5 1.4 constant_dynamic-update-slice_fusion
  7.9 0.1 copy-done.8
  8.2 0.0 copy-start.16
  8.2 0.0 copy-start.17
  8.2 0.0 copy-start.18
  8.2 0.0 copy-start.11
  8.3 1.4 copy-done.5
  9.7 0.0 all-gather.3.cloned.1.call-update
  9.7 0.9 broadcast_in_dim.76
  10.6 5.0 %all-to-all-start = ((bf16[4,512,128]{2,1,0:T(8,128)(2,1)}), bf16[4,512,128]{2,1,0:T(8,128)(2,1)S(1)}, u32[]{:S(2)}, u32[]{:S(2)}) async-start(bf16[4,512,128]{2,1,0:T(8,128)(2,1)} %broadcast_in_dim.76), calls=%async_computation | async-start | bytes 1048576 | tf_op jit(solution)/shard_map/all_to_all | solution.py:227
  15.6 0.0 copy-done.16
  15.6 0.1 reshape.301
  15.7 0.1 reshape.299
  15.8 0.1 reshape.300
  15.9 0.3 copy.29
  16.2 0.6 reshape.302
  16.8 0.1 slice_reduce_fusion
  16.9 0.2 fusion.4
  17.1 0.2 fusion.1
  17.3 0.1 iota_compare_fusion.2
  17.4 0.1 fusion.5
  17.5 0.1 select_reduce_fusion
  17.6 1.9 %broadcast_select_fusion.1 = (bf16[4,1,128,384]{2,1,0,3:T(2,128)(2,1)S(1)}, bf16[4,1,128,384]{2,1,0,3:T(2,128)(2,1)S(1)}) fusion(pred[]{:T(512)S(6)} %eq.41, bf16[4,2,128,384]{2,1,0,3:T(2,128)(2,1)S(1)} %reshape.302), kind=kLoop, calls=%fused_computation.1 | loop fusion | flops 393216 | bytes 1572865 | tf_op jit(solution)/shard_map/jit(_where)/select_n | solution.py:289
  19.5 3.0 %all-to-all-done.own_ref = bf16[4,512,128]{2,1,0:T(8,128)(2,1)S(1)} async-done(((bf16[4,512,128]{2,1,0:T(8,128)(2,1)}), bf16[4,512,128]{2,1,0:T(8,128)(2,1)S(1)}, u32[]{:S(2)}, u32[]{:S(2)}) %all-to-all-start) | async-done | bytes 524320 | tf_op jit(solution)/shard_map/all_to_all | solution.py:227
  22.5 8.4 %collective-permute-start = (bf16[4,512,128]{2,1,0:T(8,128)(2,1)S(1)}, bf16[4,512,128]{2,1,0:T(8,128)(2,1)S(1)}, u32[]{:S(2)}, u32[]{:S(2)}) collective-permute-start(bf16[4,512,128]{2,1,0:T(8,128)(2,1)S(1)} %all-to-all-done.own_ref), channel_id=1, source_target_pairs={{0,1},{1,0},{2,3},{3,2},{4,5},{5,4},{6,7},{7,6},{8,9},{9,8},{10,11... | collective-permute-start | bytes 1572872 | tf_op jit(solution)/shard_map/ppermute | solution.py:255
  30.9 0.1 select_reduce_fusion.1
  31.0 0.1 pad.4.clone
  31.1 0.1 copy.32
  31.2 0.1 copy.33
  31.3 0.6 copy.30
  31.8 0.6 copy.31
  32.4 0.0 copy-start.9
  32.4 0.6 pad_add_fusion.pairs
  33.0 1.0 pad_maximum_fusion.w_ref
  34.0 0.7 add_convert_fusion.info_ref
  34.7 0.0 collective-permute-done.far_ref
  34.7 0.8 copy-done.12
  35.5 3.8 %qkv_place.1 = (bf16[64,32,128]{2,1,0:T(8,128)(2,1)}, bf16[512,384]{1,0:T(8,128)(2,1)}) custom-call(s32[4,32]{1,0:T(4,128)} %pad_add_fusion.pairs, bf16[4,512,128]{2,1,0:T(8,128)(2,1)} %copy-done.6, bf16[4,512,128]{2,1,0:T(8,128)(2,1)} %copy-done.12, bf16[1024,384]{1,0:T(8,128)(2,1)} %pad_maximum_fusion.w_ref, f32[64,128]{1,0:T(8,128)} %add_convert_fusion.info_ref), custom_call_target="tpu_custom_call" | custom-call | flops 402653184 | bytes 3145728 | tf_op jit(solution)/shard_map/qkv_place/pallas_call | solution.py:293
  39.4 15.5 %all-to-all-start.1 = ((bf16[64,32,128]{2,1,0:T(8,128)(2,1)}), bf16[64,32,128]{2,1,0:T(8,128)(2,1)S(1)}, u32[]{:S(2)}, u32[]{:S(2)}) async-start(bf16[64,32,128]{2,1,0:T(8,128)(2,1)} %get-tuple-element.9), calls=%async_computation.1 | async-start | bytes 1048576 | tf_op jit(solution)/shard_map/all_to_all | solution.py:227
  54.8 0.4 fusion.7
  55.2 0.7 copy.43
  55.9 0.7 copy.42
  56.6 0.4 fusion.8
  56.9 0.7 copy_bitcast_fusion
  57.7 28.3 %all-to-all-done.1.got_ref = bf16[64,32,128]{2,1,0:T(8,128)(2,1)S(1)} async-done(((bf16[64,32,128]{2,1,0:T(8,128)(2,1)}), bf16[64,32,128]{2,1,0:T(8,128)(2,1)S(1)}, u32[]{:S(2)}, u32[]{:S(2)}) %all-to-all-start.1) | async-done | bytes 524320 | tf_op jit(solution)/shard_map/all_to_all | solution.py:227
  86.0 0.8 copy-done.13
  86.7 11.6 %owner_attention.1 = bf16[64,32,128]{2,1,0:T(8,128)(2,1)} custom-call(bf16[64,32,128]{2,1,0:T(8,128)(2,1)} %copy-done.13, bf16[2,256,128]{2,1,0:T(8,128)(2,1)} %get-tuple-element.32.pk_ref, bf16[2,256,128]{2,1,0:T(8,128)(2,1)} %get-tuple-element.31.pv_ref, bf16[512,128]{1,0:T(8,128)(2,1)} %bitcast.54, bf16[512,128]{1,0:T(8,128)(2,1)} %bitcast.53), custom_call_target="tpu_custom_call" | custom-call | flops 1073741824 | bytes 2097152 | tf_op jit(solution)/shard_map/owner_attention/pallas_call | solution.py:317
  98.4 7.2 %all-to-all-start.2 = ((bf16[64,32,128]{2,1,0:T(8,128)(2,1)}), bf16[64,32,128]{2,1,0:T(8,128)(2,1)S(1)}, u32[]{:S(2)}, u32[]{:S(2)}) async-start(bf16[64,32,128]{2,1,0:T(8,128)(2,1)} %owner_attention.1), calls=%async_computation.2 | async-start | bytes 1048576 | tf_op jit(solution)/shard_map/all_to_all | solution.py:227
  105.6 0.1 lt.41
  105.7 0.9 broadcast_in_dim.89.len_ref
  106.6 4.3 %own_attention.1 = (f32[512,128]{1,0:T(8,128)}, f32[512,128]{1,0:T(8,128)}) custom-call(bf16[512,384]{1,0:T(8,128)(2,1)} %get-tuple-element.10.qkv_ref, s32[512,1]{1,0:T(8,128)} %broadcast_in_dim.89.len_ref), custom_call_target="tpu_custom_call" | custom-call | flops 67108864 | bytes 1048576 | tf_op jit(solution)/shard_map/own_attention/pallas_call | solution.py:308
  110.9 0.9 select_bitcast_fusion.1
  111.8 23.1 %all-to-all-done.2.ret_ref = bf16[64,32,128]{2,1,0:T(8,128)(2,1)S(1)} async-done(((bf16[64,32,128]{2,1,0:T(8,128)(2,1)}), bf16[64,32,128]{2,1,0:T(8,128)(2,1)S(1)}, u32[]{:S(2)}, u32[]{:S(2)}) %all-to-all-start.2) | async-done | bytes 524320 | tf_op jit(solution)/shard_map/all_to_all | solution.py:227
  134.9 0.8 copy-done.7
  135.7 2.7 %merge.1 = bf16[512,128]{1,0:T(8,128)(2,1)} custom-call(s32[4,32]{1,0:T(4,128)} %pad_add_fusion.pairs, bf16[64,32,128]{2,1,0:T(8,128)(2,1)} %copy-done.7, f32[512,128]{1,0:T(8,128)} %get-tuple-element.11.own_ref, f32[512,128]{1,0:T(8,128)} %get-tuple-element.12.lse_ref), custom_call_target="tpu_custom_call" | custom-call | flops 33554432 | bytes 1048576 | tf_op jit(solution)/shard_map/merge/pallas_call | solution.py:334
  138.4 7.8 %all-to-all-start.3 = ((bf16[8,64,128]{2,1,0:T(8,128)(2,1)}), bf16[8,64,128]{2,1,0:T(8,128)(2,1)S(1)}, u32[]{:S(2)}, u32[]{:S(2)}) async-start(bf16[8,64,128]{2,1,0:T(8,128)(2,1)} %bitcast.51), calls=%async_computation.3 | async-start | bytes 262144 | tf_op jit(solution)/shard_map/all_to_all | solution.py:227
  146.2 0.1 copy.39
  146.4 0.1 reshape.304.tok_ref
  146.4 5.1 %all-to-all-done.3.att_ref = bf16[8,64,128]{2,1,0:T(8,128)(2,1)S(1)} async-done(((bf16[8,64,128]{2,1,0:T(8,128)(2,1)}), bf16[8,64,128]{2,1,0:T(8,128)(2,1)S(1)}, u32[]{:S(2)}, u32[]{:S(2)}) %all-to-all-start.3) | async-done | bytes 131104 | tf_op jit(solution)/shard_map/all_to_all | solution.py:227
  151.5 0.0 copy-done.2
  151.5 6.4 %copy-done = bf16[18432,512]{1,0:T(8,128)(2,1)S(1)} copy-done((bf16[18432,512]{1,0:T(8,128)(2,1)S(1)}, bf16[18432,512]{1,0:T(8,128)(2,1)}, u32[]{:S(2)}) %copy-start) | copy-done | bytes 18874392
  157.9 5.6 %project_norm_ffn.1 = bf16[8,64,128]{2,1,0:T(8,128)(2,1)S(1)} custom-call(bf16[8,64,128]{2,1,0:T(8,128)(2,1)S(1)} %all-to-all-done.3.att_ref, bf16[64,1024]{1,0:T(8,128)(2,1)S(1)} %reshape.304.tok_ref, bf16[8,2304,512]{2,1,0:T(8,128)(2,1)S(1)} %bitcast.42, f32[1,1024]{1,0:T(1,128)S(1)} %bitcast.45, f32[1,1024]{1,0:T(1,128)S(1)} %bitcast.46, ...), custom_call_target="tpu_custom_call" | custom-call | flops 1207959552 | bytes 19922944 | tf_op jit(solution)/shard_map/project_norm_ffn/pallas_call | solution.py:353
  163.5 8.5 %all_to_all.25 = bf16[8,64,128]{2,1,0:T(8,128)(2,1)S(1)} all-to-all(bf16[8,64,128]{2,1,0:T(8,128)(2,1)S(1)} %project_norm_ffn.1), channel_id=1, replica_groups=mesh['z'=16,'x'=4,'y'=4,'c'=2] {'y','c'}, dimensions={0} | all-to-all | bytes 262144 | tf_op jit(solution)/shard_map/all_to_all | solution.py:227
  172.0 0.7 copy.51
  (35 shorter events, 0.2 us)
Async XLA Ops:
  6.5 1.5 copy-start.8
  6.5 145.0 %all-gather.3.cloned.1.call-start = ((), (), s32[]{:S(2)}) async-start(), calls=%async_computation.5 | async-start | bytes 21233664 | tf_op jit(solution)/shard_map/all_gather | solution.py:267
  6.5 1.6 copy-start.14
  8.1 1.6 copy-start.15
  8.2 7.4 %copy-start.16 = (s32[64]{0:T(128)S(1)}, s32[64]{0:T(128)}, u32[]{:S(2)}) copy-start(s32[64]{0:T(128)} %param.25) | copy-start | bytes 772
  8.2 7.5 %copy-start.17 = (s32[64]{0:T(128)S(1)}, s32[64]{0:T(128)}, u32[]{:S(2)}) copy-start(s32[64]{0:T(128)} %param.26) | copy-start | bytes 772
  8.2 7.6 %copy-start.18 = (s32[64]{0:T(128)S(1)}, s32[64]{0:T(128)}, u32[]{:S(2)}) copy-start(s32[64]{0:T(128)} %param.27) | copy-start | bytes 772
  8.2 7.7 %copy-start.11 = (bf16[1024,3,128]{2,0,1:T(8,128)(2,1)S(1)}, bf16[1024,3,128]{2,0,1:T(8,128)(2,1)}, u32[]{:S(2)}) copy-start(bf16[1024,3,128]{2,0,1:T(8,128)(2,1)} %param.15) | copy-start | bytes 2359300
  8.3 1.4 copy-start.5
  10.6 11.9 %all-to-all-start = ((bf16[4,512,128]{2,1,0:T(8,128)(2,1)}), bf16[4,512,128]{2,1,0:T(8,128)(2,1)S(1)}, u32[]{:S(2)}, u32[]{:S(2)}) async-start(bf16[4,512,128]{2,1,0:T(8,128)(2,1)} %broadcast_in_dim.76), calls=%async_computation | async-start | bytes 1048576 | tf_op jit(solution)/shard_map/all_to_all | solution.py:227
  22.5 12.1 %copy-start.6 = (bf16[4,512,128]{2,1,0:T(8,128)(2,1)}, bf16[4,512,128]{2,1,0:T(8,128)(2,1)S(1)}, u32[]{:S(2)}) copy-start(bf16[4,512,128]{2,1,0:T(8,128)(2,1)S(1)} %all-to-all-done.own_ref) | copy-start | bytes 1572868
  22.5 12.1 %collective-permute-start = (bf16[4,512,128]{2,1,0:T(8,128)(2,1)S(1)}, bf16[4,512,128]{2,1,0:T(8,128)(2,1)S(1)}, u32[]{:S(2)}, u32[]{:S(2)}) collective-permute-start(bf16[4,512,128]{2,1,0:T(8,128)(2,1)S(1)} %all-to-all-done.own_ref), channel_id=1, source_target_pairs={{0,1},{1,0},{2,3},{3,2},{4,5},{5,4},{6,7},{7,6},{8,9},{9,8},{10,11... | collective-permute-start | bytes 1572872 | tf_op jit(solution)/shard_map/ppermute | solution.py:255
  32.4 22.4 %copy-start.9 = (bf16[32,16,2,128]{3,2,1,0:T(2,128)(2,1)S(1)}, bf16[32,16,2,128]{3,2,1,0:T(2,128)(2,1)}, u32[]{:S(2)}) copy-start(bf16[32,16,2,128]{3,2,1,0:T(2,128)(2,1)} %param.24) | copy-start | bytes 786436
  34.7 21.9 %copy-start.10 = (bf16[2,256,2,128]{3,2,1,0:T(2,128)(2,1)S(1)}, bf16[2,256,2,128]{3,2,1,0:T(2,128)(2,1)}, u32[]{:S(2)}) copy-start(bf16[2,256,2,128]{3,2,1,0:T(2,128)(2,1)} %param.23) | copy-start | bytes 786436
  34.7 0.8 copy-start.12
  39.4 46.6 %all-to-all-start.1 = ((bf16[64,32,128]{2,1,0:T(8,128)(2,1)}), bf16[64,32,128]{2,1,0:T(8,128)(2,1)S(1)}, u32[]{:S(2)}, u32[]{:S(2)}) async-start(bf16[64,32,128]{2,1,0:T(8,128)(2,1)} %get-tuple-element.9), calls=%async_computation.1 | async-start | bytes 1048576 | tf_op jit(solution)/shard_map/all_to_all | solution.py:227
  86.0 0.8 copy-start.13
  98.4 53.1 %copy-start.1 = (f32[1024]{0:T(1024)S(1)}, f32[1024]{0:T(1024)}, u32[]{:S(2)}) copy-start(f32[1024]{0:T(1024)} %param.17) | copy-start | bytes 12292
  98.4 53.1 %copy-start.2 = (f32[1024]{0:T(1024)S(1)}, f32[1024]{0:T(1024)}, u32[]{:S(2)}) copy-start(f32[1024]{0:T(1024)} %param.18) | copy-start | bytes 12292
  98.4 53.1 %copy-start.3 = (f32[1024]{0:T(1024)S(1)}, f32[1024]{0:T(1024)}, u32[]{:S(2)}) copy-start(f32[1024]{0:T(1024)} %param.21) | copy-start | bytes 12292
  98.4 53.1 %copy-start.4 = (f32[1024]{0:T(1024)S(1)}, f32[1024]{0:T(1024)}, u32[]{:S(2)}) copy-start(f32[1024]{0:T(1024)} %param.22) | copy-start | bytes 12292
  98.4 36.5 %all-to-all-start.2 = ((bf16[64,32,128]{2,1,0:T(8,128)(2,1)}), bf16[64,32,128]{2,1,0:T(8,128)(2,1)S(1)}, u32[]{:S(2)}, u32[]{:S(2)}) async-start(bf16[64,32,128]{2,1,0:T(8,128)(2,1)} %owner_attention.1), calls=%async_computation.2 | async-start | bytes 1048576 | tf_op jit(solution)/shard_map/all_to_all | solution.py:227
  134.9 0.8 copy-start.7
  138.4 13.1 %all-to-all-start.3 = ((bf16[8,64,128]{2,1,0:T(8,128)(2,1)}), bf16[8,64,128]{2,1,0:T(8,128)(2,1)S(1)}, u32[]{:S(2)}, u32[]{:S(2)}) async-start(bf16[8,64,128]{2,1,0:T(8,128)(2,1)} %bitcast.51), calls=%async_computation.3 | async-start | bytes 262144 | tf_op jit(solution)/shard_map/all_to_all | solution.py:227
  151.5 6.4 %copy-start = (bf16[18432,512]{1,0:T(8,128)(2,1)S(1)}, bf16[18432,512]{1,0:T(8,128)(2,1)}, u32[]{:S(2)}) copy-start(bf16[18432,512]{1,0:T(8,128)(2,1)} %all-gather.3.cloned.1.call-done) | copy-start | bytes 56623108
Sparse Core Ops, SparseCore 0:
  9.8 107.1 all-gather.2

commit v2 on v1

v2 whole, which is shorter than its diff:
```python
import jax
import jax.numpy as jnp
from jax import lax
from jax.experimental import pallas as pl
from jax.experimental.pallas import tpu as pltpu
from jax.sharding import Mesh, PartitionSpec as P

HD = 64
REQ = ("z", "x")
TP = ("y", "c")
SCALE = 0.125
NEG = -1e30
EPS = 1e-05
bf16 = jnp.bfloat16
f32 = jnp.float32

VM = pl.BlockSpec(memory_space=pltpu.VMEM)
SM = pl.BlockSpec(memory_space=pltpu.SMEM)
SMALL = pltpu.CompilerParams(vmem_limit_bytes=16 << 20)


def iota(shape, axis):
    return lax.broadcasted_iota(jnp.int32, shape, axis)


def head_mask(x, h):
    lane = iota(x.shape, len(x.shape) - 1)
    return jnp.where((lane >= HD) == (h == 1), x, jnp.zeros_like(x))


def dot_t(a, b):
    return lax.dot_general(a, b, (((1,), (1,)), ((), ())), preferred_element_type=f32)


def dot(a, b):
    return jnp.dot(a, b, preferred_element_type=f32)


def softmax_parts(scores, allowed):
    masked = scores if allowed is None else jnp.where(allowed, scores, NEG)
    top = jnp.max(masked, axis=-1, keepdims=True)
    weights = jnp.exp(masked - top)
    total = jnp.sum(weights, axis=-1, keepdims=True)
    return weights.astype(bf16), 1.0 / total, top + jnp.log(total)


def half_weight(w_ref, core, buf):
    for y in range(4):
        rows = pl.ds(pl.multiple_of((2 * y + core) * 128, 128), 128)
        for n in range(3):
            buf[128 * y : 128 * y + 128, 128 * n : 128 * n + 128] = w_ref[n, rows, :]


def half_rows(half_ref, rows):
    return jnp.concatenate([half_ref[i, rows, :] for i in range(4)], axis=1)


def part_kernel(core, half_ref, w_ref, part_ref, buf):
    half_weight(w_ref, core[0], buf)

    def block(b, carry):
        rows = pl.ds(pl.multiple_of(b * 256, 256), 256)
        part_ref[rows, :] = dot(half_rows(half_ref, rows), buf[...])
        return carry

    lax.fori_loop(0, 2, block, 0)


def pair_of(lens, pre, erl, g):
    first, later = erl[2 * g], erl[2 * g + 1]
    slot = jnp.maximum(first, later)
    return pre[2 * g] // 2, slot // 32, slot % 32, later >= 0, lens[2 * g]


def place_kernel(core, lens, pre, erl, part_ref, half_ref, w_ref, send_ref, qkv_ref, buf):
    row = iota((16, 128), 0)
    lane = iota((16, 128), 1)
    half_weight(w_ref, 1 - core[0], buf)
    send_ref[...] = jnp.zeros(send_ref.shape, bf16)

    def block(b, carry):
        rows = pl.ds(pl.multiple_of(b * 128, 128), 128)
        out = part_ref[rows, :] + dot(half_rows(half_ref, rows), buf[...])
        qkv_ref[rows, :] = out.astype(bf16)
        q = out[:, :128].astype(bf16)
        for p in range(8):
            g = b * 8 + p
            slot, slot_e, row_e, late, span = pair_of(lens, pre, erl, g)
            qp = q[16 * p : 16 * p + 16]
            send_ref[slot, 0:16, :] = qp
            pick = jnp.where(lane < span, pre[2 * g] % 2, pre[2 * g + 1] % 2)
            pick = jnp.where((row == 15) & (lane < 16), pick, 0).astype(f32)
            held = send_ref[slot, 16:32, :].astype(f32)
            send_ref[slot, 16:32, :] = (held + pick).astype(bf16)
            qf = qp.astype(f32)
            moved = jnp.where(late, pltpu.roll(qf, 15, 0), qf)
            held = send_ref[slot_e, 16:32, :].astype(f32)
            held = jnp.where(lane == 16, (row_e + 1).astype(f32), held)
            send_ref[slot_e, 16:32, :] = jnp.where(row == 15, held, moved).astype(bf16)
        return carry

    lax.fori_loop(0, 4, block, 0)


def own_kernel(lens, qkv_ref, out_ref, lse_ref):
    r = iota((128, 128), 0)
    c = iota((128, 128), 1)

    def block(b, carry):
        rows = pl.ds(pl.multiple_of(b * 128, 128), 128)
        q = qkv_ref[rows, 0:128]
        k = qkv_ref[rows, 128:256]
        v = qkv_ref[rows, 256:384]
        span = jnp.concatenate(
            [jnp.full((16, 128), lens[2 * (b * 8 + p)], jnp.int32) for p in range(8)], axis=0
        )
        same = ((r // 16) == (c // 16)) & (c <= r) & (((r % 16) < span) == ((c % 16) < span))
        res = []
        for h in range(2):
            w, inv, lse = softmax_parts(dot_t(head_mask(q, h), k) * SCALE, same)
            res.append((dot(w, v) * inv, jnp.broadcast_to(lse, (128, 128))))
        out_ref[rows, :] = head_mask(res[0][0], 0) + head_mask(res[1][0], 1)
        lse_ref[rows, :] = head_mask(res[0][1], 0) + head_mask(res[1][1], 1)
        return carry

    lax.fori_loop(0, 4, block, 0)


def stack_heads(q):
    q = q * jnp.asarray(SCALE, q.dtype)
    return jnp.concatenate([head_mask(q, 0), head_mask(q, 1)], axis=0)


def join_heads(x):
    n = x.shape[0] // 2
    return head_mask(x[:n], 0) + head_mask(x[n:], 1)


def owner_kernel(got_ref, pk_ref, pv_ref, ek_ref, ev_ref, ret_ref, row_v, row_s, sem):
    sub = iota((8, 16, 128), 1)
    lane = iota((8, 16, 128), 2)
    group = lane // 16
    r = iota((256, 128), 0)
    c = iota((256, 128), 1)
    near = ((r % 128) // 16) == (c // 16)

    def rows_of(b, carry):
        slots = pl.ds(pl.multiple_of(b * 8, 8), 8)
        line = got_ref[slots, 16:32, :].astype(f32)[:, 15:16, :]
        row_v[slots, :] = jnp.maximum(line.reshape(8, 128) - 1.0, 0.0).astype(jnp.int32)
        return carry

    lax.fori_loop(0, 8, rows_of, 0)
    copy = pltpu.make_async_copy(row_v, row_s, sem)
    copy.start()
    copy.wait()

    def prefix_part(b):
        slots = pl.ds(b * 8, 8)
        q = stack_heads(got_ref[slots, 0:16, :].reshape(128, 128))
        line = got_ref[slots, 16:32, :].astype(f32)[:, 15:16, :]
        info = jnp.broadcast_to(line, (8, 16, 128))
        pick = jnp.sum(jnp.where(lane == sub, info, 0.0), axis=-1, keepdims=True)
        pick = pick.reshape(128, 1) > 0.5
        pick = jnp.broadcast_to(pick, (128, 256))
        pick = jnp.concatenate([pick, pick], axis=0)
        s = jnp.where(pick, dot_t(q, pk_ref[1]), dot_t(q, pk_ref[0]))
        w, inv, lse = softmax_parts(s, None)
        none = jnp.zeros_like(w)
        o = dot(jnp.where(pick, none, w), pv_ref[0]) + dot(jnp.where(pick, w, none), pv_ref[1])
        return join_heads(o * inv), lse

    def earlier_part(b):
        slots = pl.ds(b * 8, 8)
        q = stack_heads(got_ref[slots, 16:32, :].reshape(128, 128))
        at = [pl.ds(pl.multiple_of(row_s[b * 8 + i, 16] * 16, 16), 16) for i in range(8)]
        keys = jnp.concatenate([ek_ref[x, :] for x in at], axis=0)
        values = jnp.concatenate([ev_ref[x, :] for x in at], axis=0)
        w, inv, lse = softmax_parts(dot_t(q, keys), near)
        return join_heads(dot(w, values) * inv), lse

    def block(b, carry):
        slots = pl.ds(b * 8, 8)
        pre, pre_lse = prefix_part(b)
        erl, erl_lse = earlier_part(b)
        ret_ref[slots, 0:16, :] = pre.astype(bf16).reshape(8, 16, 128)
        stats = (pre_lse[:128], pre_lse[128:], erl_lse[:128], erl_lse[128:])
        spread = jnp.zeros((8, 16, 128), f32)
        for n in range(4):
            want = ((group // 4) * 2 + group % 2) == n
            spread = jnp.where(want, stats[n].reshape(8, 16, 1), spread)
        line = jnp.sum(jnp.where(lane % 16 == sub, spread, 0.0), axis=1, keepdims=True)
        high = line.astype(bf16).astype(f32)
        line = jnp.where((group[:, 0:1] // 2) % 2 == 1, line - high, high)
        ret_ref[slots, 16:32, :] = jnp.where(
            sub == 15, jnp.broadcast_to(line, (8, 16, 128)), erl.reshape(8, 16, 128)
        ).astype(bf16)
        return carry

    lax.fori_loop(0, 8, block, 0, unroll=2)


def merge_kernel(
    lens, pre, erl, ret_ref, own_ref, lse_ref, out_ref, pre_o, pre_s, erl_o, erl_s, erl_on
):
    row = iota((16, 128), 0)
    lane = iota((16, 128), 1)
    diag = (lane % 16) == row

    def block(b, carry):
        for p in range(8):
            g = b * 8 + p
            rows = pl.ds(pl.multiple_of(b * 128, 128) + 16 * p, 16)
            slot, slot_e, _, late, span = pair_of(lens, pre, erl, g)
            pre_o[rows, :] = ret_ref[slot, 0:16, :].astype(f32)
            line = jnp.broadcast_to(ret_ref[slot, 16:32, :].astype(f32)[15:16, :], (16, 128))
            pre_s[rows, :] = jnp.where(diag & (lane < 64), line, 0.0)
            part = ret_ref[slot_e, 16:32, :].astype(f32)
            line = jnp.broadcast_to(part[15:16, :], (16, 128))
            stat = jnp.where(diag & (lane >= 64), line, 0.0)
            erl_o[rows, :] = jnp.where(late, pltpu.roll(part, 1, 0), part)
            erl_s[rows, :] = jnp.where(late, pltpu.roll(stat, 1, 0), stat)
            turn = jnp.where(late, 1, 0)
            erl_on[rows, :] = jnp.where((row < span).astype(jnp.int32) + turn == 1, 1.0, 0.0)
        rows = pl.ds(pl.multiple_of(b * 128, 128), 128)
        a = iota((128, 128), 0)
        c = iota((128, 128), 1)
        pick = (((a // 16) % 2) == (c // 64)).astype(bf16)
        l_pre = dot(pre_s[rows, :].astype(bf16), pick)
        l_erl = dot(erl_s[rows, :].astype(bf16), pick)
        on = erl_on[rows, :] > 0.5
        l_erl = jnp.where(on, l_erl, NEG)
        l_own = lse_ref[rows, :]
        top = jnp.maximum(jnp.maximum(l_own, l_pre), l_erl)
        w_own = jnp.exp(l_own - top)
        w_pre = jnp.exp(l_pre - top)
        w_erl = jnp.exp(l_erl - top)
        mixed = w_own * own_ref[rows, :] + w_pre * pre_o[rows, :]
        mixed = mixed + w_erl * jnp.where(on, erl_o[rows, :], 0.0)
        out_ref[rows, :] = (mixed / (w_own + w_pre + w_erl)).astype(bf16)
        return carry

    lax.fori_loop(0, 4, block, 0)


def norm_rows(hidden, gain, shift):
    mean = jnp.mean(hidden, axis=-1, keepdims=True)
    centred = hidden - mean
    var = jnp.mean(centred * centred, axis=-1, keepdims=True)
    return centred * lax.rsqrt(var + EPS) * gain + shift


def tail_kernel(
    att_ref, tok_ref, ag_ref, as_ref, mg_ref, ms_ref, up_hbm, rest_hbm, out_ref, w_out, up, down, sem
):
    def fetch(t):
        return (
            pltpu.make_async_copy(up_hbm.at[t], up.at[t], sem.at[2 * t + 1]),
            pltpu.make_async_copy(rest_hbm.at[t, 0:512, :], down.at[t], sem.at[2 * t + 2]),
        )

    first = pltpu.make_async_copy(rest_hbm.at[:, 512:640, :], w_out, sem.at[0])
    first.start()
    for t in range(8):
        for copy in fetch(t):
            copy.start()
    att = jnp.concatenate([att_ref[i] for i in range(8)], axis=1)
    first.wait()
    hidden = tok_ref[...].astype(f32) + dot(att, w_out[...].reshape(1024, 1024))
    normed = norm_rows(hidden, ag_ref[...], as_ref[...]).astype(bf16)

    def block(t, acc):
        up_copy, down_copy = fetch(t)
        up_copy.wait()
        h = dot(normed, up[t])
        inner = (0.5 * h * (1.0 + lax.erf(h * 0.7071067811865476))).astype(bf16)
        down_copy.wait()
        return acc + dot(inner, down[t])

    acc = lax.fori_loop(0, 8, block, jnp.zeros((64, 1024), f32))
    hidden = normed.astype(f32) + acc
    done = norm_rows(hidden, mg_ref[...], ms_ref[...]).astype(bf16)
    for i in range(8):
        out_ref[i] = done[:, 128 * i : 128 * i + 128]


def swap_all(value, axis):
    return lax.all_to_all(value, axis, split_axis=0, concat_axis=0, tiled=True)


def cost(flops, size, trans=0):
    return pl.CostEstimate(flops=flops, bytes_accessed=size, transcendentals=trans)


def local(
    tokens,
    qkv_weight,
    out_weight,
    attn_gain,
    attn_shift,
    up_weight,
    down_weight,
    mlp_gain,
    mlp_shift,
    prefix_cache,
    earlier_cache,
    suffix_len,
    prefix_id,
    earlier_slot,
):
    n_req = lax.axis_size(REQ)
    core = lax.axis_index("c")
    rank = lax.axis_index(TP)

    ups = lax.all_gather(up_weight, TP, axis=0, tiled=False)

    own_half = swap_all(jnp.broadcast_to(tokens[None], (4, 512, 128)), "y")
    far_half = lax.ppermute(own_half, "c", [(0, 1), (1, 0)])

    far_half, down_weight, out_weight = lax.optimization_barrier(
        (far_half, down_weight, out_weight)
    )
    rest = jnp.concatenate([down_weight, out_weight], axis=0)
    rest = lax.all_gather(rest, TP, axis=0, tiled=False)

    core1 = core.reshape(1)
    w_qkv = qkv_weight.transpose(1, 0, 2)
    part = pl.pallas_call(
        part_kernel,
        in_specs=[SM, VM, VM],
        out_specs=VM,
        out_shape=jax.ShapeDtypeStruct((512, 384), f32),
        scratch_shapes=[pltpu.VMEM((512, 384), bf16)],
        compiler_params=SMALL,
        cost_estimate=cost(2 * 512 * 512 * 384, 2 << 20),
        name="qkv_own_half",
    )(core1, own_half, w_qkv)
    send, qkv = pl.pallas_call(
        place_kernel,
        in_specs=[SM] * 4 + [VM] * 3,
        out_specs=[VM, VM],
        out_shape=[
            jax.ShapeDtypeStruct((n_req, 32, 128), bf16),
            jax.ShapeDtypeStruct((512, 384), bf16),
        ],
        scratch_shapes=[pltpu.VMEM((512, 384), bf16)],
        compiler_params=SMALL,
        cost_estimate=cost(2 * 512 * 512 * 384, 3 << 20),
        name="qkv_place",
    )(core1, suffix_len, prefix_id, earlier_slot, part, far_half, w_qkv)

    got = swap_all(send, REQ)

    own_out, own_lse = pl.pallas_call(
        own_kernel,
        in_specs=[SM, VM],
        out_specs=[VM, VM],
        out_shape=[jax.ShapeDtypeStruct((512, 128), f32)] * 2,
        compiler_params=SMALL,
        cost_estimate=cost(2 * 512 * 128 * 128 * 4, 1 << 20, 2 * 512 * 128),
        name="own_attention",
    )(suffix_len, qkv)

    ret = pl.pallas_call(
        owner_kernel,
        in_specs=[VM] * 5,
        out_specs=VM,
        out_shape=jax.ShapeDtypeStruct((n_req, 32, 128), bf16),
        scratch_shapes=[
            pltpu.VMEM((n_req, 128), jnp.int32),
            pltpu.SMEM((n_req, 128), jnp.int32),
            pltpu.SemaphoreType.DMA,
        ],
        compiler_params=SMALL,
        cost_estimate=cost(2 * 1024 * 128 * 2048, 2 << 20, 2 * 1024 * 384),
        name="owner_attention",
    )(
        got,
        prefix_cache[:, :, 0],
        prefix_cache[:, :, 1],
        earlier_cache[:, :, 0].reshape(512, 128),
        earlier_cache[:, :, 1].reshape(512, 128),
    )

    back = swap_all(ret, REQ)

    attended = pl.pallas_call(
        merge_kernel,
        in_specs=[SM, SM, SM, VM, VM, VM],
        out_specs=VM,
        out_shape=jax.ShapeDtypeStruct((512, 128), bf16),
        scratch_shapes=[pltpu.VMEM((512, 128), f32)] * 5,
        cost_estimate=cost(2 * 512 * 128 * 256, 1 << 20, 3 * 512 * 128),
        compiler_params=SMALL,
        name="merge",
    )(suffix_len, prefix_id, earlier_slot, back, own_out, own_lse)

    att = swap_all(attended.reshape(8, 64, 128), TP)

    own_rows = lax.dynamic_slice_in_dim(own_half, rank * 64, 64, 1)
    far_rows = lax.dynamic_slice_in_dim(far_half, rank * 64, 64, 1)
    even = jnp.where(core == 0, own_rows, far_rows)
    odd = jnp.where(core == 0, far_rows, own_rows)
    tok_rows = jnp.stack([even, odd], axis=1).transpose(2, 0, 1, 3).reshape(64, 1024)

    hbm = pl.BlockSpec(memory_space=pl.ANY)
    encoded = pl.pallas_call(
        tail_kernel,
        in_specs=[VM] * 6 + [hbm] * 2,
        out_specs=VM,
        out_shape=jax.ShapeDtypeStruct((8, 64, 128), bf16),
        scratch_shapes=[
            pltpu.VMEM((8, 128, 1024), bf16),
            pltpu.VMEM((8, 1024, 512), bf16),
            pltpu.VMEM((8, 512, 1024), bf16),
            pltpu.SemaphoreType.DMA((17,)),
        ],
        compiler_params=pltpu.CompilerParams(vmem_limit_bytes=52 << 20),
        cost_estimate=cost(2 * 64 * 9 * 1024 * 1024, 19 << 20, 64 * 4096),
        name="project_norm_ffn",
    )(
        att,
        tok_rows,
        attn_gain.reshape(1, 1024),
        attn_shift.reshape(1, 1024),
        mlp_gain.reshape(1, 1024),
        mlp_shift.reshape(1, 1024),
        ups,
        rest,
    )
    return swap_all(encoded, TP).reshape(512, 128)


def solution(mesh):
    split = Mesh(mesh.devices.reshape(16, 4, 4, 2), ("z", "x", "y", "c"))
    placed = (
        P(REQ, TP),
        P(None, None, TP),
        P(TP, None),
        P(),
        P(),
        P(None, TP),
        P(TP, None),
        P(),
        P(),
        P(REQ, None, None, TP),
        P(REQ, None, None, TP),
        P(REQ),
        P(REQ),
        P(REQ),
    )
    return jax.shard_map(
        local, mesh=split, in_specs=placed, out_specs=P(REQ, TP), check_vma=False
    )
```

time: 180 us -> 167 us (0.928)
  local copies, waits for them, and re-layouts: 20 us -> 2.7 us
  blocking collectives: 8.52 us -> 21.1 us
  waiting for transfers between devices: 59.5 us -> 65.6 us
  starting transfers between devices: 43.8 us -> 38.8 us
  Pallas kernels: 28.1 us -> 23.4 us
  other arithmetic: 5.82 us -> 1.25 us
    unnamed x46 -> x27, local copies, waits for them, and re-layouts: 14.1 us -> 0.75 us
    all_to_all x1 -> x2, blocking collectives: 8.52 us -> 21.1 us  [swap_all(): return lax.all_to_all(value, axis, split_axis=0, concat_axis=0, tiled=True)]
    pallas_call x1, Pallas kernels: 11.6 us -> 7.08 us  [local(): pl.pallas_call(owner_kernel, in_specs=[VM] * 5, out_specs=VM, out_shape=j...]
    all_to_all x4 -> x3, starting transfers between devices: 35.5 us -> 31.1 us  [swap_all(): return lax.all_to_all(value, axis, split_axis=0, concat_axis=0, tiled=True)]
    all_to_all x4 -> x3, waiting for transfers between devices: 59.5 us -> 61.8 us  [swap_all(): return lax.all_to_all(value, axis, split_axis=0, concat_axis=0, tiled=True)]
    select_n x5 -> x0, other arithmetic: 2.17 us -> none  [the longest x1 1.88 us: local(): w_own = jnp.where(core == 0, w_split[:, 0], w_split[:, 1]).reshape(512, 384)]
    pallas_call x4 -> x5, Pallas kernels: 16.5 us -> 16.3 us  [the longest x1 7.77 us: local(): pl.pallas_call(tail_kernel, in_specs=[VM] * 6 + [hbm] * 2, out_specs=VM,...]
  transfers between devices with their start and end apart: 6 -> 6, of which waited for: 4 -> 5; matrix products, arithmetic and copies ran while one was open for 7% -> 2% of each run, Pallas kernels for 13% -> 9%
where the time goes in v2:
time: 167 us; the launch traced here: 166 us
  waiting for transfers between devices  65.6 us (39%)
  starting transfers between devices  38.8 us (23%)
  Pallas kernels  23.4 us (14%)
  blocking collectives  21.1 us (13%)
  between operations  13.6 us (8%)
  local copies, waits for them, and re-layouts  2.7 us (2%)
    all_to_all x3, waiting for transfers between devices, swap_all(): return lax.all_to_all(value, axis, split_axis=0, concat_axis=0, tiled=True)  61.8 us
    all_to_all x3, starting transfers between devices, swap_all(): return lax.all_to_all(value, axis, split_axis=0, concat_axis=0, tiled=True)  31.1 us
    all_to_all x2, blocking collectives, swap_all(): return lax.all_to_all(value, axis, split_axis=0, concat_axis=0, tiled=True)  21.1 us
    pallas_call x1, Pallas kernels, local(): pl.pallas_call(tail_kernel, in_specs=[VM] * 6 + [hbm] * 2, out_specs=VM,...  7.77 us
    ppermute x1, starting transfers between devices, local(): far_half = lax.ppermute(own_half, 'c', [(0, 1), (1, 0)])  7.64 us
    pallas_call x1, Pallas kernels, local(): pl.pallas_call(owner_kernel, in_specs=[VM] * 5, out_specs=VM, out_shape=j...  7.08 us
  transfers between devices with their start and end apart: 6, of which 5 were waited for; matrix products, arithmetic and copies ran while one was open for 2% of the time, Pallas kernels for 9%

profile of v2, /device:TPU:1, one launch (start us, length us, event | category | flops | bytes accessed | tf_op | source)
XLA Modules:
  0.0 166.4 jit_solution(12613473397513902455)
XLA Ops:
  6.5 0.0 copy-start.11
  6.5 0.0 copy-start.8
  6.5 0.0 all-gather.5.cloned.1.call-start
  6.5 0.7 all-gather.5.cloned.1.call-update
  7.3 0.0 all-gather.7.cloned.1.call-start
  7.3 1.0 broadcast_in_dim.2
  8.3 0.0 copy-start
  8.3 11.9 %all_to_all.25.half_ref = bf16[4,512,128]{2,1,0:T(8,128)(2,1)S(1)} all-to-all(bf16[4,512,128]{2,1,0:T(8,128)(2,1)S(1)} %broadcast_in_dim.2), channel_id=1, replica_groups=mesh['z'=16,'x'=4,'y'=4,'c'=2] {'y'}, dimensions={0} | all-to-all | bytes 1048576 | tf_op jit(solution)/shard_map/all_to_all | solution.py:288
  20.2 0.0 copy-start.1
  20.2 0.0 copy-start.6
  20.2 0.0 copy-start.7
  20.2 7.6 %collective-permute-start = (bf16[4,512,128]{2,1,0:T(8,128)(2,1)S(1)}, bf16[4,512,128]{2,1,0:T(8,128)(2,1)S(1)}, u32[]{:S(2)}, u32[]{:S(2)}) collective-permute-start(bf16[4,512,128]{2,1,0:T(8,128)(2,1)S(1)} %all_to_all.25.half_ref), channel_id=1, source_target_pairs={{0,1},{1,0},{2,3},{3,2},{4,5},{5,4},{6,7},{7,6},{8,9},{9,8},{10,11... | collective-permute-start | bytes 1572872 | tf_op jit(solution)/shard_map/ppermute | solution.py:318
  27.8 1.5 collective-permute-done.half_ref
  29.3 0.0 copy-done.11
  29.3 0.0 copy-done.8
  29.3 1.2 pad_maximum_fusion
  30.5 0.0 all-gather.7.cloned.1.call-update
  30.6 0.0 copy-done
  30.6 0.0 copy-start.9
  30.6 0.7 qkv_own_half.1.part_ref
  31.3 0.0 copy-done.1
  31.3 0.0 copy-done.6
  31.3 0.0 copy-done.7
  31.3 0.0 copy-start.10
  31.3 2.7 %qkv_place.1 = (bf16[64,32,128]{2,1,0:T(8,128)(2,1)}, bf16[512,384]{1,0:T(8,128)(2,1)S(1)}) custom-call(s32[1]{0:T(128)} %bitcast.core, s32[64]{0:T(128)S(1)} %copy-done.1, s32[64]{0:T(128)S(1)} %copy-done.6, s32[64]{0:T(128)S(1)} %copy-done.7, f32[512,384]{1,0:T(8,128)S(1)} %qkv_own_half.1.part_ref, bf16[4,512,128]{2,1,0:T(8,128)(2,1)S(1)} %collective-permute-done.half_ref, ...), custom_call_target="tpu_custom_call" | custom-call | flops 201326592 | bytes 3145728 | tf_op jit(solution)/shard_map/qkv_place/pallas_call | solution.py:338
  34.0 16.2 %all-to-all-start.1 = ((bf16[64,32,128]{2,1,0:T(8,128)(2,1)}), bf16[64,32,128]{2,1,0:T(8,128)(2,1)S(1)}, u32[]{:S(2)}, u32[]{:S(2)}) async-start(bf16[64,32,128]{2,1,0:T(8,128)(2,1)} %get-tuple-element.13), calls=%async_computation.1 | async-start | bytes 1048576 | tf_op jit(solution)/shard_map/all_to_all | solution.py:288
  50.2 0.0 copy-done.9
  50.2 0.4 fusion
  50.6 0.0 copy-done.10
  50.6 0.4 fusion.1
  51.1 30.1 %all-to-all-done.1.got_ref = bf16[64,32,128]{2,1,0:T(8,128)(2,1)S(1)} async-done(((bf16[64,32,128]{2,1,0:T(8,128)(2,1)}), bf16[64,32,128]{2,1,0:T(8,128)(2,1)S(1)}, u32[]{:S(2)}, u32[]{:S(2)}) %all-to-all-start.1) | async-done | bytes 524320 | tf_op jit(solution)/shard_map/all_to_all | solution.py:288
  81.1 0.0 copy-start.2
  81.1 0.0 copy-start.3
  81.2 0.0 copy-start.4
  81.2 0.0 copy-start.5
  81.2 7.1 %owner_attention.1 = bf16[64,32,128]{2,1,0:T(8,128)(2,1)} custom-call(bf16[64,32,128]{2,1,0:T(8,128)(2,1)S(1)} %all-to-all-done.1.got_ref, bf16[2,256,128]{2,1,0:T(8,128)(2,1)S(1)} %get-tuple-element.26.pk_ref, bf16[2,256,128]{2,1,0:T(8,128)(2,1)S(1)} %get-tuple-element.25.pv_ref, bf16[512,128]{1,0:T(8,128)(2,1)S(1)} %bitcast.24, bf16[512,128]{1,0:T(8,128)(2,1)S(1)} %bitcast.25), custom_call_target="tpu_custom_call" | custom-call | flops 536870912 | bytes 2097152 | tf_op jit(solution)/shard_map/owner_attention/pallas_call | solution.py:364
  88.2 7.3 %all-to-all-start.2 = ((bf16[64,32,128]{2,1,0:T(8,128)(2,1)}), bf16[64,32,128]{2,1,0:T(8,128)(2,1)S(1)}, u32[]{:S(2)}, u32[]{:S(2)}) async-start(bf16[64,32,128]{2,1,0:T(8,128)(2,1)} %owner_attention.1), calls=%async_computation.2 | async-start | bytes 1048576 | tf_op jit(solution)/shard_map/all_to_all | solution.py:288
  95.5 3.0 %own_attention.1 = (f32[512,128]{1,0:T(8,128)S(1)}, f32[512,128]{1,0:T(8,128)S(1)}) custom-call(s32[64]{0:T(128)S(1)} %copy-done.1, bf16[512,384]{1,0:T(8,128)(2,1)S(1)} %get-tuple-element.14.qkv_ref), custom_call_target="tpu_custom_call" | custom-call | flops 67108864 | bytes 1048576 | tf_op jit(solution)/shard_map/own_attention/pallas_call | solution.py:354
  98.5 26.3 %all-to-all-done.2.ret_ref = bf16[64,32,128]{2,1,0:T(8,128)(2,1)S(1)} async-done(((bf16[64,32,128]{2,1,0:T(8,128)(2,1)}), bf16[64,32,128]{2,1,0:T(8,128)(2,1)S(1)}, u32[]{:S(2)}, u32[]{:S(2)}) %all-to-all-start.2) | async-done | bytes 524320 | tf_op jit(solution)/shard_map/all_to_all | solution.py:288
  124.9 2.2 %merge.1 = bf16[512,128]{1,0:T(8,128)(2,1)} custom-call(s32[64]{0:T(128)S(1)} %copy-done.1, s32[64]{0:T(128)S(1)} %copy-done.6, s32[64]{0:T(128)S(1)} %copy-done.7, bf16[64,32,128]{2,1,0:T(8,128)(2,1)S(1)} %all-to-all-done.2.ret_ref, f32[512,128]{1,0:T(8,128)S(1)} %get-tuple-element.15.own_ref, f32[512,128]{1,0:T(8,128)S(1)} %get-tuple-element.16.lse_ref), custom_call_target="tpu_custom_call" | custom-call | flops 33554432 | bytes 1048576 | tf_op jit(solution)/shard_map/merge/pallas_call | solution.py:387
  127.0 7.7 %all-to-all-start.3 = ((bf16[8,64,128]{2,1,0:T(8,128)(2,1)}), bf16[8,64,128]{2,1,0:T(8,128)(2,1)S(1)}, u32[]{:S(2)}, u32[]{:S(2)}) async-start(bf16[8,64,128]{2,1,0:T(8,128)(2,1)} %bitcast.6), calls=%async_computation.3 | async-start | bytes 262144 | tf_op jit(solution)/shard_map/all_to_all | solution.py:288
  134.8 0.1 copy.22
  134.9 0.1 reshape.27.tok_ref
  135.0 5.4 %all-to-all-done.3.att_ref = bf16[8,64,128]{2,1,0:T(8,128)(2,1)S(1)} async-done(((bf16[8,64,128]{2,1,0:T(8,128)(2,1)}), bf16[8,64,128]{2,1,0:T(8,128)(2,1)S(1)}, u32[]{:S(2)}, u32[]{:S(2)}) %all-to-all-start.3) | async-done | bytes 131104 | tf_op jit(solution)/shard_map/all_to_all | solution.py:288
  140.4 0.0 all-gather.5.cloned.1.call-done
  140.4 1.5 all-gather.7.cloned.1.call-done
  142.0 0.0 copy-done.2
  142.0 0.0 copy-done.3
  142.0 0.0 copy-done.4
  142.0 0.0 copy-done.5
  142.0 7.8 %project_norm_ffn.1 = bf16[8,64,128]{2,1,0:T(8,128)(2,1)S(1)} custom-call(bf16[8,64,128]{2,1,0:T(8,128)(2,1)S(1)} %all-to-all-done.3.att_ref, bf16[64,1024]{1,0:T(8,128)(2,1)S(1)} %reshape.27.tok_ref, f32[1,1024]{1,0:T(1,128)S(1)} %bitcast.26, f32[1,1024]{1,0:T(1,128)S(1)} %bitcast.27, f32[1,1024]{1,0:T(1,128)S(1)} %bitcast.28, f32[1,1024]{1,0:T(1,128)S(1)} %bitcast.29, ...), custom_call_target="tpu_custom_call" | custom-call | flops 1207959552 | bytes 19922944 | tf_op jit(solution)/shard_map/project_norm_ffn/pallas_call | solution.py:407
  149.7 9.2 %all_to_all.26 = bf16[8,64,128]{2,1,0:T(8,128)(2,1)S(1)} all-to-all(bf16[8,64,128]{2,1,0:T(8,128)(2,1)S(1)} %project_norm_ffn.1), channel_id=1, replica_groups=mesh['z'=16,'x'=4,'y'=4,'c'=2] {'y','c'}, dimensions={0} | all-to-all | bytes 262144 | tf_op jit(solution)/shard_map/all_to_all | solution.py:288
  158.9 0.7 copy.30
  (5 shorter events, 0.1 us)
Async XLA Ops:
  6.5 22.8 %copy-start.11 = (bf16[128,1024]{1,0:T(8,128)(2,1)S(1)}, bf16[128,1024]{1,0:T(8,128)(2,1)}, u32[]{:S(2)}) copy-start(bf16[128,1024]{1,0:T(8,128)(2,1)} %param.16) | copy-start | bytes 786436
  6.5 22.8 %copy-start.8 = (bf16[512,1024]{1,0:T(8,128)(2,1)S(1)}, bf16[512,1024]{1,0:T(8,128)(2,1)}, u32[]{:S(2)}) copy-start(bf16[512,1024]{1,0:T(8,128)(2,1)} %param.20) | copy-start | bytes 3145732
  6.5 133.9 %all-gather.5.cloned.1.call-start = ((), (), s32[]{:S(2)}) async-start(), calls=%async_computation.5 | async-start | bytes 9437184 | tf_op jit(solution)/shard_map/all_gather | solution.py:315
  7.3 134.7 %all-gather.7.cloned.1.call-start = ((), (), s32[]{:S(2)}) async-start(), calls=%async_computation.6 | async-start | bytes 11796480 | tf_op jit(solution)/shard_map/all_gather | solution.py:324
  8.3 22.3 %copy-start = (bf16[1024,3,128]{2,0,1:T(8,128)(2,1)S(1)}, bf16[1024,3,128]{2,0,1:T(8,128)(2,1)}, u32[]{:S(2)}) copy-start(bf16[1024,3,128]{2,0,1:T(8,128)(2,1)} %param.15) | copy-start | bytes 2359300
  20.2 11.1 %copy-start.1 = (s32[64]{0:T(128)S(1)}, s32[64]{0:T(128)}, u32[]{:S(2)}) copy-start(s32[64]{0:T(128)} %lens.5) | copy-start | bytes 772
  20.2 11.1 %copy-start.6 = (s32[64]{0:T(128)S(1)}, s32[64]{0:T(128)}, u32[]{:S(2)}) copy-start(s32[64]{0:T(128)} %pre.3) | copy-start | bytes 772
  20.2 11.1 %copy-start.7 = (s32[64]{0:T(128)S(1)}, s32[64]{0:T(128)}, u32[]{:S(2)}) copy-start(s32[64]{0:T(128)} %erl.3) | copy-start | bytes 772
  20.2 9.2 %collective-permute-start = (bf16[4,512,128]{2,1,0:T(8,128)(2,1)S(1)}, bf16[4,512,128]{2,1,0:T(8,128)(2,1)S(1)}, u32[]{:S(2)}, u32[]{:S(2)}) collective-permute-start(bf16[4,512,128]{2,1,0:T(8,128)(2,1)S(1)} %all_to_all.25.half_ref), channel_id=1, source_target_pairs={{0,1},{1,0},{2,3},{3,2},{4,5},{5,4},{6,7},{7,6},{8,9},{9,8},{10,11... | collective-permute-start | bytes 1572872 | tf_op jit(solution)/shard_map/ppermute | solution.py:318
  30.6 19.6 %copy-start.9 = (bf16[32,16,2,128]{3,2,1,0:T(2,128)(2,1)S(1)}, bf16[32,16,2,128]{3,2,1,0:T(2,128)(2,1)}, u32[]{:S(2)}) copy-start(bf16[32,16,2,128]{3,2,1,0:T(2,128)(2,1)} %param.24) | copy-start | bytes 786436
  31.3 19.3 %copy-start.10 = (bf16[2,256,2,128]{3,2,1,0:T(2,128)(2,1)S(1)}, bf16[2,256,2,128]{3,2,1,0:T(2,128)(2,1)}, u32[]{:S(2)}) copy-start(bf16[2,256,2,128]{3,2,1,0:T(2,128)(2,1)} %param.23) | copy-start | bytes 786436
  34.0 47.1 %all-to-all-start.1 = ((bf16[64,32,128]{2,1,0:T(8,128)(2,1)}), bf16[64,32,128]{2,1,0:T(8,128)(2,1)S(1)}, u32[]{:S(2)}, u32[]{:S(2)}) async-start(bf16[64,32,128]{2,1,0:T(8,128)(2,1)} %get-tuple-element.13), calls=%async_computation.1 | async-start | bytes 1048576 | tf_op jit(solution)/shard_map/all_to_all | solution.py:288
  81.1 60.8 %copy-start.2 = (f32[1024]{0:T(1024)S(1)}, f32[1024]{0:T(1024)}, u32[]{:S(2)}) copy-start(f32[1024]{0:T(1024)} %param.17) | copy-start | bytes 12292
  81.1 60.8 %copy-start.3 = (f32[1024]{0:T(1024)S(1)}, f32[1024]{0:T(1024)}, u32[]{:S(2)}) copy-start(f32[1024]{0:T(1024)} %param.18) | copy-start | bytes 12292
  81.2 60.8 %copy-start.4 = (f32[1024]{0:T(1024)S(1)}, f32[1024]{0:T(1024)}, u32[]{:S(2)}) copy-start(f32[1024]{0:T(1024)} %param.21) | copy-start | bytes 12292
  81.2 60.8 %copy-start.5 = (f32[1024]{0:T(1024)S(1)}, f32[1024]{0:T(1024)}, u32[]{:S(2)}) copy-start(f32[1024]{0:T(1024)} %param.22) | copy-start | bytes 12292
  88.2 36.6 %all-to-all-start.2 = ((bf16[64,32,128]{2,1,0:T(8,128)(2,1)}), bf16[64,32,128]{2,1,0:T(8,128)(2,1)S(1)}, u32[]{:S(2)}, u32[]{:S(2)}) async-start(bf16[64,32,128]{2,1,0:T(8,128)(2,1)} %owner_attention.1), calls=%async_computation.2 | async-start | bytes 1048576 | tf_op jit(solution)/shard_map/all_to_all | solution.py:288
  127.0 13.4 %all-to-all-start.3 = ((bf16[8,64,128]{2,1,0:T(8,128)(2,1)}), bf16[8,64,128]{2,1,0:T(8,128)(2,1)S(1)}, u32[]{:S(2)}, u32[]{:S(2)}) async-start(bf16[8,64,128]{2,1,0:T(8,128)(2,1)} %bitcast.6), calls=%async_computation.3 | async-start | bytes 262144 | tf_op jit(solution)/shard_map/all_to_all | solution.py:288
Sparse Core Ops, SparseCore 0:
  9.5 63.1 all-gather.4
  74.9 67.0 all-gather.6

commit v3 on v2

--- a/solution.py
+++ b/solution.py
@@ -250,36 +250,83 @@
     return centred * lax.rsqrt(var + EPS) * gain + shift
 
 
+def pack_kernel(at, up_ref, down_ref, out_ref, pack_ref, sem):
+    x = at[0]
+    up_rows = pl.ds(pl.multiple_of(x * 256, 256), 256)
+    down_rows = pl.ds(pl.multiple_of(x * 128, 128), 128)
+    out_rows = pl.ds(pl.multiple_of(x * 32, 32), 32)
+    left, right = pl.ds(0, 512), pl.ds(512, 512)
+    copies = (
+        (up_ref.at[up_rows, :], 0, 256),
+        (down_ref.at[down_rows, left], 256, 128),
+        (down_ref.at[down_rows, right], 384, 128),
+        (out_ref.at[out_rows, left], 512, 32),
+        (out_ref.at[out_rows, right], 544, 32),
+    )
+    copies = [
+        pltpu.make_async_copy(source, pack_ref.at[pl.ds(first, size), :], sem.at[i])
+        for i, (source, first, size) in enumerate(copies)
+    ]
+    for copy in copies:
+        copy.start()
+    for copy in copies:
+        copy.wait()
+
+
 def tail_kernel(
-    att_ref, tok_ref, ag_ref, as_ref, mg_ref, ms_ref, up_hbm, rest_hbm, out_ref, w_out, up, down, sem
+    att_ref,
+    tok_ref,
+    ag_ref,
+    as_ref,
+    mg_ref,
+    ms_ref,
+    w_hbm,
+    out_ref,
+    acc,
+    left,
+    right,
+    up,
+    down,
+    sem,
 ):
+    first = []
+    for x in range(4):
+        for n, half in enumerate((left, right)):
+            source = w_hbm.at[x, :, pl.ds(512 + 32 * n, 32), :]
+            first.append(pltpu.make_async_copy(source, half.at[:, x], sem.at[16 + 2 * x + n]))
+
     def fetch(t):
         return (
-            pltpu.make_async_copy(up_hbm.at[t], up.at[t], sem.at[2 * t + 1]),
-            pltpu.make_async_copy(rest_hbm.at[t, 0:512, :], down.at[t], sem.at[2 * t + 2]),
+            pltpu.make_async_copy(w_hbm.at[:, t, pl.ds(0, 256), :], up.at[t], sem.at[2 * t]),
+            pltpu.make_async_copy(w_hbm.at[:, t, pl.ds(256, 256), :], down.at[t], sem.at[2 * t + 1]),
         )
 
-    first = pltpu.make_async_copy(rest_hbm.at[:, 512:640, :], w_out, sem.at[0])
-    first.start()
+    for copy in first:
+        copy.start()
     for t in range(8):
         for copy in fetch(t):
             copy.start()
     att = jnp.concatenate([att_ref[i] for i in range(8)], axis=1)
-    first.wait()
-    hidden = tok_ref[...].astype(f32) + dot(att, w_out[...].reshape(1024, 1024))
+    for copy in first:
+        copy.wait()
+    proj = [dot(att, half[...].reshape(1024, 512)) for half in (left, right)]
+    hidden = tok_ref[...].astype(f32) + jnp.concatenate(proj, axis=1)
     normed = norm_rows(hidden, ag_ref[...], as_ref[...]).astype(bf16)
-
-    def block(t, acc):
+    acc[...] = normed.astype(f32)
+
+    def block(t, carry):
         up_copy, down_copy = fetch(t)
         up_copy.wait()
-        h = dot(normed, up[t])
+        h = dot(normed, up[t].reshape(1024, 512))
         inner = (0.5 * h * (1.0 + lax.erf(h * 0.7071067811865476))).astype(bf16)
         down_copy.wait()
-        return acc + dot(inner, down[t])
-
-    acc = lax.fori_loop(0, 8, block, jnp.zeros((64, 1024), f32))
-    hidden = normed.astype(f32) + acc
-    done = norm_rows(hidden, mg_ref[...], ms_ref[...]).astype(bf16)
+        for n in range(2):
+            weight = down[t, :, 128 * n : 128 * n + 128, :].reshape(512, 512)
+            acc[:, 512 * n : 512 * n + 512] += dot(inner, weight)
+        return carry
+
+    lax.fori_loop(0, 8, block, 0)
+    done = norm_rows(acc[...], mg_ref[...], ms_ref[...]).astype(bf16)
     for i in range(8):
         out_ref[i] = done[:, 128 * i : 128 * i + 128]
 
@@ -312,16 +359,21 @@
     core = lax.axis_index("c")
     rank = lax.axis_index(TP)
 
-    ups = lax.all_gather(up_weight, TP, axis=0, tiled=False)
+    hbm = pl.BlockSpec(memory_space=pl.ANY)
+    packed = pl.pallas_call(
+        pack_kernel,
+        in_specs=[SM] + [hbm] * 3,
+        out_specs=hbm,
+        out_shape=jax.ShapeDtypeStruct((576, 512), bf16),
+        scratch_shapes=[pltpu.SemaphoreType.DMA((5,))],
+        cost_estimate=cost(0, 1 << 20),
+        name="pack_weights",
+    )(lax.axis_index("x").reshape(1), up_weight, down_weight, out_weight)
+    shards = lax.all_gather(packed, ("x", "y", "c"), axis=0, tiled=False)
+    shards = shards.reshape(4, 8, 576, 512)
 
     own_half = swap_all(jnp.broadcast_to(tokens[None], (4, 512, 128)), "y")
     far_half = lax.ppermute(own_half, "c", [(0, 1), (1, 0)])
-
-    far_half, down_weight, out_weight = lax.optimization_barrier(
-        (far_half, down_weight, out_weight)
-    )
-    rest = jnp.concatenate([down_weight, out_weight], axis=0)
-    rest = lax.all_gather(rest, TP, axis=0, tiled=False)
 
     core1 = core.reshape(1)
     w_qkv = qkv_weight.transpose(1, 0, 2)
@@ -403,17 +455,18 @@
     odd = jnp.where(core == 0, far_rows, own_rows)
     tok_rows = jnp.stack([even, odd], axis=1).transpose(2, 0, 1, 3).reshape(64, 1024)
 
-    hbm = pl.BlockSpec(memory_space=pl.ANY)
     encoded = pl.pallas_call(
         tail_kernel,
-        in_specs=[VM] * 6 + [hbm] * 2,
+        in_specs=[VM] * 6 + [hbm],
         out_specs=VM,
         out_shape=jax.ShapeDtypeStruct((8, 64, 128), bf16),
         scratch_shapes=[
-            pltpu.VMEM((8, 128, 1024), bf16),
-            pltpu.VMEM((8, 1024, 512), bf16),
-            pltpu.VMEM((8, 512, 1024), bf16),
-            pltpu.SemaphoreType.DMA((17,)),
+            pltpu.VMEM((64, 1024), f32),
+            pltpu.VMEM((8, 4, 32, 512), bf16),
+            pltpu.VMEM((8, 4, 32, 512), bf16),
+            pltpu.VMEM((8, 4, 256, 512), bf16),
+            pltpu.VMEM((8, 4, 256, 512), bf16),
+            pltpu.SemaphoreType.DMA((24,)),
         ],
         compiler_params=pltpu.CompilerParams(vmem_limit_bytes=52 << 20),
         cost_estimate=cost(2 * 64 * 9 * 1024 * 1024, 19 << 20, 64 * 4096),
@@ -425,8 +478,7 @@
         attn_shift.reshape(1, 1024),
         mlp_gain.reshape(1, 1024),
         mlp_shift.reshape(1, 1024),
-        ups,
-        rest,
+        shards,
     )
     return swap_all(encoded, TP).reshape(512, 128)
 

time: 167 us -> 186 us (1.11)
  Pallas kernels: 23.4 us -> 42.1 us
  local copies, waits for them, and re-layouts: 2.7 us -> 11.8 us
  waiting for transfers between devices: 65.6 us -> 58.8 us
    pallas_call x1 -> x2, Pallas kernels: 7.77 us -> 26.5 us  [the longest x1 19 us: local(): pl.pallas_call(pack_kernel, in_specs=[SM] + [hbm] * 3, out_specs=hbm, out...]
    unnamed x27 -> x29, local copies, waits for them, and re-layouts: 0.75 us -> 7.62 us
    all_to_all x3, waiting for transfers between devices: 61.8 us -> 58.8 us  [swap_all(): return lax.all_to_all(value, axis, split_axis=0, concat_axis=0, tiled=True)]
  transfers between devices with their start and end apart: 6 -> 5, of which waited for: 5 -> 3; matrix products, arithmetic and copies ran while one was open for 2% -> 2% of each run, Pallas kernels for 9% -> 8%
where the time goes in v3:
time: 186 us; the launch traced here: 185 us
  waiting for transfers between devices  58.8 us (32%)
  Pallas kernels  42.1 us (23%)
  starting transfers between devices  38.5 us (21%)
  blocking collectives  20.3 us (11%)
  between operations  13.6 us (7%)
  local copies, waits for them, and re-layouts  11.8 us (6%)
    all_to_all x3, waiting for transfers between devices, swap_all(): return lax.all_to_all(value, axis, split_axis=0, concat_axis=0, tiled=True)  58.8 us
    all_to_all x3, starting transfers between devices, swap_all(): return lax.all_to_all(value, axis, split_axis=0, concat_axis=0, tiled=True)  31 us
    all_to_all x2, blocking collectives, swap_all(): return lax.all_to_all(value, axis, split_axis=0, concat_axis=0, tiled=True)  20.3 us
    pallas_call x1, Pallas kernels, local(): pl.pallas_call(pack_kernel, in_specs=[SM] + [hbm] * 3, out_specs=hbm, out...  19 us
    unnamed x29, local copies, waits for them, and re-layouts  7.62 us
    pallas_call x1, Pallas kernels, local(): pl.pallas_call(tail_kernel, in_specs=[VM] * 6 + [hbm], out_specs=VM, out_...  7.53 us
    ppermute x1, starting transfers between devices, local(): far_half = lax.ppermute(own_half, 'c', [(0, 1), (1, 0)])  7.51 us
    pallas_call x1, Pallas kernels, local(): pl.pallas_call(owner_kernel, in_specs=[VM] * 5, out_specs=VM, out_shape=j...  7.08 us
  transfers between devices with their start and end apart: 5, of which 3 were waited for; matrix products, arithmetic and copies ran while one was open for 2% of the time, Pallas kernels for 8%

profile of v3, /device:TPU:1, one launch (start us, length us, event | category | flops | bytes accessed | tf_op | source)
XLA Modules:
  0.0 185.1 jit_solution(11383331620418964355)
XLA Ops:
  6.5 0.0 copy-start.8
  6.5 0.0 copy-start.7
  6.5 0.0 copy-start.6
  6.5 0.0 copy-start.5
  6.5 0.0 all-gather.3.cloned.1.call-start
  6.6 19.0 %pack_weights.1 = bf16[576,512]{1,0:T(8,128)(2,1)} custom-call(s32[1]{0:T(128)} %bitcast.14.at, bf16[1024,512]{1,0:T(8,128)(2,1)} %up_ref.1, bf16[512,1024]{1,0:T(8,128)(2,1)} %down_ref.1, bf16[128,1024]{1,0:T(8,128)(2,1)} %out_ref.1), custom_call_target="tpu_custom_call" | custom-call | bytes 1048576 | tf_op jit(solution)/shard_map/pack_weights/pallas_call | solution.py:363
  25.6 0.0 all-gather.3.cloned.1.call-update
  25.6 1.0 broadcast_in_dim.2
  26.6 11.7 %all_to_all.25.half_ref = bf16[4,512,128]{2,1,0:T(8,128)(2,1)S(1)} all-to-all(bf16[4,512,128]{2,1,0:T(8,128)(2,1)S(1)} %broadcast_in_dim.2), channel_id=1, replica_groups=mesh['z'=16,'x'=4,'y'=4,'c'=2] {'y'}, dimensions={0} | all-to-all | bytes 1048576 | tf_op jit(solution)/shard_map/all_to_all | solution.py:335
  38.4 7.5 %collective-permute-start = (bf16[4,512,128]{2,1,0:T(8,128)(2,1)S(1)}, bf16[4,512,128]{2,1,0:T(8,128)(2,1)S(1)}, u32[]{:S(2)}, u32[]{:S(2)}) collective-permute-start(bf16[4,512,128]{2,1,0:T(8,128)(2,1)S(1)} %all_to_all.25.half_ref), channel_id=1, source_target_pairs={{0,1},{1,0},{2,3},{3,2},{4,5},{5,4},{6,7},{7,6},{8,9},{9,8},{10,11... | collective-permute-start | bytes 1572872 | tf_op jit(solution)/shard_map/ppermute | solution.py:376
  45.9 0.0 copy-start
  45.9 1.1 copy-done
  47.0 0.7 qkv_own_half.1.part_ref
  47.7 0.0 collective-permute-done.half_ref
  47.7 0.0 copy-start.1
  47.7 1.2 copy-done.1
  48.9 0.0 copy-start.2
  48.9 0.7 copy-done.2
  49.5 0.0 copy-start.9
  49.5 0.7 copy-done.9
  50.2 0.0 copy-start.11
  50.2 0.7 copy-done.11
  50.9 2.7 %qkv_place.1 = (bf16[64,32,128]{2,1,0:T(8,128)(2,1)}, bf16[512,384]{1,0:T(8,128)(2,1)S(1)}) custom-call(s32[1]{0:T(128)} %bitcast.core, s32[64]{0:T(128)S(1)} %copy-done.2, s32[64]{0:T(128)S(1)} %copy-done.9, s32[64]{0:T(128)S(1)} %copy-done.11, f32[512,384]{1,0:T(8,128)S(1)} %qkv_own_half.1.part_ref, ...), custom_call_target="tpu_custom_call" | custom-call | flops 201326592 | bytes 3145728 | tf_op jit(solution)/shard_map/qkv_place/pallas_call | solution.py:390
  53.5 16.2 %all-to-all-start.1 = ((bf16[64,32,128]{2,1,0:T(8,128)(2,1)}), bf16[64,32,128]{2,1,0:T(8,128)(2,1)S(1)}, u32[]{:S(2)}, u32[]{:S(2)}) async-start(bf16[64,32,128]{2,1,0:T(8,128)(2,1)} %get-tuple-element.9), calls=%async_computation.1 | async-start | bytes 1048576 | tf_op jit(solution)/shard_map/all_to_all | solution.py:335
  69.7 1.5 fusion
  71.3 1.5 fusion.1
  72.8 28.1 %all-to-all-done.1.got_ref = bf16[64,32,128]{2,1,0:T(8,128)(2,1)S(1)} async-done(((bf16[64,32,128]{2,1,0:T(8,128)(2,1)}), bf16[64,32,128]{2,1,0:T(8,128)(2,1)S(1)}, u32[]{:S(2)}, u32[]{:S(2)}) %all-to-all-start.1) | async-done | bytes 524320 | tf_op jit(solution)/shard_map/all_to_all | solution.py:335
  100.8 7.1 %owner_attention.1 = bf16[64,32,128]{2,1,0:T(8,128)(2,1)} custom-call(bf16[64,32,128]{2,1,0:T(8,128)(2,1)S(1)} %all-to-all-done.1.got_ref, bf16[2,256,128]{2,1,0:T(8,128)(2,1)S(1)} %get-tuple-element.20.pk_ref, bf16[2,256,128]{2,1,0:T(8,128)(2,1)S(1)} %get-tuple-element.19.pv_ref, bf16[512,128]{1,0:T(8,128)(2,1)S(1)} %bitcast.25, bf16[512,128]{1,0:T(8,128)(2,1)S(1)} %bitcast.24), custom_call_target="tpu_custom_call" | custom-call | flops 536870912 | bytes 2097152 | tf_op jit(solution)/shard_map/owner_attention/pallas_call | solution.py:416
  107.9 7.1 %all-to-all-start.2 = ((bf16[64,32,128]{2,1,0:T(8,128)(2,1)}), bf16[64,32,128]{2,1,0:T(8,128)(2,1)S(1)}, u32[]{:S(2)}, u32[]{:S(2)}) async-start(bf16[64,32,128]{2,1,0:T(8,128)(2,1)} %owner_attention.1), calls=%async_computation.2 | async-start | bytes 1048576 | tf_op jit(solution)/shard_map/all_to_all | solution.py:335
  115.0 0.0 copy-start.3
  115.0 0.6 copy-done.3
  115.7 3.0 %own_attention.1 = (f32[512,128]{1,0:T(8,128)S(1)}, f32[512,128]{1,0:T(8,128)S(1)}) custom-call(s32[64]{0:T(128)S(1)} %copy-done.3, bf16[512,384]{1,0:T(8,128)(2,1)S(1)} %get-tuple-element.10.qkv_ref), custom_call_target="tpu_custom_call" | custom-call | flops 67108864 | bytes 1048576 | tf_op jit(solution)/shard_map/own_attention/pallas_call | solution.py:406
  118.7 25.6 %all-to-all-done.2.ret_ref = bf16[64,32,128]{2,1,0:T(8,128)(2,1)S(1)} async-done(((bf16[64,32,128]{2,1,0:T(8,128)(2,1)}), bf16[64,32,128]{2,1,0:T(8,128)(2,1)S(1)}, u32[]{:S(2)}, u32[]{:S(2)}) %all-to-all-start.2) | async-done | bytes 524320 | tf_op jit(solution)/shard_map/all_to_all | solution.py:335
  144.3 0.0 copy-start.4
  144.3 0.7 copy-done.4
  145.0 0.0 copy-start.10
  145.0 0.7 copy-done.10
  145.7 0.0 copy-start.12
  145.7 0.7 copy-done.12
  146.3 2.2 %merge.1 = bf16[512,128]{1,0:T(8,128)(2,1)} custom-call(s32[64]{0:T(128)S(1)} %copy-done.4, s32[64]{0:T(128)S(1)} %copy-done.10, s32[64]{0:T(128)S(1)} %copy-done.12, bf16[64,32,128]{2,1,0:T(8,128)(2,1)S(1)} %all-to-all-done.2.ret_ref, f32[512,128]{1,0:T(8,128)S(1)} %get-tuple-element.11.own_ref, f32[512,128]{1,0:T(8,128)S(1)} %get-tuple-element.12.lse_ref), custom_call_target="tpu_custom_call" | custom-call | flops 33554432 | bytes 1048576 | tf_op jit(solution)/shard_map/merge/pallas_call | solution.py:439
  148.5 7.7 %all-to-all-start.3 = ((bf16[8,64,128]{2,1,0:T(8,128)(2,1)}), bf16[8,64,128]{2,1,0:T(8,128)(2,1)S(1)}, u32[]{:S(2)}, u32[]{:S(2)}) async-start(bf16[8,64,128]{2,1,0:T(8,128)(2,1)} %bitcast.6), calls=%async_computation.3 | async-start | bytes 262144 | tf_op jit(solution)/shard_map/all_to_all | solution.py:335
  156.2 0.1 copy.22
  156.4 0.1 reshape.33.tok_ref
  156.5 5.1 %all-to-all-done.3.att_ref = bf16[8,64,128]{2,1,0:T(8,128)(2,1)S(1)} async-done(((bf16[8,64,128]{2,1,0:T(8,128)(2,1)}), bf16[8,64,128]{2,1,0:T(8,128)(2,1)S(1)}, u32[]{:S(2)}, u32[]{:S(2)}) %all-to-all-start.3) | async-done | bytes 131104 | tf_op jit(solution)/shard_map/all_to_all | solution.py:335
  161.5 0.0 all-gather.3.cloned.1.call-done
  161.5 0.0 copy-done.8
  161.5 0.0 copy-done.7
  161.5 0.0 copy-done.6
  161.5 0.0 copy-done.5
  161.5 7.5 %project_norm_ffn.1 = bf16[8,64,128]{2,1,0:T(8,128)(2,1)S(1)} custom-call(bf16[8,64,128]{2,1,0:T(8,128)(2,1)S(1)} %all-to-all-done.3.att_ref, bf16[64,1024]{1,0:T(8,128)(2,1)S(1)} %reshape.33.tok_ref, f32[1,1024]{1,0:T(1,128)S(1)} %bitcast.26, f32[1,1024]{1,0:T(1,128)S(1)} %bitcast.27, f32[1,1024]{1,0:T(1,128)S(1)} %bitcast.28, f32[1,1024]{1,0:T(1,128)S(1)} %bitcast.29, ...), custom_call_target="tpu_custom_call" | custom-call | flops 1207959552 | bytes 19922944 | tf_op jit(solution)/shard_map/project_norm_ffn/pallas_call | solution.py:458
  169.1 8.5 %all_to_all.26 = bf16[8,64,128]{2,1,0:T(8,128)(2,1)S(1)} all-to-all(bf16[8,64,128]{2,1,0:T(8,128)(2,1)S(1)} %project_norm_ffn.1), channel_id=1, replica_groups=mesh['z'=16,'x'=4,'y'=4,'c'=2] {'y','c'}, dimensions={0} | all-to-all | bytes 262144 | tf_op jit(solution)/shard_map/all_to_all | solution.py:335
  177.6 0.7 copy.30
  (5 shorter events, 0.1 us)
Async XLA Ops:
  6.5 155.0 %copy-start.8 = (f32[1024]{0:T(1024)S(1)}, f32[1024]{0:T(1024)}, u32[]{:S(2)}) copy-start(f32[1024]{0:T(1024)} %param.22) | copy-start | bytes 12292
  6.5 155.0 %copy-start.7 = (f32[1024]{0:T(1024)S(1)}, f32[1024]{0:T(1024)}, u32[]{:S(2)}) copy-start(f32[1024]{0:T(1024)} %param.21) | copy-start | bytes 12292
  6.5 155.0 %copy-start.6 = (f32[1024]{0:T(1024)S(1)}, f32[1024]{0:T(1024)}, u32[]{:S(2)}) copy-start(f32[1024]{0:T(1024)} %param.18) | copy-start | bytes 12292
  6.5 155.0 %copy-start.5 = (f32[1024]{0:T(1024)S(1)}, f32[1024]{0:T(1024)}, u32[]{:S(2)}) copy-start(f32[1024]{0:T(1024)} %param.17) | copy-start | bytes 12292
  6.5 155.0 %all-gather.3.cloned.1.call-start = ((), (), s32[]{:S(2)}) async-start(), calls=%async_computation.5 | async-start | bytes 19464192 | tf_op jit(solution)/shard_map/all_gather | solution.py:372
  38.4 9.3 %collective-permute-start = (bf16[4,512,128]{2,1,0:T(8,128)(2,1)S(1)}, bf16[4,512,128]{2,1,0:T(8,128)(2,1)S(1)}, u32[]{:S(2)}, u32[]{:S(2)}) collective-permute-start(bf16[4,512,128]{2,1,0:T(8,128)(2,1)S(1)} %all_to_all.25.half_ref), channel_id=1, source_target_pairs={{0,1},{1,0},{2,3},{3,2},{4,5},{5,4},{6,7},{7,6},{8,9},{9,8},{10,11... | collective-permute-start | bytes 1572872 | tf_op jit(solution)/shard_map/ppermute | solution.py:376
  45.9 1.1 copy-start
  47.7 1.2 copy-start.1
  48.9 0.7 copy-start.2
  49.5 0.7 copy-start.9
  50.2 0.7 copy-start.11
  53.5 47.3 %all-to-all-start.1 = ((bf16[64,32,128]{2,1,0:T(8,128)(2,1)}), bf16[64,32,128]{2,1,0:T(8,128)(2,1)S(1)}, u32[]{:S(2)}, u32[]{:S(2)}) async-start(bf16[64,32,128]{2,1,0:T(8,128)(2,1)} %get-tuple-element.9), calls=%async_computation.1 | async-start | bytes 1048576 | tf_op jit(solution)/shard_map/all_to_all | solution.py:335
  107.9 36.4 %all-to-all-start.2 = ((bf16[64,32,128]{2,1,0:T(8,128)(2,1)}), bf16[64,32,128]{2,1,0:T(8,128)(2,1)S(1)}, u32[]{:S(2)}, u32[]{:S(2)}) async-start(bf16[64,32,128]{2,1,0:T(8,128)(2,1)} %owner_attention.1), calls=%async_computation.2 | async-start | bytes 1048576 | tf_op jit(solution)/shard_map/all_to_all | solution.py:335
  115.0 0.7 copy-start.3
  144.3 0.7 copy-start.4
  145.0 0.7 copy-start.10
  145.7 0.7 copy-start.12
  148.5 13.0 %all-to-all-start.3 = ((bf16[8,64,128]{2,1,0:T(8,128)(2,1)}), bf16[8,64,128]{2,1,0:T(8,128)(2,1)S(1)}, u32[]{:S(2)}, u32[]{:S(2)}) async-start(bf16[8,64,128]{2,1,0:T(8,128)(2,1)} %bitcast.6), calls=%async_computation.3 | async-start | bytes 262144 | tf_op jit(solution)/shard_map/all_to_all | solution.py:335
Sparse Core Ops, SparseCore 0:
  25.8 102.6 all-gather.2

commit v4 on v3

--- a/solution.py
+++ b/solution.py
@@ -44,19 +44,25 @@
     return weights.astype(bf16), 1.0 / total, top + jnp.log(total)
 
 
-def half_weight(w_ref, core, buf):
-    for y in range(4):
-        rows = pl.ds(pl.multiple_of((2 * y + core) * 128, 128), 128)
-        for n in range(3):
-            buf[128 * y : 128 * y + 128, 128 * n : 128 * n + 128] = w_ref[n, rows, :]
-
-
 def half_rows(half_ref, rows):
     return jnp.concatenate([half_ref[i, rows, :] for i in range(4)], axis=1)
 
 
-def part_kernel(core, half_ref, w_ref, part_ref, buf):
-    half_weight(w_ref, core[0], buf)
+def part_kernel(scal, half_ref, w_hbm, part_ref, far_ref, buf, sem):
+    core = scal[3, 0]
+    copies = []
+    for side, target in ((core, buf), (1 - core, far_ref)):
+        for y in range(4):
+            rows = pl.ds(pl.multiple_of((2 * y + side) * 128, 128), 128)
+            for n in range(3):
+                place = target.at[pl.ds(128 * y, 128), pl.ds(128 * n, 128)]
+                copies.append(
+                    pltpu.make_async_copy(w_hbm.at[n, rows, :], place, sem.at[len(copies)])
+                )
+    for copy in copies:
+        copy.start()
+    for copy in copies:
+        copy.wait()
 
     def block(b, carry):
         rows = pl.ds(pl.multiple_of(b * 256, 256), 256)
@@ -66,29 +72,28 @@
     lax.fori_loop(0, 2, block, 0)
 
 
-def pair_of(lens, pre, erl, g):
-    first, later = erl[2 * g], erl[2 * g + 1]
+def pair_of(scal, g):
+    first, later = scal[2, 2 * g], scal[2, 2 * g + 1]
     slot = jnp.maximum(first, later)
-    return pre[2 * g] // 2, slot // 32, slot % 32, later >= 0, lens[2 * g]
-
-
-def place_kernel(core, lens, pre, erl, part_ref, half_ref, w_ref, send_ref, qkv_ref, buf):
+    return scal[1, 2 * g] // 2, slot // 32, slot % 32, later >= 0, scal[0, 2 * g]
+
+
+def place_kernel(scal, part_ref, half_ref, w_ref, send_ref, qkv_ref):
     row = iota((16, 128), 0)
     lane = iota((16, 128), 1)
-    half_weight(w_ref, 1 - core[0], buf)
     send_ref[...] = jnp.zeros(send_ref.shape, bf16)
 
     def block(b, carry):
         rows = pl.ds(pl.multiple_of(b * 128, 128), 128)
-        out = part_ref[rows, :] + dot(half_rows(half_ref, rows), buf[...])
+        out = part_ref[rows, :] + dot(half_rows(half_ref, rows), w_ref[...])
         qkv_ref[rows, :] = out.astype(bf16)
         q = out[:, :128].astype(bf16)
         for p in range(8):
             g = b * 8 + p
-            slot, slot_e, row_e, late, span = pair_of(lens, pre, erl, g)
+            slot, slot_e, row_e, late, span = pair_of(scal, g)
             qp = q[16 * p : 16 * p + 16]
             send_ref[slot, 0:16, :] = qp
-            pick = jnp.where(lane < span, pre[2 * g] % 2, pre[2 * g + 1] % 2)
+            pick = jnp.where(lane < span, scal[1, 2 * g] % 2, scal[1, 2 * g + 1] % 2)
             pick = jnp.where((row == 15) & (lane < 16), pick, 0).astype(f32)
             held = send_ref[slot, 16:32, :].astype(f32)
             send_ref[slot, 16:32, :] = (held + pick).astype(bf16)
@@ -102,7 +107,7 @@
     lax.fori_loop(0, 4, block, 0)
 
 
-def own_kernel(lens, qkv_ref, out_ref, lse_ref):
+def own_kernel(scal, qkv_ref, out_ref, lse_ref):
     r = iota((128, 128), 0)
     c = iota((128, 128), 1)
 
@@ -112,7 +117,7 @@
         k = qkv_ref[rows, 128:256]
         v = qkv_ref[rows, 256:384]
         span = jnp.concatenate(
-            [jnp.full((16, 128), lens[2 * (b * 8 + p)], jnp.int32) for p in range(8)], axis=0
+            [jnp.full((16, 128), scal[0, 2 * (b * 8 + p)], jnp.int32) for p in range(8)], axis=0
         )
         same = ((r // 16) == (c // 16)) & (c <= r) & (((r % 16) < span) == ((c % 16) < span))
         res = []
@@ -136,7 +141,7 @@
     return head_mask(x[:n], 0) + head_mask(x[n:], 1)
 
 
-def owner_kernel(got_ref, pk_ref, pv_ref, ek_ref, ev_ref, ret_ref, row_v, row_s, sem):
+def owner_kernel(got_ref, pk_ref, pv_ref, ek_ref, ev_ref, ret_ref, row_v, row_s, stat, sem):
     sub = iota((8, 16, 128), 1)
     lane = iota((8, 16, 128), 2)
     group = lane // 16
@@ -144,22 +149,23 @@
     c = iota((256, 128), 1)
     near = ((r % 128) // 16) == (c // 16)
 
-    def rows_of(b, carry):
-        slots = pl.ds(pl.multiple_of(b * 8, 8), 8)
-        line = got_ref[slots, 16:32, :].astype(f32)[:, 15:16, :]
-        row_v[slots, :] = jnp.maximum(line.reshape(8, 128) - 1.0, 0.0).astype(jnp.int32)
-        return carry
-
-    lax.fori_loop(0, 8, rows_of, 0)
+    for b in range(8):
+        line = got_ref[8 * b : 8 * b + 8, 16:32, :].astype(f32)[:, 15:16, :].reshape(8, 128)
+        stat[8 * b : 8 * b + 8, :] = line
+        row_v[8 * b : 8 * b + 8, :] = jnp.maximum(line - 1.0, 0.0).astype(jnp.int32)
     copy = pltpu.make_async_copy(row_v, row_s, sem)
     copy.start()
-    copy.wait()
-
-    def prefix_part(b):
-        slots = pl.ds(b * 8, 8)
+
+    def stat_line(first, second):
+        both = jnp.where(group % 2 == 0, first.reshape(8, 16, 1), second.reshape(8, 16, 1))
+        line = jnp.sum(jnp.where(lane % 16 == sub, both, 0.0), axis=1)
+        high = line.astype(bf16).astype(f32)
+        return jnp.where((group[:, 0] // 2) % 2 == 1, line - high, high)
+
+    def prefix_part(b, carry):
+        slots = pl.ds(pl.multiple_of(b * 8, 8), 8)
         q = stack_heads(got_ref[slots, 0:16, :].reshape(128, 128))
-        line = got_ref[slots, 16:32, :].astype(f32)[:, 15:16, :]
-        info = jnp.broadcast_to(line, (8, 16, 128))
+        info = jnp.broadcast_to(stat[slots, :][:, None, :], (8, 16, 128))
         pick = jnp.sum(jnp.where(lane == sub, info, 0.0), axis=-1, keepdims=True)
         pick = pick.reshape(128, 1) > 0.5
         pick = jnp.broadcast_to(pick, (128, 256))
@@ -168,40 +174,31 @@
         w, inv, lse = softmax_parts(s, None)
         none = jnp.zeros_like(w)
         o = dot(jnp.where(pick, none, w), pv_ref[0]) + dot(jnp.where(pick, w, none), pv_ref[1])
-        return join_heads(o * inv), lse
-
-    def earlier_part(b):
-        slots = pl.ds(b * 8, 8)
+        ret_ref[slots, 0:16, :] = join_heads(o * inv).astype(bf16).reshape(8, 16, 128)
+        stat[slots, :] = stat_line(lse[:128], lse[128:])
+        return carry
+
+    lax.fori_loop(0, 8, prefix_part, 0, unroll=2)
+    copy.wait()
+
+    def earlier_part(b, carry):
+        slots = pl.ds(pl.multiple_of(b * 8, 8), 8)
         q = stack_heads(got_ref[slots, 16:32, :].reshape(128, 128))
         at = [pl.ds(pl.multiple_of(row_s[b * 8 + i, 16] * 16, 16), 16) for i in range(8)]
         keys = jnp.concatenate([ek_ref[x, :] for x in at], axis=0)
         values = jnp.concatenate([ev_ref[x, :] for x in at], axis=0)
         w, inv, lse = softmax_parts(dot_t(q, keys), near)
-        return join_heads(dot(w, values) * inv), lse
-
-    def block(b, carry):
-        slots = pl.ds(b * 8, 8)
-        pre, pre_lse = prefix_part(b)
-        erl, erl_lse = earlier_part(b)
-        ret_ref[slots, 0:16, :] = pre.astype(bf16).reshape(8, 16, 128)
-        stats = (pre_lse[:128], pre_lse[128:], erl_lse[:128], erl_lse[128:])
-        spread = jnp.zeros((8, 16, 128), f32)
-        for n in range(4):
-            want = ((group // 4) * 2 + group % 2) == n
-            spread = jnp.where(want, stats[n].reshape(8, 16, 1), spread)
-        line = jnp.sum(jnp.where(lane % 16 == sub, spread, 0.0), axis=1, keepdims=True)
-        high = line.astype(bf16).astype(f32)
-        line = jnp.where((group[:, 0:1] // 2) % 2 == 1, line - high, high)
-        ret_ref[slots, 16:32, :] = jnp.where(
-            sub == 15, jnp.broadcast_to(line, (8, 16, 128)), erl.reshape(8, 16, 128)
-        ).astype(bf16)
-        return carry
-
-    lax.fori_loop(0, 8, block, 0, unroll=2)
+        out = join_heads(dot(w, values) * inv).reshape(8, 16, 128)
+        line = jnp.where(group[:, 0] < 4, stat[slots, :], stat_line(lse[:128], lse[128:]))
+        line = jnp.broadcast_to(line[:, None, :], (8, 16, 128))
+        ret_ref[slots, 16:32, :] = jnp.where(sub == 15, line, out).astype(bf16)
+        return carry
+
+    lax.fori_loop(0, 8, earlier_part, 0, unroll=2)
 
 
 def merge_kernel(
-    lens, pre, erl, ret_ref, own_ref, lse_ref, out_ref, pre_o, pre_s, erl_o, erl_s, erl_on
+    scal, ret_ref, own_ref, lse_ref, out_ref, pre_o, pre_s, erl_o, erl_s, erl_on
 ):
     row = iota((16, 128), 0)
     lane = iota((16, 128), 1)
@@ -211,7 +208,7 @@
         for p in range(8):
             g = b * 8 + p
             rows = pl.ds(pl.multiple_of(b * 128, 128) + 16 * p, 16)
-            slot, slot_e, _, late, span = pair_of(lens, pre, erl, g)
+            slot, slot_e, _, late, span = pair_of(scal, g)
             pre_o[rows, :] = ret_ref[slot, 0:16, :].astype(f32)
             line = jnp.broadcast_to(ret_ref[slot, 16:32, :].astype(f32)[15:16, :], (16, 128))
             pre_s[rows, :] = jnp.where(diag & (lane < 64), line, 0.0)
@@ -250,27 +247,22 @@
     return centred * lax.rsqrt(var + EPS) * gain + shift
 
 
-def pack_kernel(at, up_ref, down_ref, out_ref, pack_ref, sem):
-    x = at[0]
-    up_rows = pl.ds(pl.multiple_of(x * 256, 256), 256)
-    down_rows = pl.ds(pl.multiple_of(x * 128, 128), 128)
-    out_rows = pl.ds(pl.multiple_of(x * 32, 32), 32)
-    left, right = pl.ds(0, 512), pl.ds(512, 512)
-    copies = (
-        (up_ref.at[up_rows, :], 0, 256),
-        (down_ref.at[down_rows, left], 256, 128),
-        (down_ref.at[down_rows, right], 384, 128),
-        (out_ref.at[out_rows, left], 512, 32),
-        (out_ref.at[out_rows, right], 544, 32),
-    )
-    copies = [
-        pltpu.make_async_copy(source, pack_ref.at[pl.ds(first, size), :], sem.at[i])
-        for i, (source, first, size) in enumerate(copies)
-    ]
-    for copy in copies:
-        copy.start()
-    for copy in copies:
-        copy.wait()
+def pack_kernel(at, up_ref, down_ref, out_ref, pack_ref):
+    pack_ref[0:256, :] = up_ref[...]
+    pack_ref[256:384, :] = down_ref[:, 0:512]
+    pack_ref[384:512, :] = down_ref[:, 512:1024]
+    pack_ref[512:544, :] = out_ref[:, 0:512]
+    pack_ref[544:576, :] = out_ref[:, 512:1024]
+
+
+def row_kernel(scal, own_ref, far_ref, rows_ref):
+    core = scal[3, 0]
+    rows = pl.ds(pl.multiple_of(scal[3, 1] * 64, 64), 64)
+    for y in range(4):
+        own, far = own_ref[y, rows, :], far_ref[y, rows, :]
+        at = 256 * y
+        rows_ref[:, at : at + 128] = jnp.where(core == 0, own, far)
+        rows_ref[:, at + 128 : at + 256] = jnp.where(core == 0, far, own)
 
 
 def tail_kernel(
@@ -362,10 +354,17 @@
     hbm = pl.BlockSpec(memory_space=pl.ANY)
     packed = pl.pallas_call(
         pack_kernel,
-        in_specs=[SM] + [hbm] * 3,
-        out_specs=hbm,
+        grid_spec=pltpu.PrefetchScalarGridSpec(
+            num_scalar_prefetch=1,
+            grid=(1,),
+            in_specs=[
+                pl.BlockSpec((256, 512), lambda i, at: (at[0], 0)),
+                pl.BlockSpec((128, 1024), lambda i, at: (at[0], 0)),
+                pl.BlockSpec((32, 1024), lambda i, at: (at[0], 0)),
+            ],
+            out_specs=pl.BlockSpec((576, 512), lambda i, at: (0, 0)),
+        ),
         out_shape=jax.ShapeDtypeStruct((576, 512), bf16),
-        scratch_shapes=[pltpu.SemaphoreType.DMA((5,))],
         cost_estimate=cost(0, 1 << 20),
         name="pack_weights",
     )(lax.axis_index("x").reshape(1), up_weight, down_weight, out_weight)
@@ -375,31 +374,33 @@
     own_half = swap_all(jnp.broadcast_to(tokens[None], (4, 512, 128)), "y")
     far_half = lax.ppermute(own_half, "c", [(0, 1), (1, 0)])
 
-    core1 = core.reshape(1)
-    w_qkv = qkv_weight.transpose(1, 0, 2)
-    part = pl.pallas_call(
+    place = jnp.where(jnp.arange(64) % 2 == 0, core, rank)
+    scal = jnp.stack([suffix_len, prefix_id, earlier_slot, place])
+    part, w_far = pl.pallas_call(
         part_kernel,
-        in_specs=[SM, VM, VM],
-        out_specs=VM,
-        out_shape=jax.ShapeDtypeStruct((512, 384), f32),
-        scratch_shapes=[pltpu.VMEM((512, 384), bf16)],
+        in_specs=[SM, VM, hbm],
+        out_specs=[VM, VM],
+        out_shape=[
+            jax.ShapeDtypeStruct((512, 384), f32),
+            jax.ShapeDtypeStruct((512, 384), bf16),
+        ],
+        scratch_shapes=[pltpu.VMEM((512, 384), bf16), pltpu.SemaphoreType.DMA((24,))],
         compiler_params=SMALL,
         cost_estimate=cost(2 * 512 * 512 * 384, 2 << 20),
         name="qkv_own_half",
-    )(core1, own_half, w_qkv)
+    )(scal, own_half, qkv_weight.transpose(1, 0, 2))
     send, qkv = pl.pallas_call(
         place_kernel,
-        in_specs=[SM] * 4 + [VM] * 3,
+        in_specs=[SM] + [VM] * 3,
         out_specs=[VM, VM],
         out_shape=[
             jax.ShapeDtypeStruct((n_req, 32, 128), bf16),
             jax.ShapeDtypeStruct((512, 384), bf16),
         ],
-        scratch_shapes=[pltpu.VMEM((512, 384), bf16)],
         compiler_params=SMALL,
         cost_estimate=cost(2 * 512 * 512 * 384, 3 << 20),
         name="qkv_place",
-    )(core1, suffix_len, prefix_id, earlier_slot, part, far_half, w_qkv)
+    )(scal, part, far_half, w_far)
 
     got = swap_all(send, REQ)
 
@@ -411,7 +412,7 @@
         compiler_params=SMALL,
         cost_estimate=cost(2 * 512 * 128 * 128 * 4, 1 << 20, 2 * 512 * 128),
         name="own_attention",
-    )(suffix_len, qkv)
+    )(scal, qkv)
 
     ret = pl.pallas_call(
         owner_kernel,
@@ -421,6 +422,7 @@
         scratch_shapes=[
             pltpu.VMEM((n_req, 128), jnp.int32),
             pltpu.SMEM((n_req, 128), jnp.int32),
+            pltpu.VMEM((n_req, 128), f32),
             pltpu.SemaphoreType.DMA,
         ],
         compiler_params=SMALL,
@@ -438,22 +440,26 @@
 
     attended = pl.pallas_call(
         merge_kernel,
-        in_specs=[SM, SM, SM, VM, VM, VM],
+        in_specs=[SM, VM, VM, VM],
         out_specs=VM,
         out_shape=jax.ShapeDtypeStruct((512, 128), bf16),
         scratch_shapes=[pltpu.VMEM((512, 128), f32)] * 5,
         cost_estimate=cost(2 * 512 * 128 * 256, 1 << 20, 3 * 512 * 128),
         compiler_params=SMALL,
         name="merge",
-    )(suffix_len, prefix_id, earlier_slot, back, own_out, own_lse)
+    )(scal, back, own_out, own_lse)
 
     att = swap_all(attended.reshape(8, 64, 128), TP)
 
-    own_rows = lax.dynamic_slice_in_dim(own_half, rank * 64, 64, 1)
-    far_rows = lax.dynamic_slice_in_dim(far_half, rank * 64, 64, 1)
-    even = jnp.where(core == 0, own_rows, far_rows)
-    odd = jnp.where(core == 0, far_rows, own_rows)
-    tok_rows = jnp.stack([even, odd], axis=1).transpose(2, 0, 1, 3).reshape(64, 1024)
+    tok_rows = pl.pallas_call(
+        row_kernel,
+        in_specs=[SM, VM, VM],
+        out_specs=VM,
+        out_shape=jax.ShapeDtypeStruct((64, 1024), bf16),
+        compiler_params=SMALL,
+        cost_estimate=cost(0, 60 << 20),
+        name="token_rows",
+    )(scal, own_half, far_half)
 
     encoded = pl.pallas_call(
         tail_kernel,

time: 186 us -> 165 us (0.89)
  Pallas kernels: 42.1 us -> 26.1 us
  local copies, waits for them, and re-layouts: 11.8 us -> 5.82 us
    pallas_call x4 -> x5, Pallas kernels: 24.5 us -> 9.11 us  [the longest x1 2.73 us: local(): pl.pallas_call(place_kernel, in_specs=[SM] + [VM] * 3, out_specs=[VM, VM]...]
    unnamed x29 -> x13, local copies, waits for them, and re-layouts: 7.62 us -> 1.84 us
  transfers between devices with their start and end apart: 5 -> 5, of which waited for: 3 -> 3; matrix products, arithmetic and copies ran while one was open for 2% -> 3% of each run, Pallas kernels for 8% -> 10%
where the time goes in v4:
time: 165 us; the launch traced here: 164 us
  waiting for transfers between devices  59.2 us (36%)
  starting transfers between devices  38.4 us (23%)
  Pallas kernels  26.1 us (16%)
  blocking collectives  20.3 us (12%)
  between operations  13.5 us (8%)
  local copies, waits for them, and re-layouts  5.82 us (4%)
    all_to_all x3, waiting for transfers between devices, swap_all(): return lax.all_to_all(value, axis, split_axis=0, concat_axis=0, tiled=True)  59.2 us
    all_to_all x3, starting transfers between devices, swap_all(): return lax.all_to_all(value, axis, split_axis=0, concat_axis=0, tiled=True)  30.9 us
    all_to_all x2, blocking collectives, swap_all(): return lax.all_to_all(value, axis, split_axis=0, concat_axis=0, tiled=True)  20.3 us
    pallas_call x1, Pallas kernels, local(): pl.pallas_call(tail_kernel, in_specs=[VM] * 6 + [hbm], out_specs=VM, out_...  7.54 us
    ppermute x1, starting transfers between devices, local(): far_half = lax.ppermute(own_half, 'c', [(0, 1), (1, 0)])  7.51 us
    pallas_call x1, Pallas kernels, local(): pl.pallas_call(owner_kernel, in_specs=[VM] * 5, out_specs=VM, out_shape=j...  6.51 us
  transfers between devices with their start and end apart: 5, of which 3 were waited for; matrix products, arithmetic and copies ran while one was open for 3% of the time, Pallas kernels for 10%

profile of v4, /device:TPU:1, one launch (start us, length us, event | category | flops | bytes accessed | tf_op | source)
XLA Modules:
  0.0 164.1 jit_solution(12841724849096449714)
XLA Ops:
  6.5 0.0 copy-start.2
  6.5 0.0 copy-start.3
  6.5 0.0 copy-start.4
  6.5 0.0 copy-start.1
  6.5 0.0 all-gather.3.cloned.1.call-start
  6.6 1.9 %pack_weights.1 = bf16[576,512]{1,0:T(8,128)(2,1)} custom-call(s32[1]{0:T(128)} %bitcast.13.at, bf16[1024,512]{1,0:T(8,128)(2,1)} %up_ref.1, bf16[512,1024]{1,0:T(8,128)(2,1)} %down_ref.1, bf16[128,1024]{1,0:T(8,128)(2,1)} %out_ref.1), custom_call_target="tpu_custom_call" | custom-call | bytes 1048576 | tf_op jit(solution)/shard_map/pack_weights/pallas_call | solution.py:355
  8.5 0.0 all-gather.3.cloned.1.call-update
  8.5 1.0 broadcast_in_dim.16
  9.5 11.7 %all_to_all.25.half_ref.own_ref = bf16[4,512,128]{2,1,0:T(8,128)(2,1)S(1)} all-to-all(bf16[4,512,128]{2,1,0:T(8,128)(2,1)S(1)} %broadcast_in_dim.16), channel_id=1, replica_groups=mesh['z'=16,'x'=4,'y'=4,'c'=2] {'y'}, dimensions={0} | all-to-all | bytes 1048576 | tf_op jit(solution)/shard_map/all_to_all | solution.py:327
  21.2 7.5 %collective-permute-start = (bf16[4,512,128]{2,1,0:T(8,128)(2,1)S(1)}, bf16[4,512,128]{2,1,0:T(8,128)(2,1)S(1)}, u32[]{:S(2)}, u32[]{:S(2)}) collective-permute-start(bf16[4,512,128]{2,1,0:T(8,128)(2,1)S(1)} %all_to_all.25.half_ref.own_ref), channel_id=1, source_target_pairs={{0,1},{1,0},{2,3},{3,2},{4,5},{5,4},{6,7},{7,6},{8,9},{9,8},{10,11... | collective-permute-start | bytes 1572872 | tf_op jit(solution)/shard_map/ppermute | solution.py:375
  28.8 0.7 pad_add_fusion.scal
  29.5 0.0 copy-start
  29.5 1.1 copy-done
  30.6 1.6 qkv_own_half.1
  32.2 0.0 collective-permute-done.half_ref.far_ref
  32.2 2.7 %qkv_place.1 = (bf16[64,32,128]{2,1,0:T(8,128)(2,1)}, bf16[512,384]{1,0:T(8,128)(2,1)S(1)}) custom-call(s32[4,64]{1,0:T(4,128)S(1)} %pad_add_fusion.scal, f32[512,384]{1,0:T(8,128)S(1)} %get-tuple-element.11.part_ref, bf16[4,512,128]{2,1,0:T(8,128)(2,1)S(1)} %collective-permute-done.half_ref.far_ref, bf16[512,384]{1,0:T(8,128)(2,1)S(1)} %get-tuple-element.12.w_ref), custom_call_target="tpu_custom_call" | custom-call | flops 201326592 | bytes 3145728 | tf_op jit(solution)/shard_map/qkv_place/pallas_call | solution.py:392
  34.9 16.2 %all-to-all-start.1 = ((bf16[64,32,128]{2,1,0:T(8,128)(2,1)}), bf16[64,32,128]{2,1,0:T(8,128)(2,1)S(1)}, u32[]{:S(2)}, u32[]{:S(2)}) async-start(bf16[64,32,128]{2,1,0:T(8,128)(2,1)} %get-tuple-element.13), calls=%async_computation.1 | async-start | bytes 1048576 | tf_op jit(solution)/shard_map/all_to_all | solution.py:327
  51.1 1.5 fusion
  52.6 1.5 fusion.1
  54.2 28.1 %all-to-all-done.1.got_ref = bf16[64,32,128]{2,1,0:T(8,128)(2,1)S(1)} async-done(((bf16[64,32,128]{2,1,0:T(8,128)(2,1)}), bf16[64,32,128]{2,1,0:T(8,128)(2,1)S(1)}, u32[]{:S(2)}, u32[]{:S(2)}) %all-to-all-start.1) | async-done | bytes 524320 | tf_op jit(solution)/shard_map/all_to_all | solution.py:327
  82.3 6.5 %owner_attention.1 = bf16[64,32,128]{2,1,0:T(8,128)(2,1)} custom-call(bf16[64,32,128]{2,1,0:T(8,128)(2,1)S(1)} %all-to-all-done.1.got_ref, bf16[2,256,128]{2,1,0:T(8,128)(2,1)S(1)} %get-tuple-element.22.pk_ref, bf16[2,256,128]{2,1,0:T(8,128)(2,1)S(1)} %get-tuple-element.21.pv_ref, bf16[512,128]{1,0:T(8,128)(2,1)S(1)} %bitcast.19, bf16[512,128]{1,0:T(8,128)(2,1)S(1)} %bitcast.20), custom_call_target="tpu_custom_call" | custom-call | flops 536870912 | bytes 2097152 | tf_op jit(solution)/shard_map/owner_attention/pallas_call | solution.py:417
  88.8 7.0 %all-to-all-start.2 = ((bf16[64,32,128]{2,1,0:T(8,128)(2,1)}), bf16[64,32,128]{2,1,0:T(8,128)(2,1)S(1)}, u32[]{:S(2)}, u32[]{:S(2)}) async-start(bf16[64,32,128]{2,1,0:T(8,128)(2,1)} %owner_attention.1), calls=%async_computation.2 | async-start | bytes 1048576 | tf_op jit(solution)/shard_map/all_to_all | solution.py:327
  95.9 3.0 %own_attention.1 = (f32[512,128]{1,0:T(8,128)S(1)}, f32[512,128]{1,0:T(8,128)S(1)}) custom-call(s32[4,64]{1,0:T(4,128)S(1)} %pad_add_fusion.scal, bf16[512,384]{1,0:T(8,128)(2,1)S(1)} %get-tuple-element.14.qkv_ref), custom_call_target="tpu_custom_call" | custom-call | flops 67108864 | bytes 1048576 | tf_op jit(solution)/shard_map/own_attention/pallas_call | solution.py:407
  98.9 26.4 %all-to-all-done.2.ret_ref = bf16[64,32,128]{2,1,0:T(8,128)(2,1)S(1)} async-done(((bf16[64,32,128]{2,1,0:T(8,128)(2,1)}), bf16[64,32,128]{2,1,0:T(8,128)(2,1)S(1)}, u32[]{:S(2)}, u32[]{:S(2)}) %all-to-all-start.2) | async-done | bytes 524320 | tf_op jit(solution)/shard_map/all_to_all | solution.py:327
  125.3 2.3 %merge.1 = bf16[512,128]{1,0:T(8,128)(2,1)} custom-call(s32[4,64]{1,0:T(4,128)S(1)} %pad_add_fusion.scal, bf16[64,32,128]{2,1,0:T(8,128)(2,1)S(1)} %all-to-all-done.2.ret_ref, f32[512,128]{1,0:T(8,128)S(1)} %get-tuple-element.15.own_ref, f32[512,128]{1,0:T(8,128)S(1)} %get-tuple-element.16.lse_ref), custom_call_target="tpu_custom_call" | custom-call | flops 33554432 | bytes 1048576 | tf_op jit(solution)/shard_map/merge/pallas_call | solution.py:441
  127.6 7.7 %all-to-all-start.3 = ((bf16[8,64,128]{2,1,0:T(8,128)(2,1)}), bf16[8,64,128]{2,1,0:T(8,128)(2,1)S(1)}, u32[]{:S(2)}, u32[]{:S(2)}) async-start(bf16[8,64,128]{2,1,0:T(8,128)(2,1)} %bitcast.8), calls=%async_computation.3 | async-start | bytes 262144 | tf_op jit(solution)/shard_map/all_to_all | solution.py:327
  135.2 0.6 token_rows.1.tok_ref
  135.8 4.7 %all-to-all-done.3.att_ref = bf16[8,64,128]{2,1,0:T(8,128)(2,1)S(1)} async-done(((bf16[8,64,128]{2,1,0:T(8,128)(2,1)}), bf16[8,64,128]{2,1,0:T(8,128)(2,1)S(1)}, u32[]{:S(2)}, u32[]{:S(2)}) %all-to-all-start.3) | async-done | bytes 131104 | tf_op jit(solution)/shard_map/all_to_all | solution.py:327
  140.5 0.0 all-gather.3.cloned.1.call-done
  140.5 0.0 copy-done.2
  140.5 0.0 copy-done.3
  140.5 0.0 copy-done.4
  140.5 0.0 copy-done.1
  140.6 7.5 %project_norm_ffn.1 = bf16[8,64,128]{2,1,0:T(8,128)(2,1)S(1)} custom-call(bf16[8,64,128]{2,1,0:T(8,128)(2,1)S(1)} %all-to-all-done.3.att_ref, bf16[64,1024]{1,0:T(8,128)(2,1)S(1)} %token_rows.1.tok_ref, f32[1,1024]{1,0:T(1,128)S(1)} %bitcast.21, f32[1,1024]{1,0:T(1,128)S(1)} %bitcast.22, f32[1,1024]{1,0:T(1,128)S(1)} %bitcast.23, f32[1,1024]{1,0:T(1,128)S(1)} %bitcast.24, ...), custom_call_target="tpu_custom_call" | custom-call | flops 1207959552 | bytes 19922944 | tf_op jit(solution)/shard_map/project_norm_ffn/pallas_call | solution.py:464
  148.1 8.5 %all_to_all.26 = bf16[8,64,128]{2,1,0:T(8,128)(2,1)S(1)} all-to-all(bf16[8,64,128]{2,1,0:T(8,128)(2,1)S(1)} %project_norm_ffn.1), channel_id=1, replica_groups=mesh['z'=16,'x'=4,'y'=4,'c'=2] {'y','c'}, dimensions={0} | all-to-all | bytes 262144 | tf_op jit(solution)/shard_map/all_to_all | solution.py:327
  156.6 0.7 copy.28
  (4 shorter events, 0.1 us)
Async XLA Ops:
  6.5 134.0 %copy-start.2 = (f32[1024]{0:T(1024)S(1)}, f32[1024]{0:T(1024)}, u32[]{:S(2)}) copy-start(f32[1024]{0:T(1024)} %param.18) | copy-start | bytes 12292
  6.5 134.0 %copy-start.3 = (f32[1024]{0:T(1024)S(1)}, f32[1024]{0:T(1024)}, u32[]{:S(2)}) copy-start(f32[1024]{0:T(1024)} %param.21) | copy-start | bytes 12292
  6.5 134.0 %copy-start.4 = (f32[1024]{0:T(1024)S(1)}, f32[1024]{0:T(1024)}, u32[]{:S(2)}) copy-start(f32[1024]{0:T(1024)} %param.22) | copy-start | bytes 12292
  6.5 134.0 %copy-start.1 = (f32[1024]{0:T(1024)S(1)}, f32[1024]{0:T(1024)}, u32[]{:S(2)}) copy-start(f32[1024]{0:T(1024)} %param.17) | copy-start | bytes 12292
  6.5 134.0 %all-gather.3.cloned.1.call-start = ((), (), s32[]{:S(2)}) async-start(), calls=%async_computation.5 | async-start | bytes 19464192 | tf_op jit(solution)/shard_map/all_gather | solution.py:371
  21.2 11.0 %collective-permute-start = (bf16[4,512,128]{2,1,0:T(8,128)(2,1)S(1)}, bf16[4,512,128]{2,1,0:T(8,128)(2,1)S(1)}, u32[]{:S(2)}, u32[]{:S(2)}) collective-permute-start(bf16[4,512,128]{2,1,0:T(8,128)(2,1)S(1)} %all_to_all.25.half_ref.own_ref), channel_id=1, source_target_pairs={{0,1},{1,0},{2,3},{3,2},{4,5},{5,4},{6,7},{7,6},{8,9},{9,8},{10,11... | collective-permute-start | bytes 1572872 | tf_op jit(solution)/shard_map/ppermute | solution.py:375
  29.5 1.1 copy-start
  34.9 47.4 %all-to-all-start.1 = ((bf16[64,32,128]{2,1,0:T(8,128)(2,1)}), bf16[64,32,128]{2,1,0:T(8,128)(2,1)S(1)}, u32[]{:S(2)}, u32[]{:S(2)}) async-start(bf16[64,32,128]{2,1,0:T(8,128)(2,1)} %get-tuple-element.13), calls=%async_computation.1 | async-start | bytes 1048576 | tf_op jit(solution)/shard_map/all_to_all | solution.py:327
  88.8 36.4 %all-to-all-start.2 = ((bf16[64,32,128]{2,1,0:T(8,128)(2,1)}), bf16[64,32,128]{2,1,0:T(8,128)(2,1)S(1)}, u32[]{:S(2)}, u32[]{:S(2)}) async-start(bf16[64,32,128]{2,1,0:T(8,128)(2,1)} %owner_attention.1), calls=%async_computation.2 | async-start | bytes 1048576 | tf_op jit(solution)/shard_map/all_to_all | solution.py:327
  127.6 13.0 %all-to-all-start.3 = ((bf16[8,64,128]{2,1,0:T(8,128)(2,1)}), bf16[8,64,128]{2,1,0:T(8,128)(2,1)S(1)}, u32[]{:S(2)}, u32[]{:S(2)}) async-start(bf16[8,64,128]{2,1,0:T(8,128)(2,1)} %bitcast.8), calls=%async_computation.3 | async-start | bytes 262144 | tf_op jit(solution)/shard_map/all_to_all | solution.py:327
Sparse Core Ops, SparseCore 0:
  10.5 103.3 all-gather.2

commit v5 on v4

--- a/solution.py
+++ b/solution.py
@@ -48,28 +48,16 @@
     return jnp.concatenate([half_ref[i, rows, :] for i in range(4)], axis=1)
 
 
-def part_kernel(scal, half_ref, w_hbm, part_ref, far_ref, buf, sem):
+def part_kernel(scal, half_ref, w_ref, part_ref, far_ref, buf):
     core = scal[3, 0]
-    copies = []
     for side, target in ((core, buf), (1 - core, far_ref)):
         for y in range(4):
             rows = pl.ds(pl.multiple_of((2 * y + side) * 128, 128), 128)
             for n in range(3):
-                place = target.at[pl.ds(128 * y, 128), pl.ds(128 * n, 128)]
-                copies.append(
-                    pltpu.make_async_copy(w_hbm.at[n, rows, :], place, sem.at[len(copies)])
-                )
-    for copy in copies:
-        copy.start()
-    for copy in copies:
-        copy.wait()
-
-    def block(b, carry):
-        rows = pl.ds(pl.multiple_of(b * 256, 256), 256)
+                target[128 * y : 128 * y + 128, 128 * n : 128 * n + 128] = w_ref[n, rows, :]
+    for b in range(2):
+        rows = pl.ds(256 * b, 256)
         part_ref[rows, :] = dot(half_rows(half_ref, rows), buf[...])
-        return carry
-
-    lax.fori_loop(0, 2, block, 0)
 
 
 def pair_of(scal, g):
@@ -104,7 +92,7 @@
             send_ref[slot_e, 16:32, :] = jnp.where(row == 15, held, moved).astype(bf16)
         return carry
 
-    lax.fori_loop(0, 4, block, 0)
+    lax.fori_loop(0, 4, block, 0, unroll=4)
 
 
 def own_kernel(scal, qkv_ref, out_ref, lse_ref):
@@ -178,7 +166,7 @@
         stat[slots, :] = stat_line(lse[:128], lse[128:])
         return carry
 
-    lax.fori_loop(0, 8, prefix_part, 0, unroll=2)
+    lax.fori_loop(0, 8, prefix_part, 0, unroll=8)
     copy.wait()
 
     def earlier_part(b, carry):
@@ -194,7 +182,7 @@
         ret_ref[slots, 16:32, :] = jnp.where(sub == 15, line, out).astype(bf16)
         return carry
 
-    lax.fori_loop(0, 8, earlier_part, 0, unroll=2)
+    lax.fori_loop(0, 8, earlier_part, 0, unroll=8)
 
 
 def merge_kernel(
@@ -237,7 +225,7 @@
         out_ref[rows, :] = (mixed / (w_own + w_pre + w_erl)).astype(bf16)
         return carry
 
-    lax.fori_loop(0, 4, block, 0)
+    lax.fori_loop(0, 4, block, 0, unroll=4)
 
 
 def norm_rows(hidden, gain, shift):
@@ -265,6 +253,18 @@
         rows_ref[:, at + 128 : at + 256] = jnp.where(core == 0, far, own)
 
 
+def stage_kernel(w_hbm, left, right, sem):
+    copies = []
+    for x in range(4):
+        for n, half in enumerate((left, right)):
+            source = w_hbm.at[x, :, pl.ds(512 + 32 * n, 32), :]
+            copies.append(pltpu.make_async_copy(source, half.at[:, x], sem.at[2 * x + n]))
+    for copy in copies:
+        copy.start()
+    for copy in copies:
+        copy.wait()
+
+
 def tail_kernel(
     att_ref,
     tok_ref,
@@ -272,35 +272,25 @@
     as_ref,
     mg_ref,
     ms_ref,
+    left,
+    right,
     w_hbm,
     out_ref,
     acc,
-    left,
-    right,
     up,
     down,
     sem,
 ):
-    first = []
-    for x in range(4):
-        for n, half in enumerate((left, right)):
-            source = w_hbm.at[x, :, pl.ds(512 + 32 * n, 32), :]
-            first.append(pltpu.make_async_copy(source, half.at[:, x], sem.at[16 + 2 * x + n]))
-
     def fetch(t):
         return (
             pltpu.make_async_copy(w_hbm.at[:, t, pl.ds(0, 256), :], up.at[t], sem.at[2 * t]),
             pltpu.make_async_copy(w_hbm.at[:, t, pl.ds(256, 256), :], down.at[t], sem.at[2 * t + 1]),
         )
 
-    for copy in first:
-        copy.start()
     for t in range(8):
         for copy in fetch(t):
             copy.start()
     att = jnp.concatenate([att_ref[i] for i in range(8)], axis=1)
-    for copy in first:
-        copy.wait()
     proj = [dot(att, half[...].reshape(1024, 512)) for half in (left, right)]
     hidden = tok_ref[...].astype(f32) + jnp.concatenate(proj, axis=1)
     normed = norm_rows(hidden, ag_ref[...], as_ref[...]).astype(bf16)
@@ -317,7 +307,7 @@
             acc[:, 512 * n : 512 * n + 512] += dot(inner, weight)
         return carry
 
-    lax.fori_loop(0, 8, block, 0)
+    lax.fori_loop(0, 8, block, 0, unroll=2)
     done = norm_rows(acc[...], mg_ref[...], ms_ref[...]).astype(bf16)
     for i in range(8):
         out_ref[i] = done[:, 128 * i : 128 * i + 128]
@@ -378,13 +368,13 @@
     scal = jnp.stack([suffix_len, prefix_id, earlier_slot, place])
     part, w_far = pl.pallas_call(
         part_kernel,
-        in_specs=[SM, VM, hbm],
+        in_specs=[SM, VM, VM],
         out_specs=[VM, VM],
         out_shape=[
             jax.ShapeDtypeStruct((512, 384), f32),
             jax.ShapeDtypeStruct((512, 384), bf16),
         ],
-        scratch_shapes=[pltpu.VMEM((512, 384), bf16), pltpu.SemaphoreType.DMA((24,))],
+        scratch_shapes=[pltpu.VMEM((512, 384), bf16)],
         compiler_params=SMALL,
         cost_estimate=cost(2 * 512 * 512 * 384, 2 << 20),
         name="qkv_own_half",
@@ -461,18 +451,26 @@
         name="token_rows",
     )(scal, own_half, far_half)
 
+    halves = pl.pallas_call(
+        stage_kernel,
+        in_specs=[hbm],
+        out_specs=[VM] * 2,
+        out_shape=[jax.ShapeDtypeStruct((8, 4, 32, 512), bf16)] * 2,
+        scratch_shapes=[pltpu.SemaphoreType.DMA((8,))],
+        compiler_params=pltpu.CompilerParams(vmem_limit_bytes=48 << 20),
+        cost_estimate=cost(0, 4 << 20),
+        name="stage_out_weight",
+    )(shards)
     encoded = pl.pallas_call(
         tail_kernel,
-        in_specs=[VM] * 6 + [hbm],
+        in_specs=[VM] * 8 + [hbm],
         out_specs=VM,
         out_shape=jax.ShapeDtypeStruct((8, 64, 128), bf16),
         scratch_shapes=[
             pltpu.VMEM((64, 1024), f32),
-            pltpu.VMEM((8, 4, 32, 512), bf16),
-            pltpu.VMEM((8, 4, 32, 512), bf16),
             pltpu.VMEM((8, 4, 256, 512), bf16),
             pltpu.VMEM((8, 4, 256, 512), bf16),
-            pltpu.SemaphoreType.DMA((24,)),
+            pltpu.SemaphoreType.DMA((16,)),
         ],
         compiler_params=pltpu.CompilerParams(vmem_limit_bytes=52 << 20),
         cost_estimate=cost(2 * 64 * 9 * 1024 * 1024, 19 << 20, 64 * 4096),
@@ -484,6 +482,7 @@
         attn_shift.reshape(1, 1024),
         mlp_gain.reshape(1, 1024),
         mlp_shift.reshape(1, 1024),
+        *halves,
         shards,
     )
     return swap_all(encoded, TP).reshape(512, 128)

time: 165 us -> 163 us (0.988)
  waiting for transfers between devices: 59.2 us -> 56.6 us
    all_to_all x3, waiting for transfers between devices: 59.2 us -> 56.6 us  [swap_all(): return lax.all_to_all(value, axis, split_axis=0, concat_axis=0, tiled=True)]
    pallas_call x2 -> x3, Pallas kernels: 9.11 us -> 10.8 us  [the longest x1 8.15 us: local(): pl.pallas_call(tail_kernel, in_specs=[VM] * 8 + [hbm], out_specs=VM, out_...]
where the time goes in v5:
time: 163 us; the launch traced here: 162 us
  waiting for transfers between devices  56.6 us (35%)
  starting transfers between devices  38.4 us (24%)
  Pallas kernels  25.5 us (16%)
  blocking collectives  20.3 us (12%)
  between operations  13.6 us (8%)
  local copies, waits for them, and re-layouts  6.81 us (4%)
    all_to_all x3, waiting for transfers between devices, swap_all(): return lax.all_to_all(value, axis, split_axis=0, concat_axis=0, tiled=True)  56.6 us
    all_to_all x3, starting transfers between devices, swap_all(): return lax.all_to_all(value, axis, split_axis=0, concat_axis=0, tiled=True)  30.9 us
    all_to_all x2, blocking collectives, swap_all(): return lax.all_to_all(value, axis, split_axis=0, concat_axis=0, tiled=True)  20.3 us
    pallas_call x1, Pallas kernels, local(): pl.pallas_call(tail_kernel, in_specs=[VM] * 8 + [hbm], out_specs=VM, out_...  8.15 us
    ppermute x1, starting transfers between devices, local(): far_half = lax.ppermute(own_half, 'c', [(0, 1), (1, 0)])  7.51 us
    pallas_call x1, Pallas kernels, local(): pl.pallas_call(owner_kernel, in_specs=[VM] * 5, out_specs=VM, out_shape=j...  5.17 us
  transfers between devices with their start and end apart: 5, of which 3 were waited for; matrix products, arithmetic and copies ran while one was open for 3% of the time, Pallas kernels for 10%

profile of v5, /device:TPU:1, one launch (start us, length us, event | category | flops | bytes accessed | tf_op | source)
XLA Modules:
  0.0 161.9 jit_solution(13498928820377816404)
XLA Ops:
  6.5 0.0 all-gather.3.cloned.1.call-start
  6.5 0.0 copy-start.2
  6.5 0.0 copy-start.3
  6.5 0.0 copy-start.4
  6.5 0.0 copy-start.5
  6.5 1.9 %pack_weights.1 = bf16[576,512]{1,0:T(8,128)(2,1)} custom-call(s32[1]{0:T(128)} %bitcast.13.at, bf16[1024,512]{1,0:T(8,128)(2,1)} %up_ref.1, bf16[512,1024]{1,0:T(8,128)(2,1)} %down_ref.1, bf16[128,1024]{1,0:T(8,128)(2,1)} %out_ref.1), custom_call_target="tpu_custom_call" | custom-call | bytes 1048576 | tf_op jit(solution)/shard_map/pack_weights/pallas_call | solution.py:345
  8.5 0.0 all-gather.3.cloned.1.call-update
  8.5 1.0 broadcast_in_dim.16
  9.5 11.7 %all_to_all.25.half_ref.own_ref = bf16[4,512,128]{2,1,0:T(8,128)(2,1)S(1)} all-to-all(bf16[4,512,128]{2,1,0:T(8,128)(2,1)S(1)} %broadcast_in_dim.16), channel_id=1, replica_groups=mesh['z'=16,'x'=4,'y'=4,'c'=2] {'y'}, dimensions={0} | all-to-all | bytes 1048576 | tf_op jit(solution)/shard_map/all_to_all | solution.py:317
  21.2 7.5 %collective-permute-start = (bf16[4,512,128]{2,1,0:T(8,128)(2,1)S(1)}, bf16[4,512,128]{2,1,0:T(8,128)(2,1)S(1)}, u32[]{:S(2)}, u32[]{:S(2)}) collective-permute-start(bf16[4,512,128]{2,1,0:T(8,128)(2,1)S(1)} %all_to_all.25.half_ref.own_ref), channel_id=1, source_target_pairs={{0,1},{1,0},{2,3},{3,2},{4,5},{5,4},{6,7},{7,6},{8,9},{9,8},{10,11... | collective-permute-start | bytes 1572872 | tf_op jit(solution)/shard_map/ppermute | solution.py:365
  28.8 0.7 pad_add_fusion.scal
  29.5 0.0 copy-start.1
  29.5 1.1 copy-done.1
  30.6 1.1 qkv_own_half.1
  31.7 0.0 collective-permute-done.half_ref.far_ref
  31.7 2.1 %qkv_place.1 = (bf16[64,32,128]{2,1,0:T(8,128)(2,1)}, bf16[512,384]{1,0:T(8,128)(2,1)S(1)}) custom-call(s32[4,64]{1,0:T(4,128)S(1)} %pad_add_fusion.scal, f32[512,384]{1,0:T(8,128)S(1)} %get-tuple-element.13.part_ref, bf16[4,512,128]{2,1,0:T(8,128)(2,1)S(1)} %collective-permute-done.half_ref.far_ref, bf16[512,384]{1,0:T(8,128)(2,1)S(1)} %get-tuple-element.14.w_ref), custom_call_target="tpu_custom_call" | custom-call | flops 201326592 | bytes 3145728 | tf_op jit(solution)/shard_map/qkv_place/pallas_call | solution.py:382
  33.9 16.2 %all-to-all-start.1 = ((bf16[64,32,128]{2,1,0:T(8,128)(2,1)}), bf16[64,32,128]{2,1,0:T(8,128)(2,1)S(1)}, u32[]{:S(2)}, u32[]{:S(2)}) async-start(bf16[64,32,128]{2,1,0:T(8,128)(2,1)} %get-tuple-element.15), calls=%async_computation.1 | async-start | bytes 1048576 | tf_op jit(solution)/shard_map/all_to_all | solution.py:317
  50.0 1.5 fusion
  51.6 1.5 fusion.1
  53.1 28.1 %all-to-all-done.1.got_ref = bf16[64,32,128]{2,1,0:T(8,128)(2,1)S(1)} async-done(((bf16[64,32,128]{2,1,0:T(8,128)(2,1)}), bf16[64,32,128]{2,1,0:T(8,128)(2,1)S(1)}, u32[]{:S(2)}, u32[]{:S(2)}) %all-to-all-start.1) | async-done | bytes 524320 | tf_op jit(solution)/shard_map/all_to_all | solution.py:317
  81.2 5.2 %owner_attention.1 = bf16[64,32,128]{2,1,0:T(8,128)(2,1)} custom-call(bf16[64,32,128]{2,1,0:T(8,128)(2,1)S(1)} %all-to-all-done.1.got_ref, bf16[2,256,128]{2,1,0:T(8,128)(2,1)S(1)} %get-tuple-element.26.pk_ref, bf16[2,256,128]{2,1,0:T(8,128)(2,1)S(1)} %get-tuple-element.25.pv_ref, bf16[512,128]{1,0:T(8,128)(2,1)S(1)} %bitcast.19, bf16[512,128]{1,0:T(8,128)(2,1)S(1)} %bitcast.20), custom_call_target="tpu_custom_call" | custom-call | flops 536870912 | bytes 2097152 | tf_op jit(solution)/shard_map/owner_attention/pallas_call | solution.py:407
  86.4 7.1 %all-to-all-start.2 = ((bf16[64,32,128]{2,1,0:T(8,128)(2,1)}), bf16[64,32,128]{2,1,0:T(8,128)(2,1)S(1)}, u32[]{:S(2)}, u32[]{:S(2)}) async-start(bf16[64,32,128]{2,1,0:T(8,128)(2,1)} %owner_attention.1), calls=%async_computation.2 | async-start | bytes 1048576 | tf_op jit(solution)/shard_map/all_to_all | solution.py:317
  93.5 3.0 %own_attention.1 = (f32[512,128]{1,0:T(8,128)S(1)}, f32[512,128]{1,0:T(8,128)S(1)}) custom-call(s32[4,64]{1,0:T(4,128)S(1)} %pad_add_fusion.scal, bf16[512,384]{1,0:T(8,128)(2,1)S(1)} %get-tuple-element.16.qkv_ref), custom_call_target="tpu_custom_call" | custom-call | flops 67108864 | bytes 1048576 | tf_op jit(solution)/shard_map/own_attention/pallas_call | solution.py:397
  96.4 26.4 %all-to-all-done.2.ret_ref = bf16[64,32,128]{2,1,0:T(8,128)(2,1)S(1)} async-done(((bf16[64,32,128]{2,1,0:T(8,128)(2,1)}), bf16[64,32,128]{2,1,0:T(8,128)(2,1)S(1)}, u32[]{:S(2)}, u32[]{:S(2)}) %all-to-all-start.2) | async-done | bytes 524320 | tf_op jit(solution)/shard_map/all_to_all | solution.py:317
  122.8 1.9 %merge.1 = bf16[512,128]{1,0:T(8,128)(2,1)} custom-call(s32[4,64]{1,0:T(4,128)S(1)} %pad_add_fusion.scal, bf16[64,32,128]{2,1,0:T(8,128)(2,1)S(1)} %all-to-all-done.2.ret_ref, f32[512,128]{1,0:T(8,128)S(1)} %get-tuple-element.17.own_ref, f32[512,128]{1,0:T(8,128)S(1)} %get-tuple-element.18.lse_ref), custom_call_target="tpu_custom_call" | custom-call | flops 33554432 | bytes 1048576 | tf_op jit(solution)/shard_map/merge/pallas_call | solution.py:431
  124.7 7.7 %all-to-all-start.3 = ((bf16[8,64,128]{2,1,0:T(8,128)(2,1)}), bf16[8,64,128]{2,1,0:T(8,128)(2,1)S(1)}, u32[]{:S(2)}, u32[]{:S(2)}) async-start(bf16[8,64,128]{2,1,0:T(8,128)(2,1)} %bitcast.8), calls=%async_computation.3 | async-start | bytes 262144 | tf_op jit(solution)/shard_map/all_to_all | solution.py:317
  132.4 0.6 token_rows.1.tok_ref
  133.0 0.0 all-gather.3.cloned.1.call-done
  133.0 1.6 stage_out_weight.1
  134.6 0.0 copy-start
  134.6 1.0 copy-done
  135.6 2.1 %all-to-all-done.3.att_ref = bf16[8,64,128]{2,1,0:T(8,128)(2,1)S(1)} async-done(((bf16[8,64,128]{2,1,0:T(8,128)(2,1)}), bf16[8,64,128]{2,1,0:T(8,128)(2,1)S(1)}, u32[]{:S(2)}, u32[]{:S(2)}) %all-to-all-start.3) | async-done | bytes 131104 | tf_op jit(solution)/shard_map/all_to_all | solution.py:317
  137.7 0.0 copy-done.2
  137.7 0.0 copy-done.3
  137.7 0.0 copy-done.4
  137.7 0.0 copy-done.5
  137.7 8.2 %project_norm_ffn.1 = bf16[8,64,128]{2,1,0:T(8,128)(2,1)S(1)} custom-call(bf16[8,64,128]{2,1,0:T(8,128)(2,1)S(1)} %all-to-all-done.3.att_ref, bf16[64,1024]{1,0:T(8,128)(2,1)S(1)} %token_rows.1.tok_ref, f32[1,1024]{1,0:T(1,128)S(1)} %bitcast.21, f32[1,1024]{1,0:T(1,128)S(1)} %bitcast.22, f32[1,1024]{1,0:T(1,128)S(1)} %bitcast.23, f32[1,1024]{1,0:T(1,128)S(1)} %bitcast.24, ...), custom_call_target="tpu_custom_call" | custom-call | flops 1207959552 | bytes 19922944 | tf_op jit(solution)/shard_map/project_norm_ffn/pallas_call | solution.py:464
  145.9 8.5 %all_to_all.26 = bf16[8,64,128]{2,1,0:T(8,128)(2,1)S(1)} all-to-all(bf16[8,64,128]{2,1,0:T(8,128)(2,1)S(1)} %project_norm_ffn.1), channel_id=1, replica_groups=mesh['z'=16,'x'=4,'y'=4,'c'=2] {'y','c'}, dimensions={0} | all-to-all | bytes 262144 | tf_op jit(solution)/shard_map/all_to_all | solution.py:317
  154.4 0.7 copy.28
  (4 shorter events, 0.1 us)
Async XLA Ops:
  6.5 126.5 %all-gather.3.cloned.1.call-start = ((), (), s32[]{:S(2)}) async-start(), calls=%async_computation.5 | async-start | bytes 19464192 | tf_op jit(solution)/shard_map/all_gather | solution.py:361
  6.5 131.2 %copy-start.2 = (f32[1024]{0:T(1024)S(1)}, f32[1024]{0:T(1024)}, u32[]{:S(2)}) copy-start(f32[1024]{0:T(1024)} %param.17) | copy-start | bytes 12292
  6.5 131.2 %copy-start.3 = (f32[1024]{0:T(1024)S(1)}, f32[1024]{0:T(1024)}, u32[]{:S(2)}) copy-start(f32[1024]{0:T(1024)} %param.18) | copy-start | bytes 12292
  6.5 131.2 %copy-start.4 = (f32[1024]{0:T(1024)S(1)}, f32[1024]{0:T(1024)}, u32[]{:S(2)}) copy-start(f32[1024]{0:T(1024)} %param.21) | copy-start | bytes 12292
  6.5 131.2 %copy-start.5 = (f32[1024]{0:T(1024)S(1)}, f32[1024]{0:T(1024)}, u32[]{:S(2)}) copy-start(f32[1024]{0:T(1024)} %param.22) | copy-start | bytes 12292
  21.2 10.5 %collective-permute-start = (bf16[4,512,128]{2,1,0:T(8,128)(2,1)S(1)}, bf16[4,512,128]{2,1,0:T(8,128)(2,1)S(1)}, u32[]{:S(2)}, u32[]{:S(2)}) collective-permute-start(bf16[4,512,128]{2,1,0:T(8,128)(2,1)S(1)} %all_to_all.25.half_ref.own_ref), channel_id=1, source_target_pairs={{0,1},{1,0},{2,3},{3,2},{4,5},{5,4},{6,7},{7,6},{8,9},{9,8},{10,11... | collective-permute-start | bytes 1572872 | tf_op jit(solution)/shard_map/ppermute | solution.py:365
  29.5 1.1 copy-start.1
  33.9 47.4 %all-to-all-start.1 = ((bf16[64,32,128]{2,1,0:T(8,128)(2,1)}), bf16[64,32,128]{2,1,0:T(8,128)(2,1)S(1)}, u32[]{:S(2)}, u32[]{:S(2)}) async-start(bf16[64,32,128]{2,1,0:T(8,128)(2,1)} %get-tuple-element.15), calls=%async_computation.1 | async-start | bytes 1048576 | tf_op jit(solution)/shard_map/all_to_all | solution.py:317
  86.4 36.5 %all-to-all-start.2 = ((bf16[64,32,128]{2,1,0:T(8,128)(2,1)}), bf16[64,32,128]{2,1,0:T(8,128)(2,1)S(1)}, u32[]{:S(2)}, u32[]{:S(2)}) async-start(bf16[64,32,128]{2,1,0:T(8,128)(2,1)} %owner_attention.1), calls=%async_computation.2 | async-start | bytes 1048576 | tf_op jit(solution)/shard_map/all_to_all | solution.py:317
  124.7 13.0 %all-to-all-start.3 = ((bf16[8,64,128]{2,1,0:T(8,128)(2,1)}), bf16[8,64,128]{2,1,0:T(8,128)(2,1)S(1)}, u32[]{:S(2)}, u32[]{:S(2)}) async-start(bf16[8,64,128]{2,1,0:T(8,128)(2,1)} %bitcast.8), calls=%async_computation.3 | async-start | bytes 262144 | tf_op jit(solution)/shard_map/all_to_all | solution.py:317
  134.6 1.0 copy-start
Sparse Core Ops, SparseCore 0:
  10.5 103.7 all-gather.2

commit v6 on v4

--- a/solution.py
+++ b/solution.py
@@ -48,28 +48,19 @@
     return jnp.concatenate([half_ref[i, rows, :] for i in range(4)], axis=1)
 
 
-def part_kernel(scal, half_ref, w_hbm, part_ref, far_ref, buf, sem):
+def order_kernel(scal, w_ref, own_ref, far_ref):
     core = scal[3, 0]
-    copies = []
-    for side, target in ((core, buf), (1 - core, far_ref)):
+    for side, target in ((core, own_ref), (1 - core, far_ref)):
         for y in range(4):
             rows = pl.ds(pl.multiple_of((2 * y + side) * 128, 128), 128)
             for n in range(3):
-                place = target.at[pl.ds(128 * y, 128), pl.ds(128 * n, 128)]
-                copies.append(
-                    pltpu.make_async_copy(w_hbm.at[n, rows, :], place, sem.at[len(copies)])
-                )
-    for copy in copies:
-        copy.start()
-    for copy in copies:
-        copy.wait()
-
-    def block(b, carry):
-        rows = pl.ds(pl.multiple_of(b * 256, 256), 256)
-        part_ref[rows, :] = dot(half_rows(half_ref, rows), buf[...])
-        return carry
-
-    lax.fori_loop(0, 2, block, 0)
+                target[128 * y : 128 * y + 128, 128 * n : 128 * n + 128] = w_ref[n, rows, :]
+
+
+def part_kernel(half_ref, w_ref, part_ref):
+    for b in range(2):
+        rows = pl.ds(256 * b, 256)
+        part_ref[rows, :] = dot(half_rows(half_ref, rows), w_ref[...])
 
 
 def pair_of(scal, g):
@@ -104,7 +95,7 @@
             send_ref[slot_e, 16:32, :] = jnp.where(row == 15, held, moved).astype(bf16)
         return carry
 
-    lax.fori_loop(0, 4, block, 0)
+    lax.fori_loop(0, 4, block, 0, unroll=4)
 
 
 def own_kernel(scal, qkv_ref, out_ref, lse_ref):
@@ -178,7 +169,7 @@
         stat[slots, :] = stat_line(lse[:128], lse[128:])
         return carry
 
-    lax.fori_loop(0, 8, prefix_part, 0, unroll=2)
+    lax.fori_loop(0, 8, prefix_part, 0, unroll=8)
     copy.wait()
 
     def earlier_part(b, carry):
@@ -194,7 +185,7 @@
         ret_ref[slots, 16:32, :] = jnp.where(sub == 15, line, out).astype(bf16)
         return carry
 
-    lax.fori_loop(0, 8, earlier_part, 0, unroll=2)
+    lax.fori_loop(0, 8, earlier_part, 0, unroll=8)
 
 
 def merge_kernel(
@@ -237,7 +228,7 @@
         out_ref[rows, :] = (mixed / (w_own + w_pre + w_erl)).astype(bf16)
         return carry
 
-    lax.fori_loop(0, 4, block, 0)
+    lax.fori_loop(0, 4, block, 0, unroll=4)
 
 
 def norm_rows(hidden, gain, shift):
@@ -317,7 +308,7 @@
             acc[:, 512 * n : 512 * n + 512] += dot(inner, weight)
         return carry
 
-    lax.fori_loop(0, 8, block, 0)
+    lax.fori_loop(0, 8, block, 0, unroll=2)
     done = norm_rows(acc[...], mg_ref[...], ms_ref[...]).astype(bf16)
     for i in range(8):
         out_ref[i] = done[:, 128 * i : 128 * i + 128]
@@ -351,6 +342,18 @@
     core = lax.axis_index("c")
     rank = lax.axis_index(TP)
 
+    place = jnp.where(jnp.arange(64) % 2 == 0, core, rank)
+    scal = jnp.stack([suffix_len, prefix_id, earlier_slot, place])
+    w_own, w_far = pl.pallas_call(
+        order_kernel,
+        in_specs=[SM, VM],
+        out_specs=[VM, VM],
+        out_shape=[jax.ShapeDtypeStruct((512, 384), bf16)] * 2,
+        compiler_params=SMALL,
+        cost_estimate=cost(0, 2 << 20),
+        name="order_qkv_weight",
+    )(scal, qkv_weight.transpose(1, 0, 2))
+
     hbm = pl.BlockSpec(memory_space=pl.ANY)
     packed = pl.pallas_call(
         pack_kernel,
@@ -365,30 +368,29 @@
             out_specs=pl.BlockSpec((576, 512), lambda i, at: (0, 0)),
         ),
         out_shape=jax.ShapeDtypeStruct((576, 512), bf16),
+        compiler_params=SMALL,
         cost_estimate=cost(0, 1 << 20),
         name="pack_weights",
     )(lax.axis_index("x").reshape(1), up_weight, down_weight, out_weight)
+
+    own_half = swap_all(jnp.broadcast_to(tokens[None], (4, 512, 128)), "y")
+    own_half, scal, w_own, w_far, packed = lax.optimization_barrier(
+        (own_half, scal, w_own, w_far, packed)
+    )
     shards = lax.all_gather(packed, ("x", "y", "c"), axis=0, tiled=False)
     shards = shards.reshape(4, 8, 576, 512)
 
-    own_half = swap_all(jnp.broadcast_to(tokens[None], (4, 512, 128)), "y")
     far_half = lax.ppermute(own_half, "c", [(0, 1), (1, 0)])
 
-    place = jnp.where(jnp.arange(64) % 2 == 0, core, rank)
-    scal = jnp.stack([suffix_len, prefix_id, earlier_slot, place])
-    part, w_far = pl.pallas_call(
+    part = pl.pallas_call(
         part_kernel,
-        in_specs=[SM, VM, hbm],
-        out_specs=[VM, VM],
-        out_shape=[
-            jax.ShapeDtypeStruct((512, 384), f32),
-            jax.ShapeDtypeStruct((512, 384), bf16),
-        ],
-        scratch_shapes=[pltpu.VMEM((512, 384), bf16), pltpu.SemaphoreType.DMA((24,))],
+        in_specs=[VM, VM],
+        out_specs=VM,
+        out_shape=jax.ShapeDtypeStruct((512, 384), f32),
         compiler_params=SMALL,
         cost_estimate=cost(2 * 512 * 512 * 384, 2 << 20),
         name="qkv_own_half",
-    )(scal, own_half, qkv_weight.transpose(1, 0, 2))
+    )(own_half, w_own)
     send, qkv = pl.pallas_call(
         place_kernel,
         in_specs=[SM] + [VM] * 3,

time: 165 us -> 159 us (0.964)
  blocking collectives: 20.3 us -> 8.52 us
  starting transfers between devices: 38.4 us -> 43.6 us
  local copies, waits for them, and re-layouts: 5.82 us -> 10.1 us
  Pallas kernels: 26.1 us -> 21.9 us
    all_to_all x2 -> x1, blocking collectives: 20.3 us -> 8.52 us  [swap_all(): return lax.all_to_all(value, axis, split_axis=0, concat_axis=0, tiled=True)]
    all_to_all x3 -> x4, starting transfers between devices: 30.9 us -> 35.3 us  [swap_all(): return lax.all_to_all(value, axis, split_axis=0, concat_axis=0, tiled=True)]
    unnamed x13 -> x19, local copies, waits for them, and re-layouts: 1.84 us -> 5.23 us
    all_to_all x3 -> x4, waiting for transfers between devices: 59.2 us -> 59 us  [swap_all(): return lax.all_to_all(value, axis, split_axis=0, concat_axis=0, tiled=True)]
  transfers between devices with their start and end apart: 5 -> 6, of which waited for: 3 -> 5; matrix products, arithmetic and copies ran while one was open for 3% -> 2% of each run, Pallas kernels for 10% -> 9%
where the time goes in v6:
time: 159 us; the launch traced here: 158 us
  waiting for transfers between devices  60.1 us (38%)
  starting transfers between devices  43.6 us (27%)
  Pallas kernels  21.9 us (14%)
  between operations  13.5 us (8%)
  local copies, waits for them, and re-layouts  10.1 us (6%)
  blocking collectives  8.52 us (5%)
    all_to_all x4, waiting for transfers between devices, swap_all(): return lax.all_to_all(value, axis, split_axis=0, concat_axis=0, tiled=True)  59 us
    all_to_all x4, starting transfers between devices, swap_all(): return lax.all_to_all(value, axis, split_axis=0, concat_axis=0, tiled=True)  35.3 us
    all_to_all x1, blocking collectives, swap_all(): return lax.all_to_all(value, axis, split_axis=0, concat_axis=0, tiled=True)  8.52 us
    ppermute x1, starting transfers between devices, local(): far_half = lax.ppermute(own_half, 'c', [(0, 1), (1, 0)])  8.36 us
    pallas_call x1, Pallas kernels, local(): pl.pallas_call(tail_kernel, in_specs=[VM] * 6 + [hbm], out_specs=VM, out_...  7.14 us
    unnamed x19, local copies, waits for them, and re-layouts  5.23 us
    pallas_call x1, Pallas kernels, local(): pl.pallas_call(owner_kernel, in_specs=[VM] * 5, out_specs=VM, out_shape=j...  5.16 us
  transfers between devices with their start and end apart: 6, of which 5 were waited for; matrix products, arithmetic and copies ran while one was open for 2% of the time, Pallas kernels for 9%

profile of v6, /device:TPU:1, one launch (start us, length us, event | category | flops | bytes accessed | tf_op | source)
XLA Modules:
  0.0 158.5 jit_solution(10370952148664363494)
XLA Ops:
  6.5 0.0 copy-start.4
  6.5 0.0 copy-start.5
  6.5 0.0 copy-start.6
  6.5 0.0 copy-start.7
  6.5 1.8 %broadcast_in_dim.14 = bf16[4,512,128]{2,1,0:T(8,128)(2,1)} broadcast(bf16[512,128]{1,0:T(8,128)(2,1)} %param.14), dimensions={1,2} | broadcast | bytes 655360 | tf_op jit(solution)/shard_map/broadcast_in_dim | solution.py:376
  8.4 5.0 %all-to-all-start = ((bf16[4,512,128]{2,1,0:T(8,128)(2,1)}), bf16[4,512,128]{2,1,0:T(8,128)(2,1)S(1)}, u32[]{:S(2)}, u32[]{:S(2)}) async-start(bf16[4,512,128]{2,1,0:T(8,128)(2,1)} %broadcast_in_dim.14), calls=%async_computation | async-start | bytes 1048576 | tf_op jit(solution)/shard_map/all_to_all | solution.py:318
  13.4 0.0 all-gather.3.cloned.1.call-start
  13.4 0.7 pad_add_fusion.scal
  14.1 0.0 copy-start.2
  14.1 1.1 copy-done.2
  15.2 0.7 order_qkv_weight.1
  15.9 0.0 copy-start
  16.0 1.2 copy-done
  17.2 0.0 copy-start.1
  17.2 1.2 copy-done.1
  18.4 0.0 copy-start.3
  18.4 0.9 copy-done.3
  19.4 0.9 pack_weights.1
  20.2 0.1 all-to-all-done.half_ref.own_ref
  20.3 0.0 all-gather.3.cloned.1.call-update
  20.3 8.4 %collective-permute-start = (bf16[4,512,128]{2,1,0:T(8,128)(2,1)S(1)}, bf16[4,512,128]{2,1,0:T(8,128)(2,1)S(1)}, u32[]{:S(2)}, u32[]{:S(2)}) collective-permute-start(bf16[4,512,128]{2,1,0:T(8,128)(2,1)S(1)} %all-to-all-done.half_ref.own_ref), channel_id=1, source_target_pairs={{0,1},{1,0},{2,3},{3,2},{4,5},{5,4},{6,7},{7,6},{8,9},{9,8},{10,11... | collective-permute-start | bytes 1572872 | tf_op jit(solution)/shard_map/ppermute | solution.py:383
  28.7 0.4 qkv_own_half.1.part_ref
  29.1 1.1 collective-permute-done.half_ref.far_ref
  30.2 2.1 %qkv_place.1 = (bf16[64,32,128]{2,1,0:T(8,128)(2,1)}, bf16[512,384]{1,0:T(8,128)(2,1)S(1)}) custom-call(s32[4,64]{1,0:T(4,128)S(1)} %pad_add_fusion.scal, f32[512,384]{1,0:T(8,128)S(1)} %qkv_own_half.1.part_ref, bf16[4,512,128]{2,1,0:T(8,128)(2,1)S(1)} %collective-permute-done.half_ref.far_ref, bf16[512,384]{1,0:T(8,128)(2,1)S(1)} %get-tuple-element.21.w_ref), custom_call_target="tpu_custom_call" | custom-call | flops 201326592 | bytes 3145728 | tf_op jit(solution)/shard_map/qkv_place/pallas_call | solution.py:394
  32.3 15.3 %all-to-all-start.1 = ((bf16[64,32,128]{2,1,0:T(8,128)(2,1)}), bf16[64,32,128]{2,1,0:T(8,128)(2,1)S(1)}, u32[]{:S(2)}, u32[]{:S(2)}) async-start(bf16[64,32,128]{2,1,0:T(8,128)(2,1)} %get-tuple-element.22), calls=%async_computation.1 | async-start | bytes 1048576 | tf_op jit(solution)/shard_map/all_to_all | solution.py:318
  47.7 1.5 fusion
  49.2 1.5 fusion.1
  50.7 27.9 %all-to-all-done.1.got_ref = bf16[64,32,128]{2,1,0:T(8,128)(2,1)S(1)} async-done(((bf16[64,32,128]{2,1,0:T(8,128)(2,1)}), bf16[64,32,128]{2,1,0:T(8,128)(2,1)S(1)}, u32[]{:S(2)}, u32[]{:S(2)}) %all-to-all-start.1) | async-done | bytes 524320 | tf_op jit(solution)/shard_map/all_to_all | solution.py:318
  78.6 5.2 %owner_attention.1 = bf16[64,32,128]{2,1,0:T(8,128)(2,1)} custom-call(bf16[64,32,128]{2,1,0:T(8,128)(2,1)S(1)} %all-to-all-done.1.got_ref, bf16[2,256,128]{2,1,0:T(8,128)(2,1)S(1)} %get-tuple-element.32.pk_ref, bf16[2,256,128]{2,1,0:T(8,128)(2,1)S(1)} %get-tuple-element.31.pv_ref, bf16[512,128]{1,0:T(8,128)(2,1)S(1)} %bitcast.19, bf16[512,128]{1,0:T(8,128)(2,1)S(1)} %bitcast.20), custom_call_target="tpu_custom_call" | custom-call | flops 536870912 | bytes 2097152 | tf_op jit(solution)/shard_map/owner_attention/pallas_call | solution.py:419
  83.8 7.2 %all-to-all-start.2 = ((bf16[64,32,128]{2,1,0:T(8,128)(2,1)}), bf16[64,32,128]{2,1,0:T(8,128)(2,1)S(1)}, u32[]{:S(2)}, u32[]{:S(2)}) async-start(bf16[64,32,128]{2,1,0:T(8,128)(2,1)} %owner_attention.1), calls=%async_computation.2 | async-start | bytes 1048576 | tf_op jit(solution)/shard_map/all_to_all | solution.py:318
  91.0 3.0 %own_attention.1 = (f32[512,128]{1,0:T(8,128)S(1)}, f32[512,128]{1,0:T(8,128)S(1)}) custom-call(s32[4,64]{1,0:T(4,128)S(1)} %pad_add_fusion.scal, bf16[512,384]{1,0:T(8,128)(2,1)S(1)} %get-tuple-element.23.qkv_ref), custom_call_target="tpu_custom_call" | custom-call | flops 67108864 | bytes 1048576 | tf_op jit(solution)/shard_map/own_attention/pallas_call | solution.py:409
  94.0 26.4 %all-to-all-done.2.ret_ref = bf16[64,32,128]{2,1,0:T(8,128)(2,1)S(1)} async-done(((bf16[64,32,128]{2,1,0:T(8,128)(2,1)}), bf16[64,32,128]{2,1,0:T(8,128)(2,1)S(1)}, u32[]{:S(2)}, u32[]{:S(2)}) %all-to-all-start.2) | async-done | bytes 524320 | tf_op jit(solution)/shard_map/all_to_all | solution.py:318
  120.4 1.9 %merge.1 = bf16[512,128]{1,0:T(8,128)(2,1)} custom-call(s32[4,64]{1,0:T(4,128)S(1)} %pad_add_fusion.scal, bf16[64,32,128]{2,1,0:T(8,128)(2,1)S(1)} %all-to-all-done.2.ret_ref, f32[512,128]{1,0:T(8,128)S(1)} %get-tuple-element.24.own_ref, f32[512,128]{1,0:T(8,128)S(1)} %get-tuple-element.25.lse_ref), custom_call_target="tpu_custom_call" | custom-call | flops 33554432 | bytes 1048576 | tf_op jit(solution)/shard_map/merge/pallas_call | solution.py:443
  122.3 7.7 %all-to-all-start.3 = ((bf16[8,64,128]{2,1,0:T(8,128)(2,1)}), bf16[8,64,128]{2,1,0:T(8,128)(2,1)S(1)}, u32[]{:S(2)}, u32[]{:S(2)}) async-start(bf16[8,64,128]{2,1,0:T(8,128)(2,1)} %bitcast.9), calls=%async_computation.3 | async-start | bytes 262144 | tf_op jit(solution)/shard_map/all_to_all | solution.py:318
  130.0 0.6 token_rows.1.tok_ref
  130.6 4.7 %all-to-all-done.3.att_ref = bf16[8,64,128]{2,1,0:T(8,128)(2,1)S(1)} async-done(((bf16[8,64,128]{2,1,0:T(8,128)(2,1)}), bf16[8,64,128]{2,1,0:T(8,128)(2,1)S(1)}, u32[]{:S(2)}, u32[]{:S(2)}) %all-to-all-start.3) | async-done | bytes 131104 | tf_op jit(solution)/shard_map/all_to_all | solution.py:318
  135.3 0.0 all-gather.3.cloned.1.call-done
  135.3 0.0 copy-done.4
  135.3 0.0 copy-done.5
  135.3 0.0 copy-done.6
  135.3 0.0 copy-done.7
  135.3 7.1 %project_norm_ffn.1 = bf16[8,64,128]{2,1,0:T(8,128)(2,1)S(1)} custom-call(bf16[8,64,128]{2,1,0:T(8,128)(2,1)S(1)} %all-to-all-done.3.att_ref, bf16[64,1024]{1,0:T(8,128)(2,1)S(1)} %token_rows.1.tok_ref, f32[1,1024]{1,0:T(1,128)S(1)} %bitcast.21, f32[1,1024]{1,0:T(1,128)S(1)} %bitcast.22, f32[1,1024]{1,0:T(1,128)S(1)} %bitcast.23, f32[1,1024]{1,0:T(1,128)S(1)} %bitcast.24, ...), custom_call_target="tpu_custom_call" | custom-call | flops 1207959552 | bytes 19922944 | tf_op jit(solution)/shard_map/project_norm_ffn/pallas_call | solution.py:466
  142.5 8.5 %all_to_all.25 = bf16[8,64,128]{2,1,0:T(8,128)(2,1)S(1)} all-to-all(bf16[8,64,128]{2,1,0:T(8,128)(2,1)S(1)} %project_norm_ffn.1), channel_id=1, replica_groups=mesh['z'=16,'x'=4,'y'=4,'c'=2] {'y','c'}, dimensions={0} | all-to-all | bytes 262144 | tf_op jit(solution)/shard_map/all_to_all | solution.py:318
  151.0 0.7 copy.28
  (4 shorter events, 0.1 us)
Async XLA Ops:
  6.5 128.8 %copy-start.4 = (f32[1024]{0:T(1024)S(1)}, f32[1024]{0:T(1024)}, u32[]{:S(2)}) copy-start(f32[1024]{0:T(1024)} %param.17) | copy-start | bytes 12292
  6.5 128.8 %copy-start.5 = (f32[1024]{0:T(1024)S(1)}, f32[1024]{0:T(1024)}, u32[]{:S(2)}) copy-start(f32[1024]{0:T(1024)} %param.18) | copy-start | bytes 12292
  6.5 128.8 %copy-start.6 = (f32[1024]{0:T(1024)S(1)}, f32[1024]{0:T(1024)}, u32[]{:S(2)}) copy-start(f32[1024]{0:T(1024)} %param.21) | copy-start | bytes 12292
  6.5 128.8 %copy-start.7 = (f32[1024]{0:T(1024)S(1)}, f32[1024]{0:T(1024)}, u32[]{:S(2)}) copy-start(f32[1024]{0:T(1024)} %param.22) | copy-start | bytes 12292
  8.4 11.9 %all-to-all-start = ((bf16[4,512,128]{2,1,0:T(8,128)(2,1)}), bf16[4,512,128]{2,1,0:T(8,128)(2,1)S(1)}, u32[]{:S(2)}, u32[]{:S(2)}) async-start(bf16[4,512,128]{2,1,0:T(8,128)(2,1)} %broadcast_in_dim.14), calls=%async_computation | async-start | bytes 1048576 | tf_op jit(solution)/shard_map/all_to_all | solution.py:318
  13.4 121.9 %all-gather.3.cloned.1.call-start = ((), (), s32[]{:S(2)}) async-start(), calls=%async_computation.5 | async-start | bytes 19464192 | tf_op jit(solution)/shard_map/all_gather | solution.py:380
  14.1 1.1 copy-start.2
  15.9 1.2 copy-start
  17.2 1.2 copy-start.1
  18.4 0.9 copy-start.3
  20.3 9.9 %collective-permute-start = (bf16[4,512,128]{2,1,0:T(8,128)(2,1)S(1)}, bf16[4,512,128]{2,1,0:T(8,128)(2,1)S(1)}, u32[]{:S(2)}, u32[]{:S(2)}) collective-permute-start(bf16[4,512,128]{2,1,0:T(8,128)(2,1)S(1)} %all-to-all-done.half_ref.own_ref), channel_id=1, source_target_pairs={{0,1},{1,0},{2,3},{3,2},{4,5},{5,4},{6,7},{7,6},{8,9},{9,8},{10,11... | collective-permute-start | bytes 1572872 | tf_op jit(solution)/shard_map/ppermute | solution.py:383
  32.3 46.3 %all-to-all-start.1 = ((bf16[64,32,128]{2,1,0:T(8,128)(2,1)}), bf16[64,32,128]{2,1,0:T(8,128)(2,1)S(1)}, u32[]{:S(2)}, u32[]{:S(2)}) async-start(bf16[64,32,128]{2,1,0:T(8,128)(2,1)} %get-tuple-element.22), calls=%async_computation.1 | async-start | bytes 1048576 | tf_op jit(solution)/shard_map/all_to_all | solution.py:318
  83.8 36.6 %all-to-all-start.2 = ((bf16[64,32,128]{2,1,0:T(8,128)(2,1)}), bf16[64,32,128]{2,1,0:T(8,128)(2,1)S(1)}, u32[]{:S(2)}, u32[]{:S(2)}) async-start(bf16[64,32,128]{2,1,0:T(8,128)(2,1)} %owner_attention.1), calls=%async_computation.2 | async-start | bytes 1048576 | tf_op jit(solution)/shard_map/all_to_all | solution.py:318
  122.3 13.0 %all-to-all-start.3 = ((bf16[8,64,128]{2,1,0:T(8,128)(2,1)}), bf16[8,64,128]{2,1,0:T(8,128)(2,1)S(1)}, u32[]{:S(2)}, u32[]{:S(2)}) async-start(bf16[8,64,128]{2,1,0:T(8,128)(2,1)} %bitcast.9), calls=%async_computation.3 | async-start | bytes 262144 | tf_op jit(solution)/shard_map/all_to_all | solution.py:318
Sparse Core Ops, SparseCore 0:
  20.5 105.3 all-gather.2

commit v7 on v6

--- a/solution.py
+++ b/solution.py
@@ -344,16 +344,6 @@
 
     place = jnp.where(jnp.arange(64) % 2 == 0, core, rank)
     scal = jnp.stack([suffix_len, prefix_id, earlier_slot, place])
-    w_own, w_far = pl.pallas_call(
-        order_kernel,
-        in_specs=[SM, VM],
-        out_specs=[VM, VM],
-        out_shape=[jax.ShapeDtypeStruct((512, 384), bf16)] * 2,
-        compiler_params=SMALL,
-        cost_estimate=cost(0, 2 << 20),
-        name="order_qkv_weight",
-    )(scal, qkv_weight.transpose(1, 0, 2))
-
     hbm = pl.BlockSpec(memory_space=pl.ANY)
     packed = pl.pallas_call(
         pack_kernel,
@@ -368,10 +358,20 @@
             out_specs=pl.BlockSpec((576, 512), lambda i, at: (0, 0)),
         ),
         out_shape=jax.ShapeDtypeStruct((576, 512), bf16),
-        compiler_params=SMALL,
+        compiler_params=pltpu.CompilerParams(vmem_limit_bytes=61 << 20),
         cost_estimate=cost(0, 1 << 20),
         name="pack_weights",
     )(lax.axis_index("x").reshape(1), up_weight, down_weight, out_weight)
+    scal, packed = lax.optimization_barrier((scal, packed))
+    w_own, w_far = pl.pallas_call(
+        order_kernel,
+        in_specs=[SM, VM],
+        out_specs=[VM, VM],
+        out_shape=[jax.ShapeDtypeStruct((512, 384), bf16)] * 2,
+        compiler_params=SMALL,
+        cost_estimate=cost(0, 2 << 20),
+        name="order_qkv_weight",
+    )(scal, qkv_weight.transpose(1, 0, 2))
 
     own_half = swap_all(jnp.broadcast_to(tokens[None], (4, 512, 128)), "y")
     own_half, scal, w_own, w_far, packed = lax.optimization_barrier(

time: 159 us -> 159 us (level)
  local copies, waits for them, and re-layouts: 10.1 us -> 6.69 us
  waiting for transfers between devices: 60.1 us -> 62.5 us
    unnamed x19 -> x13, local copies, waits for them, and re-layouts: 5.23 us -> 1.84 us
    all_to_all x4, waiting for transfers between devices: 59 us -> 61.4 us  [swap_all(): return lax.all_to_all(value, axis, split_axis=0, concat_axis=0, tiled=True)]
  transfers between devices with their start and end apart: 6 -> 6, of which waited for: 5 -> 5; matrix products, arithmetic and copies ran while one was open for 2% -> 2% of each run, Pallas kernels for 9% -> 10%
where the time goes in v7:
time: 159 us; the launch traced here: 158 us
  waiting for transfers between devices  62.5 us (39%)
  starting transfers between devices  43.6 us (27%)
  Pallas kernels  22.9 us (14%)
  between operations  13.5 us (8%)
  blocking collectives  8.52 us (5%)
  local copies, waits for them, and re-layouts  6.69 us (4%)
    all_to_all x4, waiting for transfers between devices, swap_all(): return lax.all_to_all(value, axis, split_axis=0, concat_axis=0, tiled=True)  61.4 us
    all_to_all x4, starting transfers between devices, swap_all(): return lax.all_to_all(value, axis, split_axis=0, concat_axis=0, tiled=True)  35.3 us
    all_to_all x1, blocking collectives, swap_all(): return lax.all_to_all(value, axis, split_axis=0, concat_axis=0, tiled=True)  8.52 us
    ppermute x1, starting transfers between devices, local(): far_half = lax.ppermute(own_half, 'c', [(0, 1), (1, 0)])  8.36 us
    pallas_call x1, Pallas kernels, local(): pl.pallas_call(tail_kernel, in_specs=[VM] * 6 + [hbm], out_specs=VM, out_...  7.14 us
    pallas_call x1, Pallas kernels, local(): pl.pallas_call(owner_kernel, in_specs=[VM] * 5, out_specs=VM, out_shape=j...  5.16 us
  transfers between devices with their start and end apart: 6, of which 5 were waited for; matrix products, arithmetic and copies ran while one was open for 2% of the time, Pallas kernels for 10%

profile of v7, /device:TPU:1, one launch (start us, length us, event | category | flops | bytes accessed | tf_op | source)
XLA Modules:
  0.0 158.5 jit_solution(2425096420587218308)
XLA Ops:
  6.5 0.0 copy-start.1
  6.5 0.0 copy-start.2
  6.5 0.0 copy-start.3
  6.5 0.0 copy-start.4
  6.5 1.8 %broadcast_in_dim.14 = bf16[4,512,128]{2,1,0:T(8,128)(2,1)} broadcast(bf16[512,128]{1,0:T(8,128)(2,1)} %param.14), dimensions={1,2} | broadcast | bytes 655360 | tf_op jit(solution)/shard_map/broadcast_in_dim | solution.py:376
  8.4 5.0 %all-to-all-start = ((bf16[4,512,128]{2,1,0:T(8,128)(2,1)}), bf16[4,512,128]{2,1,0:T(8,128)(2,1)S(1)}, u32[]{:S(2)}, u32[]{:S(2)}) async-start(bf16[4,512,128]{2,1,0:T(8,128)(2,1)} %broadcast_in_dim.14), calls=%async_computation | async-start | bytes 1048576 | tf_op jit(solution)/shard_map/all_to_all | solution.py:318
  13.4 0.0 all-gather.3.cloned.1.call-start
  13.4 1.9 %pack_weights.1 = bf16[576,512]{1,0:T(8,128)(2,1)} custom-call(s32[1]{0:T(128)} %bitcast.3.at, bf16[1024,512]{1,0:T(8,128)(2,1)} %up_ref.1, bf16[512,1024]{1,0:T(8,128)(2,1)} %down_ref.1, bf16[128,1024]{1,0:T(8,128)(2,1)} %out_ref.1), custom_call_target="tpu_custom_call" | custom-call | bytes 1048576 | tf_op jit(solution)/shard_map/pack_weights/pallas_call | solution.py:348
  15.3 0.7 pad_add_fusion.scal
  16.0 0.0 copy-start
  16.0 1.1 copy-done
  17.1 0.7 order_qkv_weight.1
  17.8 2.5 %all-to-all-done.half_ref.own_ref = bf16[4,512,128]{2,1,0:T(8,128)(2,1)S(1)} async-done(((bf16[4,512,128]{2,1,0:T(8,128)(2,1)}), bf16[4,512,128]{2,1,0:T(8,128)(2,1)S(1)}, u32[]{:S(2)}, u32[]{:S(2)}) %all-to-all-start) | async-done | bytes 524320 | tf_op jit(solution)/shard_map/all_to_all | solution.py:318
  20.3 0.0 all-gather.3.cloned.1.call-update
  20.3 8.4 %collective-permute-start = (bf16[4,512,128]{2,1,0:T(8,128)(2,1)S(1)}, bf16[4,512,128]{2,1,0:T(8,128)(2,1)S(1)}, u32[]{:S(2)}, u32[]{:S(2)}) collective-permute-start(bf16[4,512,128]{2,1,0:T(8,128)(2,1)S(1)} %all-to-all-done.half_ref.own_ref), channel_id=1, source_target_pairs={{0,1},{1,0},{2,3},{3,2},{4,5},{5,4},{6,7},{7,6},{8,9},{9,8},{10,11... | collective-permute-start | bytes 1572872 | tf_op jit(solution)/shard_map/ppermute | solution.py:383
  28.7 0.4 qkv_own_half.1.part_ref
  29.2 1.1 collective-permute-done.half_ref.far_ref
  30.2 2.1 %qkv_place.1 = (bf16[64,32,128]{2,1,0:T(8,128)(2,1)}, bf16[512,384]{1,0:T(8,128)(2,1)S(1)}) custom-call(s32[4,64]{1,0:T(4,128)S(1)} %pad_add_fusion.scal, f32[512,384]{1,0:T(8,128)S(1)} %qkv_own_half.1.part_ref, bf16[4,512,128]{2,1,0:T(8,128)(2,1)S(1)} %collective-permute-done.half_ref.far_ref, bf16[512,384]{1,0:T(8,128)(2,1)S(1)} %get-tuple-element.25.w_ref), custom_call_target="tpu_custom_call" | custom-call | flops 201326592 | bytes 3145728 | tf_op jit(solution)/shard_map/qkv_place/pallas_call | solution.py:394
  32.3 15.3 %all-to-all-start.1 = ((bf16[64,32,128]{2,1,0:T(8,128)(2,1)}), bf16[64,32,128]{2,1,0:T(8,128)(2,1)S(1)}, u32[]{:S(2)}, u32[]{:S(2)}) async-start(bf16[64,32,128]{2,1,0:T(8,128)(2,1)} %get-tuple-element.26), calls=%async_computation.1 | async-start | bytes 1048576 | tf_op jit(solution)/shard_map/all_to_all | solution.py:318
  47.7 1.5 fusion
  49.2 1.5 fusion.1
  50.8 27.9 %all-to-all-done.1.got_ref = bf16[64,32,128]{2,1,0:T(8,128)(2,1)S(1)} async-done(((bf16[64,32,128]{2,1,0:T(8,128)(2,1)}), bf16[64,32,128]{2,1,0:T(8,128)(2,1)S(1)}, u32[]{:S(2)}, u32[]{:S(2)}) %all-to-all-start.1) | async-done | bytes 524320 | tf_op jit(solution)/shard_map/all_to_all | solution.py:318
  78.6 5.2 %owner_attention.1 = bf16[64,32,128]{2,1,0:T(8,128)(2,1)} custom-call(bf16[64,32,128]{2,1,0:T(8,128)(2,1)S(1)} %all-to-all-done.1.got_ref, bf16[2,256,128]{2,1,0:T(8,128)(2,1)S(1)} %get-tuple-element.36.pk_ref, bf16[2,256,128]{2,1,0:T(8,128)(2,1)S(1)} %get-tuple-element.35.pv_ref, bf16[512,128]{1,0:T(8,128)(2,1)S(1)} %bitcast.19, bf16[512,128]{1,0:T(8,128)(2,1)S(1)} %bitcast.20), custom_call_target="tpu_custom_call" | custom-call | flops 536870912 | bytes 2097152 | tf_op jit(solution)/shard_map/owner_attention/pallas_call | solution.py:419
  83.8 7.2 %all-to-all-start.2 = ((bf16[64,32,128]{2,1,0:T(8,128)(2,1)}), bf16[64,32,128]{2,1,0:T(8,128)(2,1)S(1)}, u32[]{:S(2)}, u32[]{:S(2)}) async-start(bf16[64,32,128]{2,1,0:T(8,128)(2,1)} %owner_attention.1), calls=%async_computation.2 | async-start | bytes 1048576 | tf_op jit(solution)/shard_map/all_to_all | solution.py:318
  91.1 3.0 %own_attention.1 = (f32[512,128]{1,0:T(8,128)S(1)}, f32[512,128]{1,0:T(8,128)S(1)}) custom-call(s32[4,64]{1,0:T(4,128)S(1)} %pad_add_fusion.scal, bf16[512,384]{1,0:T(8,128)(2,1)S(1)} %get-tuple-element.27.qkv_ref), custom_call_target="tpu_custom_call" | custom-call | flops 67108864 | bytes 1048576 | tf_op jit(solution)/shard_map/own_attention/pallas_call | solution.py:409
  94.0 26.4 %all-to-all-done.2.ret_ref = bf16[64,32,128]{2,1,0:T(8,128)(2,1)S(1)} async-done(((bf16[64,32,128]{2,1,0:T(8,128)(2,1)}), bf16[64,32,128]{2,1,0:T(8,128)(2,1)S(1)}, u32[]{:S(2)}, u32[]{:S(2)}) %all-to-all-start.2) | async-done | bytes 524320 | tf_op jit(solution)/shard_map/all_to_all | solution.py:318
  120.4 1.9 %merge.1 = bf16[512,128]{1,0:T(8,128)(2,1)} custom-call(s32[4,64]{1,0:T(4,128)S(1)} %pad_add_fusion.scal, bf16[64,32,128]{2,1,0:T(8,128)(2,1)S(1)} %all-to-all-done.2.ret_ref, f32[512,128]{1,0:T(8,128)S(1)} %get-tuple-element.28.own_ref, f32[512,128]{1,0:T(8,128)S(1)} %get-tuple-element.29.lse_ref), custom_call_target="tpu_custom_call" | custom-call | flops 33554432 | bytes 1048576 | tf_op jit(solution)/shard_map/merge/pallas_call | solution.py:443
  122.3 7.7 %all-to-all-start.3 = ((bf16[8,64,128]{2,1,0:T(8,128)(2,1)}), bf16[8,64,128]{2,1,0:T(8,128)(2,1)S(1)}, u32[]{:S(2)}, u32[]{:S(2)}) async-start(bf16[8,64,128]{2,1,0:T(8,128)(2,1)} %bitcast.9), calls=%async_computation.3 | async-start | bytes 262144 | tf_op jit(solution)/shard_map/all_to_all | solution.py:318
  130.0 0.6 token_rows.1.tok_ref
  130.6 4.7 %all-to-all-done.3.att_ref = bf16[8,64,128]{2,1,0:T(8,128)(2,1)S(1)} async-done(((bf16[8,64,128]{2,1,0:T(8,128)(2,1)}), bf16[8,64,128]{2,1,0:T(8,128)(2,1)S(1)}, u32[]{:S(2)}, u32[]{:S(2)}) %all-to-all-start.3) | async-done | bytes 131104 | tf_op jit(solution)/shard_map/all_to_all | solution.py:318
  135.3 0.0 all-gather.3.cloned.1.call-done
  135.3 0.0 copy-done.1
  135.3 0.0 copy-done.2
  135.3 0.0 copy-done.3
  135.3 0.0 copy-done.4
  135.3 7.1 %project_norm_ffn.1 = bf16[8,64,128]{2,1,0:T(8,128)(2,1)S(1)} custom-call(bf16[8,64,128]{2,1,0:T(8,128)(2,1)S(1)} %all-to-all-done.3.att_ref, bf16[64,1024]{1,0:T(8,128)(2,1)S(1)} %token_rows.1.tok_ref, f32[1,1024]{1,0:T(1,128)S(1)} %bitcast.21, f32[1,1024]{1,0:T(1,128)S(1)} %bitcast.22, f32[1,1024]{1,0:T(1,128)S(1)} %bitcast.23, f32[1,1024]{1,0:T(1,128)S(1)} %bitcast.24, ...), custom_call_target="tpu_custom_call" | custom-call | flops 1207959552 | bytes 19922944 | tf_op jit(solution)/shard_map/project_norm_ffn/pallas_call | solution.py:466
  142.5 8.5 %all_to_all.25 = bf16[8,64,128]{2,1,0:T(8,128)(2,1)S(1)} all-to-all(bf16[8,64,128]{2,1,0:T(8,128)(2,1)S(1)} %project_norm_ffn.1), channel_id=1, replica_groups=mesh['z'=16,'x'=4,'y'=4,'c'=2] {'y','c'}, dimensions={0} | all-to-all | bytes 262144 | tf_op jit(solution)/shard_map/all_to_all | solution.py:318
  151.0 0.7 copy.28
  (4 shorter events, 0.1 us)
Async XLA Ops:
  6.5 128.8 %copy-start.1 = (f32[1024]{0:T(1024)S(1)}, f32[1024]{0:T(1024)}, u32[]{:S(2)}) copy-start(f32[1024]{0:T(1024)} %param.17) | copy-start | bytes 12292
  6.5 128.8 %copy-start.2 = (f32[1024]{0:T(1024)S(1)}, f32[1024]{0:T(1024)}, u32[]{:S(2)}) copy-start(f32[1024]{0:T(1024)} %param.18) | copy-start | bytes 12292
  6.5 128.8 %copy-start.3 = (f32[1024]{0:T(1024)S(1)}, f32[1024]{0:T(1024)}, u32[]{:S(2)}) copy-start(f32[1024]{0:T(1024)} %param.21) | copy-start | bytes 12292
  6.5 128.8 %copy-start.4 = (f32[1024]{0:T(1024)S(1)}, f32[1024]{0:T(1024)}, u32[]{:S(2)}) copy-start(f32[1024]{0:T(1024)} %param.22) | copy-start | bytes 12292
  8.4 11.9 %all-to-all-start = ((bf16[4,512,128]{2,1,0:T(8,128)(2,1)}), bf16[4,512,128]{2,1,0:T(8,128)(2,1)S(1)}, u32[]{:S(2)}, u32[]{:S(2)}) async-start(bf16[4,512,128]{2,1,0:T(8,128)(2,1)} %broadcast_in_dim.14), calls=%async_computation | async-start | bytes 1048576 | tf_op jit(solution)/shard_map/all_to_all | solution.py:318
  13.4 121.9 %all-gather.3.cloned.1.call-start = ((), (), s32[]{:S(2)}) async-start(), calls=%async_computation.5 | async-start | bytes 19464192 | tf_op jit(solution)/shard_map/all_gather | solution.py:380
  16.0 1.1 copy-start
  20.3 9.9 %collective-permute-start = (bf16[4,512,128]{2,1,0:T(8,128)(2,1)S(1)}, bf16[4,512,128]{2,1,0:T(8,128)(2,1)S(1)}, u32[]{:S(2)}, u32[]{:S(2)}) collective-permute-start(bf16[4,512,128]{2,1,0:T(8,128)(2,1)S(1)} %all-to-all-done.half_ref.own_ref), channel_id=1, source_target_pairs={{0,1},{1,0},{2,3},{3,2},{4,5},{5,4},{6,7},{7,6},{8,9},{9,8},{10,11... | collective-permute-start | bytes 1572872 | tf_op jit(solution)/shard_map/ppermute | solution.py:383
  32.3 46.3 %all-to-all-start.1 = ((bf16[64,32,128]{2,1,0:T(8,128)(2,1)}), bf16[64,32,128]{2,1,0:T(8,128)(2,1)S(1)}, u32[]{:S(2)}, u32[]{:S(2)}) async-start(bf16[64,32,128]{2,1,0:T(8,128)(2,1)} %get-tuple-element.26), calls=%async_computation.1 | async-start | bytes 1048576 | tf_op jit(solution)/shard_map/all_to_all | solution.py:318
  83.8 36.6 %all-to-all-start.2 = ((bf16[64,32,128]{2,1,0:T(8,128)(2,1)}), bf16[64,32,128]{2,1,0:T(8,128)(2,1)S(1)}, u32[]{:S(2)}, u32[]{:S(2)}) async-start(bf16[64,32,128]{2,1,0:T(8,128)(2,1)} %owner_attention.1), calls=%async_computation.2 | async-start | bytes 1048576 | tf_op jit(solution)/shard_map/all_to_all | solution.py:318
  122.3 13.0 %all-to-all-start.3 = ((bf16[8,64,128]{2,1,0:T(8,128)(2,1)}), bf16[8,64,128]{2,1,0:T(8,128)(2,1)S(1)}, u32[]{:S(2)}, u32[]{:S(2)}) async-start(bf16[8,64,128]{2,1,0:T(8,128)(2,1)} %bitcast.9), calls=%async_computation.3 | async-start | bytes 262144 | tf_op jit(solution)/shard_map/all_to_all | solution.py:318
Sparse Core Ops, SparseCore 0:
  20.5 105.1 all-gather.2

commit v8 on v7

--- a/solution.py
+++ b/solution.py
@@ -127,9 +127,17 @@
     return jnp.concatenate([head_mask(q, 0), head_mask(q, 1)], axis=0)
 
 
-def join_heads(x):
-    n = x.shape[0] // 2
-    return head_mask(x[:n], 0) + head_mask(x[n:], 1)
+def with_ones(v, h):
+    lane = iota(v.shape, 1)
+    return jnp.where((lane >= HD) == (h == 1), v, jnp.ones_like(v))
+
+
+def finish_heads(top, first, second):
+    n = first.shape[0]
+    low = iota((n, 128), 1) < HD
+    total = pltpu.roll(jnp.where(low, second, first), HD, 1)
+    lse = jnp.where(low, top[:n], top[n:]) + jnp.log(total)
+    return jnp.where(low, first, second) / total, lse
 
 
 def owner_kernel(got_ref, pk_ref, pv_ref, ek_ref, ev_ref, ret_ref, row_v, row_s, stat, sem):
@@ -147,11 +155,12 @@
     copy = pltpu.make_async_copy(row_v, row_s, sem)
     copy.start()
 
-    def stat_line(first, second):
-        both = jnp.where(group % 2 == 0, first.reshape(8, 16, 1), second.reshape(8, 16, 1))
-        line = jnp.sum(jnp.where(lane % 16 == sub, both, 0.0), axis=1)
+    def stat_line(lse):
+        line = jnp.sum(jnp.where(lane % 16 == sub, lse.reshape(8, 16, 128), 0.0), axis=1)
         high = line.astype(bf16).astype(f32)
-        return jnp.where((group[:, 0] // 2) % 2 == 1, line - high, high)
+        return jnp.where(group[:, 0] % 2 == 1, line - high, high)
+
+    values = [[with_ones(pv_ref[p], h) for h in range(2)] for p in range(2)]
 
     def prefix_part(b, carry):
         slots = pl.ds(pl.multiple_of(b * 8, 8), 8)
@@ -162,11 +171,17 @@
         pick = jnp.broadcast_to(pick, (128, 256))
         pick = jnp.concatenate([pick, pick], axis=0)
         s = jnp.where(pick, dot_t(q, pk_ref[1]), dot_t(q, pk_ref[0]))
-        w, inv, lse = softmax_parts(s, None)
+        top = jnp.max(s, axis=-1, keepdims=True)
+        w = jnp.exp(s - top).astype(bf16)
         none = jnp.zeros_like(w)
-        o = dot(jnp.where(pick, none, w), pv_ref[0]) + dot(jnp.where(pick, w, none), pv_ref[1])
-        ret_ref[slots, 0:16, :] = join_heads(o * inv).astype(bf16).reshape(8, 16, 128)
-        stat[slots, :] = stat_line(lse[:128], lse[128:])
+        w0, w1 = jnp.where(pick, none, w), jnp.where(pick, w, none)
+        parts = [
+            dot(w0[n : n + 128], values[0][h]) + dot(w1[n : n + 128], values[1][h])
+            for h, n in enumerate((0, 128))
+        ]
+        out, lse = finish_heads(top, *parts)
+        ret_ref[slots, 0:16, :] = out.astype(bf16).reshape(8, 16, 128)
+        stat[slots, :] = stat_line(lse)
         return carry
 
     lax.fori_loop(0, 8, prefix_part, 0, unroll=8)
@@ -177,10 +192,14 @@
         q = stack_heads(got_ref[slots, 16:32, :].reshape(128, 128))
         at = [pl.ds(pl.multiple_of(row_s[b * 8 + i, 16] * 16, 16), 16) for i in range(8)]
         keys = jnp.concatenate([ek_ref[x, :] for x in at], axis=0)
-        values = jnp.concatenate([ev_ref[x, :] for x in at], axis=0)
-        w, inv, lse = softmax_parts(dot_t(q, keys), near)
-        out = join_heads(dot(w, values) * inv).reshape(8, 16, 128)
-        line = jnp.where(group[:, 0] < 4, stat[slots, :], stat_line(lse[:128], lse[128:]))
+        rows = jnp.concatenate([ev_ref[x, :] for x in at], axis=0)
+        s = jnp.where(near, dot_t(q, keys), NEG)
+        top = jnp.max(s, axis=-1, keepdims=True)
+        w = jnp.exp(s - top).astype(bf16)
+        parts = [dot(w[n : n + 128], with_ones(rows, h)) for h, n in enumerate((0, 128))]
+        out, lse = finish_heads(top, *parts)
+        out = out.reshape(8, 16, 128)
+        line = jnp.where(group[:, 0] % 4 < 2, stat[slots, :], stat_line(lse))
         line = jnp.broadcast_to(line[:, None, :], (8, 16, 128))
         ret_ref[slots, 16:32, :] = jnp.where(sub == 15, line, out).astype(bf16)
         return carry
@@ -202,10 +221,10 @@
             slot, slot_e, _, late, span = pair_of(scal, g)
             pre_o[rows, :] = ret_ref[slot, 0:16, :].astype(f32)
             line = jnp.broadcast_to(ret_ref[slot, 16:32, :].astype(f32)[15:16, :], (16, 128))
-            pre_s[rows, :] = jnp.where(diag & (lane < 64), line, 0.0)
+            pre_s[rows, :] = jnp.where(diag & ((lane // 32) % 2 == 0), line, 0.0)
             part = ret_ref[slot_e, 16:32, :].astype(f32)
             line = jnp.broadcast_to(part[15:16, :], (16, 128))
-            stat = jnp.where(diag & (lane >= 64), line, 0.0)
+            stat = jnp.where(diag & ((lane // 32) % 2 == 1), line, 0.0)
             erl_o[rows, :] = jnp.where(late, pltpu.roll(part, 1, 0), part)
             erl_s[rows, :] = jnp.where(late, pltpu.roll(stat, 1, 0), stat)
             turn = jnp.where(late, 1, 0)
@@ -213,7 +232,7 @@
         rows = pl.ds(pl.multiple_of(b * 128, 128), 128)
         a = iota((128, 128), 0)
         c = iota((128, 128), 1)
-        pick = (((a // 16) % 2) == (c // 64)).astype(bf16)
+        pick = ((a // 64) == (c // 64)).astype(bf16)
         l_pre = dot(pre_s[rows, :].astype(bf16), pick)
         l_erl = dot(erl_s[rows, :].astype(bf16), pick)
         on = erl_on[rows, :] > 0.5

time: 159 us -> 159 us (level)
  no operation moved by 1% of the time
where the time goes in v8:
time: 159 us; the launch traced here: 158 us
  waiting for transfers between devices  62.5 us (39%)
  starting transfers between devices  43.6 us (27%)
  Pallas kernels  22.6 us (14%)
  between operations  13.5 us (8%)
  blocking collectives  8.52 us (5%)
  local copies, waits for them, and re-layouts  6.69 us (4%)
    all_to_all x4, waiting for transfers between devices, swap_all(): return lax.all_to_all(value, axis, split_axis=0, concat_axis=0, tiled=True)  61.4 us
    all_to_all x4, starting transfers between devices, swap_all(): return lax.all_to_all(value, axis, split_axis=0, concat_axis=0, tiled=True)  35.3 us
    all_to_all x1, blocking collectives, swap_all(): return lax.all_to_all(value, axis, split_axis=0, concat_axis=0, tiled=True)  8.52 us
    ppermute x1, starting transfers between devices, local(): far_half = lax.ppermute(own_half, 'c', [(0, 1), (1, 0)])  8.36 us
    pallas_call x1, Pallas kernels, local(): pl.pallas_call(tail_kernel, in_specs=[VM] * 6 + [hbm], out_specs=VM, out_...  7.14 us
    pallas_call x1, Pallas kernels, local(): pl.pallas_call(owner_kernel, in_specs=[VM] * 5, out_specs=VM, out_shape=j...  4.84 us
  transfers between devices with their start and end apart: 6, of which 5 were waited for; matrix products, arithmetic and copies ran while one was open for 2% of the time, Pallas kernels for 10%

profile of v8, /device:TPU:1, one launch (start us, length us, event | category | flops | bytes accessed | tf_op | source)
XLA Modules:
  0.0 158.2 jit_solution(6072344664675869382)
XLA Ops:
  6.5 0.0 copy-start.1
  6.5 0.0 copy-start.2
  6.5 0.0 copy-start.3
  6.5 0.0 copy-start.4
  6.5 1.8 %broadcast_in_dim.14 = bf16[4,512,128]{2,1,0:T(8,128)(2,1)} broadcast(bf16[512,128]{1,0:T(8,128)(2,1)} %param.14), dimensions={1,2} | broadcast | bytes 655360 | tf_op jit(solution)/shard_map/broadcast_in_dim | solution.py:395
  8.4 5.0 %all-to-all-start = ((bf16[4,512,128]{2,1,0:T(8,128)(2,1)}), bf16[4,512,128]{2,1,0:T(8,128)(2,1)S(1)}, u32[]{:S(2)}, u32[]{:S(2)}) async-start(bf16[4,512,128]{2,1,0:T(8,128)(2,1)} %broadcast_in_dim.14), calls=%async_computation | async-start | bytes 1048576 | tf_op jit(solution)/shard_map/all_to_all | solution.py:337
  13.4 0.0 all-gather.3.cloned.1.call-start
  13.4 1.9 %pack_weights.1 = bf16[576,512]{1,0:T(8,128)(2,1)} custom-call(s32[1]{0:T(128)} %bitcast.3.at, bf16[1024,512]{1,0:T(8,128)(2,1)} %up_ref.1, bf16[512,1024]{1,0:T(8,128)(2,1)} %down_ref.1, bf16[128,1024]{1,0:T(8,128)(2,1)} %out_ref.1), custom_call_target="tpu_custom_call" | custom-call | bytes 1048576 | tf_op jit(solution)/shard_map/pack_weights/pallas_call | solution.py:367
  15.3 0.7 pad_add_fusion.scal
  16.0 0.0 copy-start
  16.0 1.1 copy-done
  17.1 0.7 order_qkv_weight.1
  17.8 2.5 %all-to-all-done.half_ref.own_ref = bf16[4,512,128]{2,1,0:T(8,128)(2,1)S(1)} async-done(((bf16[4,512,128]{2,1,0:T(8,128)(2,1)}), bf16[4,512,128]{2,1,0:T(8,128)(2,1)S(1)}, u32[]{:S(2)}, u32[]{:S(2)}) %all-to-all-start) | async-done | bytes 524320 | tf_op jit(solution)/shard_map/all_to_all | solution.py:337
  20.3 0.0 all-gather.3.cloned.1.call-update
  20.3 8.4 %collective-permute-start = (bf16[4,512,128]{2,1,0:T(8,128)(2,1)S(1)}, bf16[4,512,128]{2,1,0:T(8,128)(2,1)S(1)}, u32[]{:S(2)}, u32[]{:S(2)}) collective-permute-start(bf16[4,512,128]{2,1,0:T(8,128)(2,1)S(1)} %all-to-all-done.half_ref.own_ref), channel_id=1, source_target_pairs={{0,1},{1,0},{2,3},{3,2},{4,5},{5,4},{6,7},{7,6},{8,9},{9,8},{10,11... | collective-permute-start | bytes 1572872 | tf_op jit(solution)/shard_map/ppermute | solution.py:402
  28.7 0.4 qkv_own_half.1.part_ref
  29.2 1.1 collective-permute-done.half_ref.far_ref
  30.2 2.1 %qkv_place.1 = (bf16[64,32,128]{2,1,0:T(8,128)(2,1)}, bf16[512,384]{1,0:T(8,128)(2,1)S(1)}) custom-call(s32[4,64]{1,0:T(4,128)S(1)} %pad_add_fusion.scal, f32[512,384]{1,0:T(8,128)S(1)} %qkv_own_half.1.part_ref, bf16[4,512,128]{2,1,0:T(8,128)(2,1)S(1)} %collective-permute-done.half_ref.far_ref, bf16[512,384]{1,0:T(8,128)(2,1)S(1)} %get-tuple-element.25.w_ref), custom_call_target="tpu_custom_call" | custom-call | flops 201326592 | bytes 3145728 | tf_op jit(solution)/shard_map/qkv_place/pallas_call | solution.py:413
  32.3 15.3 %all-to-all-start.1 = ((bf16[64,32,128]{2,1,0:T(8,128)(2,1)}), bf16[64,32,128]{2,1,0:T(8,128)(2,1)S(1)}, u32[]{:S(2)}, u32[]{:S(2)}) async-start(bf16[64,32,128]{2,1,0:T(8,128)(2,1)} %get-tuple-element.26), calls=%async_computation.1 | async-start | bytes 1048576 | tf_op jit(solution)/shard_map/all_to_all | solution.py:337
  47.7 1.5 fusion
  49.2 1.5 fusion.1
  50.8 27.9 %all-to-all-done.1.got_ref = bf16[64,32,128]{2,1,0:T(8,128)(2,1)S(1)} async-done(((bf16[64,32,128]{2,1,0:T(8,128)(2,1)}), bf16[64,32,128]{2,1,0:T(8,128)(2,1)S(1)}, u32[]{:S(2)}, u32[]{:S(2)}) %all-to-all-start.1) | async-done | bytes 524320 | tf_op jit(solution)/shard_map/all_to_all | solution.py:337
  78.6 4.8 %owner_attention.1 = bf16[64,32,128]{2,1,0:T(8,128)(2,1)} custom-call(bf16[64,32,128]{2,1,0:T(8,128)(2,1)S(1)} %all-to-all-done.1.got_ref, bf16[2,256,128]{2,1,0:T(8,128)(2,1)S(1)} %get-tuple-element.36.pk_ref, bf16[2,256,128]{2,1,0:T(8,128)(2,1)S(1)} %get-tuple-element.35.pv_ref, bf16[512,128]{1,0:T(8,128)(2,1)S(1)} %bitcast.19, bf16[512,128]{1,0:T(8,128)(2,1)S(1)} %bitcast.20), custom_call_target="tpu_custom_call" | custom-call | flops 536870912 | bytes 2097152 | tf_op jit(solution)/shard_map/owner_attention/pallas_call | solution.py:438
  83.5 7.2 %all-to-all-start.2 = ((bf16[64,32,128]{2,1,0:T(8,128)(2,1)}), bf16[64,32,128]{2,1,0:T(8,128)(2,1)S(1)}, u32[]{:S(2)}, u32[]{:S(2)}) async-start(bf16[64,32,128]{2,1,0:T(8,128)(2,1)} %owner_attention.1), calls=%async_computation.2 | async-start | bytes 1048576 | tf_op jit(solution)/shard_map/all_to_all | solution.py:337
  90.7 3.0 %own_attention.1 = (f32[512,128]{1,0:T(8,128)S(1)}, f32[512,128]{1,0:T(8,128)S(1)}) custom-call(s32[4,64]{1,0:T(4,128)S(1)} %pad_add_fusion.scal, bf16[512,384]{1,0:T(8,128)(2,1)S(1)} %get-tuple-element.27.qkv_ref), custom_call_target="tpu_custom_call" | custom-call | flops 67108864 | bytes 1048576 | tf_op jit(solution)/shard_map/own_attention/pallas_call | solution.py:428
  93.7 26.4 %all-to-all-done.2.ret_ref = bf16[64,32,128]{2,1,0:T(8,128)(2,1)S(1)} async-done(((bf16[64,32,128]{2,1,0:T(8,128)(2,1)}), bf16[64,32,128]{2,1,0:T(8,128)(2,1)S(1)}, u32[]{:S(2)}, u32[]{:S(2)}) %all-to-all-start.2) | async-done | bytes 524320 | tf_op jit(solution)/shard_map/all_to_all | solution.py:337
  120.1 1.9 %merge.1 = bf16[512,128]{1,0:T(8,128)(2,1)} custom-call(s32[4,64]{1,0:T(4,128)S(1)} %pad_add_fusion.scal, bf16[64,32,128]{2,1,0:T(8,128)(2,1)S(1)} %all-to-all-done.2.ret_ref, f32[512,128]{1,0:T(8,128)S(1)} %get-tuple-element.28.own_ref, f32[512,128]{1,0:T(8,128)S(1)} %get-tuple-element.29.lse_ref), custom_call_target="tpu_custom_call" | custom-call | flops 33554432 | bytes 1048576 | tf_op jit(solution)/shard_map/merge/pallas_call | solution.py:462
  122.0 7.7 %all-to-all-start.3 = ((bf16[8,64,128]{2,1,0:T(8,128)(2,1)}), bf16[8,64,128]{2,1,0:T(8,128)(2,1)S(1)}, u32[]{:S(2)}, u32[]{:S(2)}) async-start(bf16[8,64,128]{2,1,0:T(8,128)(2,1)} %bitcast.9), calls=%async_computation.3 | async-start | bytes 262144 | tf_op jit(solution)/shard_map/all_to_all | solution.py:337
  129.7 0.6 token_rows.1.tok_ref
  130.3 4.7 %all-to-all-done.3.att_ref = bf16[8,64,128]{2,1,0:T(8,128)(2,1)S(1)} async-done(((bf16[8,64,128]{2,1,0:T(8,128)(2,1)}), bf16[8,64,128]{2,1,0:T(8,128)(2,1)S(1)}, u32[]{:S(2)}, u32[]{:S(2)}) %all-to-all-start.3) | async-done | bytes 131104 | tf_op jit(solution)/shard_map/all_to_all | solution.py:337
  135.0 0.0 all-gather.3.cloned.1.call-done
  135.0 0.0 copy-done.1
  135.0 0.0 copy-done.2
  135.0 0.0 copy-done.3
  135.0 0.0 copy-done.4
  135.0 7.1 %project_norm_ffn.1 = bf16[8,64,128]{2,1,0:T(8,128)(2,1)S(1)} custom-call(bf16[8,64,128]{2,1,0:T(8,128)(2,1)S(1)} %all-to-all-done.3.att_ref, bf16[64,1024]{1,0:T(8,128)(2,1)S(1)} %token_rows.1.tok_ref, f32[1,1024]{1,0:T(1,128)S(1)} %bitcast.21, f32[1,1024]{1,0:T(1,128)S(1)} %bitcast.22, f32[1,1024]{1,0:T(1,128)S(1)} %bitcast.23, f32[1,1024]{1,0:T(1,128)S(1)} %bitcast.24, ...), custom_call_target="tpu_custom_call" | custom-call | flops 1207959552 | bytes 19922944 | tf_op jit(solution)/shard_map/project_norm_ffn/pallas_call | solution.py:485
  142.2 8.5 %all_to_all.25 = bf16[8,64,128]{2,1,0:T(8,128)(2,1)S(1)} all-to-all(bf16[8,64,128]{2,1,0:T(8,128)(2,1)S(1)} %project_norm_ffn.1), channel_id=1, replica_groups=mesh['z'=16,'x'=4,'y'=4,'c'=2] {'y','c'}, dimensions={0} | all-to-all | bytes 262144 | tf_op jit(solution)/shard_map/all_to_all | solution.py:337
  150.7 0.7 copy.28
  (4 shorter events, 0.1 us)
Async XLA Ops:
  6.5 128.4 %copy-start.1 = (f32[1024]{0:T(1024)S(1)}, f32[1024]{0:T(1024)}, u32[]{:S(2)}) copy-start(f32[1024]{0:T(1024)} %param.17) | copy-start | bytes 12292
  6.5 128.5 %copy-start.2 = (f32[1024]{0:T(1024)S(1)}, f32[1024]{0:T(1024)}, u32[]{:S(2)}) copy-start(f32[1024]{0:T(1024)} %param.18) | copy-start | bytes 12292
  6.5 128.5 %copy-start.3 = (f32[1024]{0:T(1024)S(1)}, f32[1024]{0:T(1024)}, u32[]{:S(2)}) copy-start(f32[1024]{0:T(1024)} %param.21) | copy-start | bytes 12292
  6.5 128.5 %copy-start.4 = (f32[1024]{0:T(1024)S(1)}, f32[1024]{0:T(1024)}, u32[]{:S(2)}) copy-start(f32[1024]{0:T(1024)} %param.22) | copy-start | bytes 12292
  8.4 11.9 %all-to-all-start = ((bf16[4,512,128]{2,1,0:T(8,128)(2,1)}), bf16[4,512,128]{2,1,0:T(8,128)(2,1)S(1)}, u32[]{:S(2)}, u32[]{:S(2)}) async-start(bf16[4,512,128]{2,1,0:T(8,128)(2,1)} %broadcast_in_dim.14), calls=%async_computation | async-start | bytes 1048576 | tf_op jit(solution)/shard_map/all_to_all | solution.py:337
  13.4 121.6 %all-gather.3.cloned.1.call-start = ((), (), s32[]{:S(2)}) async-start(), calls=%async_computation.5 | async-start | bytes 19464192 | tf_op jit(solution)/shard_map/all_gather | solution.py:399
  16.0 1.1 copy-start
  20.3 9.9 %collective-permute-start = (bf16[4,512,128]{2,1,0:T(8,128)(2,1)S(1)}, bf16[4,512,128]{2,1,0:T(8,128)(2,1)S(1)}, u32[]{:S(2)}, u32[]{:S(2)}) collective-permute-start(bf16[4,512,128]{2,1,0:T(8,128)(2,1)S(1)} %all-to-all-done.half_ref.own_ref), channel_id=1, source_target_pairs={{0,1},{1,0},{2,3},{3,2},{4,5},{5,4},{6,7},{7,6},{8,9},{9,8},{10,11... | collective-permute-start | bytes 1572872 | tf_op jit(solution)/shard_map/ppermute | solution.py:402
  32.3 46.3 %all-to-all-start.1 = ((bf16[64,32,128]{2,1,0:T(8,128)(2,1)}), bf16[64,32,128]{2,1,0:T(8,128)(2,1)S(1)}, u32[]{:S(2)}, u32[]{:S(2)}) async-start(bf16[64,32,128]{2,1,0:T(8,128)(2,1)} %get-tuple-element.26), calls=%async_computation.1 | async-start | bytes 1048576 | tf_op jit(solution)/shard_map/all_to_all | solution.py:337
  83.5 36.6 %all-to-all-start.2 = ((bf16[64,32,128]{2,1,0:T(8,128)(2,1)}), bf16[64,32,128]{2,1,0:T(8,128)(2,1)S(1)}, u32[]{:S(2)}, u32[]{:S(2)}) async-start(bf16[64,32,128]{2,1,0:T(8,128)(2,1)} %owner_attention.1), calls=%async_computation.2 | async-start | bytes 1048576 | tf_op jit(solution)/shard_map/all_to_all | solution.py:337
  122.0 13.0 %all-to-all-start.3 = ((bf16[8,64,128]{2,1,0:T(8,128)(2,1)}), bf16[8,64,128]{2,1,0:T(8,128)(2,1)S(1)}, u32[]{:S(2)}, u32[]{:S(2)}) async-start(bf16[8,64,128]{2,1,0:T(8,128)(2,1)} %bitcast.9), calls=%async_computation.3 | async-start | bytes 262144 | tf_op jit(solution)/shard_map/all_to_all | solution.py:337
Sparse Core Ops, SparseCore 0:
  20.5 105.2 all-gather.2

commit v9 on v8

--- a/solution.py
+++ b/solution.py
@@ -69,16 +69,16 @@
     return scal[1, 2 * g] // 2, slot // 32, slot % 32, later >= 0, scal[0, 2 * g]
 
 
-def place_kernel(scal, part_ref, half_ref, w_ref, send_ref, qkv_ref):
+def place_kernel(scal, part_ref, half_ref, w_ref, send_ref, q_ref):
     row = iota((16, 128), 0)
     lane = iota((16, 128), 1)
     send_ref[...] = jnp.zeros(send_ref.shape, bf16)
 
     def block(b, carry):
         rows = pl.ds(pl.multiple_of(b * 128, 128), 128)
-        out = part_ref[rows, :] + dot(half_rows(half_ref, rows), w_ref[...])
-        qkv_ref[rows, :] = out.astype(bf16)
-        q = out[:, :128].astype(bf16)
+        out = part_ref[rows, 0:128] + dot(half_rows(half_ref, rows), w_ref[:, 0:128])
+        q = out.astype(bf16)
+        q_ref[rows, :] = q
         for p in range(8):
             g = b * 8 + p
             slot, slot_e, row_e, late, span = pair_of(scal, g)
@@ -98,15 +98,16 @@
     lax.fori_loop(0, 4, block, 0, unroll=4)
 
 
-def own_kernel(scal, qkv_ref, out_ref, lse_ref):
+def own_kernel(scal, q_ref, part_ref, half_ref, w_ref, out_ref, lse_ref):
     r = iota((128, 128), 0)
     c = iota((128, 128), 1)
 
     def block(b, carry):
         rows = pl.ds(pl.multiple_of(b * 128, 128), 128)
-        q = qkv_ref[rows, 0:128]
-        k = qkv_ref[rows, 128:256]
-        v = qkv_ref[rows, 256:384]
+        q = q_ref[rows, :]
+        kv = part_ref[rows, 128:384] + dot(half_rows(half_ref, rows), w_ref[:, 128:384])
+        k = kv[:, 0:128].astype(bf16)
+        v = kv[:, 128:256].astype(bf16)
         span = jnp.concatenate(
             [jnp.full((16, 128), scal[0, 2 * (b * 8 + p)], jnp.int32) for p in range(8)], axis=0
         )
@@ -410,13 +411,13 @@
         cost_estimate=cost(2 * 512 * 512 * 384, 2 << 20),
         name="qkv_own_half",
     )(own_half, w_own)
-    send, qkv = pl.pallas_call(
+    send, q = pl.pallas_call(
         place_kernel,
         in_specs=[SM] + [VM] * 3,
         out_specs=[VM, VM],
         out_shape=[
             jax.ShapeDtypeStruct((n_req, 32, 128), bf16),
-            jax.ShapeDtypeStruct((512, 384), bf16),
+            jax.ShapeDtypeStruct((512, 128), bf16),
         ],
         compiler_params=SMALL,
         cost_estimate=cost(2 * 512 * 512 * 384, 3 << 20),
@@ -427,13 +428,13 @@
 
     own_out, own_lse = pl.pallas_call(
         own_kernel,
-        in_specs=[SM, VM],
+        in_specs=[SM, VM, VM, VM, VM],
         out_specs=[VM, VM],
         out_shape=[jax.ShapeDtypeStruct((512, 128), f32)] * 2,
         compiler_params=SMALL,
         cost_estimate=cost(2 * 512 * 128 * 128 * 4, 1 << 20, 2 * 512 * 128),
         name="own_attention",
-    )(scal, qkv)
+    )(scal, q, part, far_half, w_far)
 
     ret = pl.pallas_call(
         owner_kernel,

time: 159 us -> 159 us (level)
  no operation moved by 1% of the time
where the time goes in v9:
time: 159 us; the launch traced here: 158 us
  waiting for transfers between devices  61.8 us (39%)
  starting transfers between devices  43.6 us (27%)
  Pallas kernels  23.3 us (15%)
  between operations  13.5 us (8%)
  blocking collectives  8.52 us (5%)
  local copies, waits for them, and re-layouts  6.69 us (4%)
    all_to_all x4, waiting for transfers between devices, swap_all(): return lax.all_to_all(value, axis, split_axis=0, concat_axis=0, tiled=True)  60.7 us
    all_to_all x4, starting transfers between devices, swap_all(): return lax.all_to_all(value, axis, split_axis=0, concat_axis=0, tiled=True)  35.3 us
    all_to_all x1, blocking collectives, swap_all(): return lax.all_to_all(value, axis, split_axis=0, concat_axis=0, tiled=True)  8.52 us
    ppermute x1, starting transfers between devices, local(): far_half = lax.ppermute(own_half, 'c', [(0, 1), (1, 0)])  8.36 us
    pallas_call x1, Pallas kernels, local(): pl.pallas_call(tail_kernel, in_specs=[VM] * 6 + [hbm], out_specs=VM, out_...  7.14 us
    pallas_call x1, Pallas kernels, local(): pl.pallas_call(owner_kernel, in_specs=[VM] * 5, out_specs=VM, out_shape=j...  4.84 us
    pallas_call x1, Pallas kernels, local(): pl.pallas_call(own_kernel, in_specs=[SM, VM, VM, VM, VM], out_specs=[VM,...  3.74 us
  transfers between devices with their start and end apart: 6, of which 5 were waited for; matrix products, arithmetic and copies ran while one was open for 2% of the time, Pallas kernels for 10%

profile of v9, /device:TPU:1, one launch (start us, length us, event | category | flops | bytes accessed | tf_op | source)
XLA Modules:
  0.0 158.1 jit_solution(13962303623973930006)
XLA Ops:
  6.5 0.0 copy-start.1
  6.5 0.0 copy-start.2
  6.5 0.0 copy-start.3
  6.5 0.0 copy-start.4
  6.5 1.8 %broadcast_in_dim.14 = bf16[4,512,128]{2,1,0:T(8,128)(2,1)} broadcast(bf16[512,128]{1,0:T(8,128)(2,1)} %param.14), dimensions={1,2} | broadcast | bytes 655360 | tf_op jit(solution)/shard_map/broadcast_in_dim | solution.py:396
  8.4 5.0 %all-to-all-start = ((bf16[4,512,128]{2,1,0:T(8,128)(2,1)}), bf16[4,512,128]{2,1,0:T(8,128)(2,1)S(1)}, u32[]{:S(2)}, u32[]{:S(2)}) async-start(bf16[4,512,128]{2,1,0:T(8,128)(2,1)} %broadcast_in_dim.14), calls=%async_computation | async-start | bytes 1048576 | tf_op jit(solution)/shard_map/all_to_all | solution.py:338
  13.4 0.0 all-gather.3.cloned.1.call-start
  13.4 1.9 %pack_weights.1 = bf16[576,512]{1,0:T(8,128)(2,1)} custom-call(s32[1]{0:T(128)} %bitcast.3.at, bf16[1024,512]{1,0:T(8,128)(2,1)} %up_ref.1, bf16[512,1024]{1,0:T(8,128)(2,1)} %down_ref.1, bf16[128,1024]{1,0:T(8,128)(2,1)} %out_ref.1), custom_call_target="tpu_custom_call" | custom-call | bytes 1048576 | tf_op jit(solution)/shard_map/pack_weights/pallas_call | solution.py:368
  15.3 0.7 pad_add_fusion.scal
  16.0 0.0 copy-start
  16.0 1.1 copy-done
  17.1 0.7 order_qkv_weight.1
  17.8 2.5 %all-to-all-done.half_ref.own_ref = bf16[4,512,128]{2,1,0:T(8,128)(2,1)S(1)} async-done(((bf16[4,512,128]{2,1,0:T(8,128)(2,1)}), bf16[4,512,128]{2,1,0:T(8,128)(2,1)S(1)}, u32[]{:S(2)}, u32[]{:S(2)}) %all-to-all-start) | async-done | bytes 524320 | tf_op jit(solution)/shard_map/all_to_all | solution.py:338
  20.3 0.0 all-gather.3.cloned.1.call-update
  20.3 8.4 %collective-permute-start = (bf16[4,512,128]{2,1,0:T(8,128)(2,1)S(1)}, bf16[4,512,128]{2,1,0:T(8,128)(2,1)S(1)}, u32[]{:S(2)}, u32[]{:S(2)}) collective-permute-start(bf16[4,512,128]{2,1,0:T(8,128)(2,1)S(1)} %all-to-all-done.half_ref.own_ref), channel_id=1, source_target_pairs={{0,1},{1,0},{2,3},{3,2},{4,5},{5,4},{6,7},{7,6},{8,9},{9,8},{10,11... | collective-permute-start | bytes 1572872 | tf_op jit(solution)/shard_map/ppermute | solution.py:403
  28.7 0.4 qkv_own_half.1.part_ref
  29.2 1.1 collective-permute-done.half_ref.far_ref
  30.2 2.0 %qkv_place.1 = (bf16[64,32,128]{2,1,0:T(8,128)(2,1)}, bf16[512,128]{1,0:T(8,128)(2,1)S(1)}) custom-call(s32[4,64]{1,0:T(4,128)S(1)} %pad_add_fusion.scal, f32[512,384]{1,0:T(8,128)S(1)} %qkv_own_half.1.part_ref, bf16[4,512,128]{2,1,0:T(8,128)(2,1)S(1)} %collective-permute-done.half_ref.far_ref, bf16[512,384]{1,0:T(8,128)(2,1)S(1)} %get-tuple-element.25.w_ref), custom_call_target="tpu_custom_call" | custom-call | flops 201326592 | bytes 3145728 | tf_op jit(solution)/shard_map/qkv_place/pallas_call | solution.py:414
  32.2 15.3 %all-to-all-start.1 = ((bf16[64,32,128]{2,1,0:T(8,128)(2,1)}), bf16[64,32,128]{2,1,0:T(8,128)(2,1)S(1)}, u32[]{:S(2)}, u32[]{:S(2)}) async-start(bf16[64,32,128]{2,1,0:T(8,128)(2,1)} %get-tuple-element.26), calls=%async_computation.1 | async-start | bytes 1048576 | tf_op jit(solution)/shard_map/all_to_all | solution.py:338
  47.6 1.5 fusion
  49.1 1.5 fusion.1
  50.7 27.9 %all-to-all-done.1.got_ref = bf16[64,32,128]{2,1,0:T(8,128)(2,1)S(1)} async-done(((bf16[64,32,128]{2,1,0:T(8,128)(2,1)}), bf16[64,32,128]{2,1,0:T(8,128)(2,1)S(1)}, u32[]{:S(2)}, u32[]{:S(2)}) %all-to-all-start.1) | async-done | bytes 524320 | tf_op jit(solution)/shard_map/all_to_all | solution.py:338
  78.5 4.8 %owner_attention.1 = bf16[64,32,128]{2,1,0:T(8,128)(2,1)} custom-call(bf16[64,32,128]{2,1,0:T(8,128)(2,1)S(1)} %all-to-all-done.1.got_ref, bf16[2,256,128]{2,1,0:T(8,128)(2,1)S(1)} %get-tuple-element.36.pk_ref, bf16[2,256,128]{2,1,0:T(8,128)(2,1)S(1)} %get-tuple-element.35.pv_ref, bf16[512,128]{1,0:T(8,128)(2,1)S(1)} %bitcast.19, bf16[512,128]{1,0:T(8,128)(2,1)S(1)} %bitcast.20), custom_call_target="tpu_custom_call" | custom-call | flops 536870912 | bytes 2097152 | tf_op jit(solution)/shard_map/owner_attention/pallas_call | solution.py:439
  83.4 7.2 %all-to-all-start.2 = ((bf16[64,32,128]{2,1,0:T(8,128)(2,1)}), bf16[64,32,128]{2,1,0:T(8,128)(2,1)S(1)}, u32[]{:S(2)}, u32[]{:S(2)}) async-start(bf16[64,32,128]{2,1,0:T(8,128)(2,1)} %owner_attention.1), calls=%async_computation.2 | async-start | bytes 1048576 | tf_op jit(solution)/shard_map/all_to_all | solution.py:338
  90.7 3.7 %own_attention.1 = (f32[512,128]{1,0:T(8,128)S(1)}, f32[512,128]{1,0:T(8,128)S(1)}) custom-call(s32[4,64]{1,0:T(4,128)S(1)} %pad_add_fusion.scal, bf16[512,128]{1,0:T(8,128)(2,1)S(1)} %get-tuple-element.27.q_ref, f32[512,384]{1,0:T(8,128)S(1)} %qkv_own_half.1.part_ref, bf16[4,512,128]{2,1,0:T(8,128)(2,1)S(1)} %collective-permute-done.half_ref.far_ref, ...), custom_call_target="tpu_custom_call" | custom-call | flops 67108864 | bytes 1048576 | tf_op jit(solution)/shard_map/own_attention/pallas_call | solution.py:429
  94.4 25.6 %all-to-all-done.2.ret_ref = bf16[64,32,128]{2,1,0:T(8,128)(2,1)S(1)} async-done(((bf16[64,32,128]{2,1,0:T(8,128)(2,1)}), bf16[64,32,128]{2,1,0:T(8,128)(2,1)S(1)}, u32[]{:S(2)}, u32[]{:S(2)}) %all-to-all-start.2) | async-done | bytes 524320 | tf_op jit(solution)/shard_map/all_to_all | solution.py:338
  120.0 1.9 %merge.1 = bf16[512,128]{1,0:T(8,128)(2,1)} custom-call(s32[4,64]{1,0:T(4,128)S(1)} %pad_add_fusion.scal, bf16[64,32,128]{2,1,0:T(8,128)(2,1)S(1)} %all-to-all-done.2.ret_ref, f32[512,128]{1,0:T(8,128)S(1)} %get-tuple-element.28.own_ref, f32[512,128]{1,0:T(8,128)S(1)} %get-tuple-element.29.lse_ref), custom_call_target="tpu_custom_call" | custom-call | flops 33554432 | bytes 1048576 | tf_op jit(solution)/shard_map/merge/pallas_call | solution.py:463
  121.9 7.7 %all-to-all-start.3 = ((bf16[8,64,128]{2,1,0:T(8,128)(2,1)}), bf16[8,64,128]{2,1,0:T(8,128)(2,1)S(1)}, u32[]{:S(2)}, u32[]{:S(2)}) async-start(bf16[8,64,128]{2,1,0:T(8,128)(2,1)} %bitcast.9), calls=%async_computation.3 | async-start | bytes 262144 | tf_op jit(solution)/shard_map/all_to_all | solution.py:338
  129.6 0.6 token_rows.1.tok_ref
  130.2 4.7 %all-to-all-done.3.att_ref = bf16[8,64,128]{2,1,0:T(8,128)(2,1)S(1)} async-done(((bf16[8,64,128]{2,1,0:T(8,128)(2,1)}), bf16[8,64,128]{2,1,0:T(8,128)(2,1)S(1)}, u32[]{:S(2)}, u32[]{:S(2)}) %all-to-all-start.3) | async-done | bytes 131104 | tf_op jit(solution)/shard_map/all_to_all | solution.py:338
  134.9 0.0 all-gather.3.cloned.1.call-done
  134.9 0.0 copy-done.1
  134.9 0.0 copy-done.2
  134.9 0.0 copy-done.3
  134.9 0.0 copy-done.4
  134.9 7.1 %project_norm_ffn.1 = bf16[8,64,128]{2,1,0:T(8,128)(2,1)S(1)} custom-call(bf16[8,64,128]{2,1,0:T(8,128)(2,1)S(1)} %all-to-all-done.3.att_ref, bf16[64,1024]{1,0:T(8,128)(2,1)S(1)} %token_rows.1.tok_ref, f32[1,1024]{1,0:T(1,128)S(1)} %bitcast.21, f32[1,1024]{1,0:T(1,128)S(1)} %bitcast.22, f32[1,1024]{1,0:T(1,128)S(1)} %bitcast.23, f32[1,1024]{1,0:T(1,128)S(1)} %bitcast.24, ...), custom_call_target="tpu_custom_call" | custom-call | flops 1207959552 | bytes 19922944 | tf_op jit(solution)/shard_map/project_norm_ffn/pallas_call | solution.py:486
  142.1 8.5 %all_to_all.25 = bf16[8,64,128]{2,1,0:T(8,128)(2,1)S(1)} all-to-all(bf16[8,64,128]{2,1,0:T(8,128)(2,1)S(1)} %project_norm_ffn.1), channel_id=1, replica_groups=mesh['z'=16,'x'=4,'y'=4,'c'=2] {'y','c'}, dimensions={0} | all-to-all | bytes 262144 | tf_op jit(solution)/shard_map/all_to_all | solution.py:338
  150.6 0.7 copy.28
  (4 shorter events, 0.1 us)
Async XLA Ops:
  6.5 128.4 %copy-start.1 = (f32[1024]{0:T(1024)S(1)}, f32[1024]{0:T(1024)}, u32[]{:S(2)}) copy-start(f32[1024]{0:T(1024)} %param.17) | copy-start | bytes 12292
  6.5 128.4 %copy-start.2 = (f32[1024]{0:T(1024)S(1)}, f32[1024]{0:T(1024)}, u32[]{:S(2)}) copy-start(f32[1024]{0:T(1024)} %param.18) | copy-start | bytes 12292
  6.5 128.4 %copy-start.3 = (f32[1024]{0:T(1024)S(1)}, f32[1024]{0:T(1024)}, u32[]{:S(2)}) copy-start(f32[1024]{0:T(1024)} %param.21) | copy-start | bytes 12292
  6.5 128.4 %copy-start.4 = (f32[1024]{0:T(1024)S(1)}, f32[1024]{0:T(1024)}, u32[]{:S(2)}) copy-start(f32[1024]{0:T(1024)} %param.22) | copy-start | bytes 12292
  8.4 11.9 %all-to-all-start = ((bf16[4,512,128]{2,1,0:T(8,128)(2,1)}), bf16[4,512,128]{2,1,0:T(8,128)(2,1)S(1)}, u32[]{:S(2)}, u32[]{:S(2)}) async-start(bf16[4,512,128]{2,1,0:T(8,128)(2,1)} %broadcast_in_dim.14), calls=%async_computation | async-start | bytes 1048576 | tf_op jit(solution)/shard_map/all_to_all | solution.py:338
  13.4 121.5 %all-gather.3.cloned.1.call-start = ((), (), s32[]{:S(2)}) async-start(), calls=%async_computation.5 | async-start | bytes 19464192 | tf_op jit(solution)/shard_map/all_gather | solution.py:400
  16.0 1.1 copy-start
  20.3 9.9 %collective-permute-start = (bf16[4,512,128]{2,1,0:T(8,128)(2,1)S(1)}, bf16[4,512,128]{2,1,0:T(8,128)(2,1)S(1)}, u32[]{:S(2)}, u32[]{:S(2)}) collective-permute-start(bf16[4,512,128]{2,1,0:T(8,128)(2,1)S(1)} %all-to-all-done.half_ref.own_ref), channel_id=1, source_target_pairs={{0,1},{1,0},{2,3},{3,2},{4,5},{5,4},{6,7},{7,6},{8,9},{9,8},{10,11... | collective-permute-start | bytes 1572872 | tf_op jit(solution)/shard_map/ppermute | solution.py:403
  32.2 46.3 %all-to-all-start.1 = ((bf16[64,32,128]{2,1,0:T(8,128)(2,1)}), bf16[64,32,128]{2,1,0:T(8,128)(2,1)S(1)}, u32[]{:S(2)}, u32[]{:S(2)}) async-start(bf16[64,32,128]{2,1,0:T(8,128)(2,1)} %get-tuple-element.26), calls=%async_computation.1 | async-start | bytes 1048576 | tf_op jit(solution)/shard_map/all_to_all | solution.py:338
  83.4 36.6 %all-to-all-start.2 = ((bf16[64,32,128]{2,1,0:T(8,128)(2,1)}), bf16[64,32,128]{2,1,0:T(8,128)(2,1)S(1)}, u32[]{:S(2)}, u32[]{:S(2)}) async-start(bf16[64,32,128]{2,1,0:T(8,128)(2,1)} %owner_attention.1), calls=%async_computation.2 | async-start | bytes 1048576 | tf_op jit(solution)/shard_map/all_to_all | solution.py:338
  121.9 13.0 %all-to-all-start.3 = ((bf16[8,64,128]{2,1,0:T(8,128)(2,1)}), bf16[8,64,128]{2,1,0:T(8,128)(2,1)S(1)}, u32[]{:S(2)}, u32[]{:S(2)}) async-start(bf16[8,64,128]{2,1,0:T(8,128)(2,1)} %bitcast.9), calls=%async_computation.3 | async-start | bytes 262144 | tf_op jit(solution)/shard_map/all_to_all | solution.py:338
Sparse Core Ops, SparseCore 0:
  20.5 105.1 all-gather.2
